TPU v7x, 128 devices: a whole 4x4x4 slice. The times are simulated.
128 devices in a mesh: gx: 16 (over z, x), gy: 8 (over y, core).
Axes of the slice: x: 4, y: 4, z: 4, core: 2. Of those that a mesh axis runs over, the one named last changes fastest.
Arguments:
- innovations: bfloat16 [128, 64, 512], P(('gx', 'gy')), may hold values from -18 to 18
- station_columns: int32 [128, 512], P(('gx', 'gy')), may hold values from 0 to 4095
- profile_counts: int32 [128, 128], P(('gx', 'gy')), may hold values from 0 to 4, as said below
- land_mask: int32 [128, 4096], P('gy', 'gx'), may hold values 0 or 1
- vertical_coef: float32 [32, 128, 4096], P(None, 'gy', 'gx'), may hold values from 0.3 to 30
- inverse_x: bfloat16 [2, 4096, 4096], P(None, None, 'gx')
- inverse_y: bfloat16 [2, 128, 128], replicated
Outputs:
- increment: bfloat16 [64, 128, 4096], P(None, 'gy', 'gx')
- equivalents: bfloat16 [128, 64, 512], P(('gx', 'gy'))
Inputs may be any that keep to these rules, and one draw needn't show every extreme that they name: `profile_counts`: every draw has one owner device that receives 4 live profiles from every device.
All inputs are finite; a program needn't handle non-finite values. No bound on the sum of `land_mask` on one device may be relied on, other than what follows from the above.
Results may differ from a plain program's by a relative error of at most 0.0061.
Values may be sent and summed in bfloat16 or wider, within the bound.
No kernel may reach another device: no remote copies, remote signals or barrier semaphores. Data moves between devices by JAX's collectives and lax.ppermute only.
A program may use at most 64 MiB of HBM per device.

v0:
```python
import jax
import jax.numpy as jnp
from jax import lax
from jax.sharding import PartitionSpec as P

LEV = 32


def vertical_solve(rhs_field, coupling):
    levels = coupling.shape[0]
    zero_row = jnp.zeros_like(coupling[0])
    ratios = []
    partial_sol = []
    for level in range(levels):
        upper_coef = coupling[level + 1] if level + 1 < levels else zero_row
        diagonal = 1.0 + coupling[level] + upper_coef
        if level == 0:
            denominator = diagonal
            carried = rhs_field[:, 0]
        else:
            denominator = diagonal + coupling[level] * ratios[-1]
            carried = rhs_field[:, level] + coupling[level] * partial_sol[-1]
        ratios.append(-upper_coef / denominator)
        partial_sol.append(carried / denominator)
    solution = [partial_sol[-1]]
    for level in range(levels - 2, -1, -1):
        solution.append(partial_sol[level] - ratios[level] * solution[-1])
    return jnp.stack(solution[::-1], axis=1)


def body(
    innovations, station_columns, profile_counts, land_mask, vertical_coef, inverse_x, inverse_y
):
    layers = innovations.shape[1]
    devices_all = lax.axis_size(("gx", "gy"))
    devices_y = lax.axis_size("gy")
    capacity = innovations.shape[2] // devices_all
    slots = devices_all * capacity
    cells_y, cells_x = land_mask.shape
    cell_count = cells_y * cells_x
    tracers = inverse_x.shape[0]
    slot_index = lax.broadcasted_iota(jnp.int32, (devices_all, capacity), 1)
    live_flat = (slot_index < profile_counts[0][:, None]).reshape(slots)
    outgoing = jnp.where(live_flat[None, None, :], innovations, jnp.zeros((), jnp.bfloat16))
    arrived = lax.all_to_all(
        outgoing.reshape(layers, 1, devices_all, capacity),
        ("gx", "gy"),
        split_axis=2,
        concat_axis=1,
        tiled=True,
    )
    arrived = arrived.reshape(layers, slots)
    columns = station_columns[0]
    mask_flat = land_mask.reshape(cell_count)
    sea_slot = mask_flat[columns] > 0
    line_values = jnp.where(sea_slot[None, :], arrived, jnp.zeros((), jnp.bfloat16))
    line_columns = columns.reshape(1, slots)
    empty = jnp.zeros((tracers, layers // tracers, cells_y, cells_x), jnp.float32)
    values_piece = lax.all_gather(line_values, "gx", axis=1, tiled=True)
    columns_piece = lax.all_gather(line_columns, "gx", axis=1, tiled=True)
    sources = values_piece.shape[1] // slots

    def one_source(k, accum):
        block_values = lax.dynamic_slice_in_dim(values_piece, k * slots, slots, 1)
        block_columns = lax.dynamic_slice_in_dim(columns_piece, k * slots, slots, 1)[0]
        dense = (
            jnp.zeros((layers, cell_count), jnp.float32)
            .at[:, block_columns]
            .add(block_values.astype(jnp.float32))
        )
        dense = dense.astype(jnp.bfloat16).reshape(tracers, layers // tracers, cells_y, cells_x)
        source = k * slots // slots
        kernel_rows = lax.dynamic_slice_in_dim(inverse_x, source * cells_x, cells_x, 1)
        return accum + jnp.einsum(
            "tkjn,tnm->tkjm", dense, kernel_rows, preferred_element_type=jnp.float32
        )

    summed_x = lax.fori_loop(0, sources, one_source, empty)
    along_x = summed_x.astype(jnp.bfloat16).reshape(layers, cells_y, cells_x)
    rows_y = layers // devices_y
    tracer_y = lax.axis_index("gy") * rows_y // LEV
    matrix_y = lax.dynamic_index_in_dim(inverse_y, tracer_y, 0, keepdims=False)
    product = jnp.einsum(
        "rjc,jm->rmc",
        lax.all_to_all(along_x, "gy", split_axis=0, concat_axis=1, tiled=True),
        matrix_y,
        preferred_element_type=jnp.float32,
    ).astype(jnp.bfloat16)
    along_y = lax.all_to_all(product, "gy", split_axis=1, concat_axis=0, tiled=True)
    mask_field = mask_flat.astype(jnp.float32)
    column_field = along_y.astype(jnp.float32).reshape(2, LEV, cell_count)
    solved = vertical_solve(column_field, vertical_coef.reshape(LEV, cell_count))
    increment = (
        (solved * mask_field[None, None, :]).astype(jnp.bfloat16).reshape(layers, cells_y, cells_x)
    )
    picked = increment.reshape(layers, cell_count)[:, columns]
    returned = lax.all_to_all(
        picked.reshape(layers, 1, devices_all, capacity),
        ("gx", "gy"),
        split_axis=2,
        concat_axis=1,
        tiled=True,
    )
    returned = returned.reshape(1, layers, slots)
    equivalents = jnp.where(live_flat[None, None, :], returned, jnp.zeros((), jnp.bfloat16))
    return (increment, equivalents)


def solution(mesh):
    in_specs = (
        P(("gx", "gy"), None, None),
        P(("gx", "gy"), None),
        P(("gx", "gy"), None),
        P("gy", "gx"),
        P(None, "gy", "gx"),
        P(None, None, "gx"),
        P(),
    )
    out_specs = (P(None, "gy", "gx"), P(("gx", "gy"), None, None))
    return jax.shard_map(body, mesh=mesh, in_specs=in_specs, out_specs=out_specs, check_vma=False)
```

profile of v0, /device:TPU:1, one launch (start us, length us, event | category | flops | bytes accessed | tf_op | source)
XLA Modules:
  0.0 277.1 jit_solution(8280165503097479602)
XLA Ops:
  7.2 1.0 copy.76
  8.2 0.7 iota_compare_fusion
  9.2 0.7 reshape.25774
  9.9 11.5 %all-to-all-start = ((bf16[128,2,128]{2,1,0:T(2,128)(2,1)}), bf16[128,2,128]{2,1,0:T(2,128)(2,1)S(1)}, u32[]{:S(2)}, u32[]{:S(2)}) async-start(bf16[128,2,128]{2,1,0:T(2,128)(2,1)} %reshape.25774), calls=%async_computation | async-start | bytes 131072 | tf_op jit(solution)/shard_map/all_to_all | solution.py:45
  21.5 1.5 slice_bitcast_fusion
  23.0 1.5 slice_bitcast_fusion.1
  24.6 0.7 copy.152
  25.3 0.7 compare_select_fusion.1
  28.2 0.6 negate_divide_fusion.25
  31.4 3.1 %gather_fusion = s32[512]{0:T(512)S(1)} fusion(s32[4096]{0:T(1024)S(1)} %bitcast.176, s32[1024]{0:T(1024)S(1)} %pad_clamp_fusion), kind=kCustom, calls=%fused_computation | custom fusion | bytes 6144 | tf_op jit(solution)/shard_map/gather | solution.py:55
  34.8 18.8 %all_gather.6 = s32[1,8192]{1,0:T(1,128)S(1)} all-gather(s32[1,512]{1,0:T(1,128)S(1)} %copy-done.56), channel_id=1, replica_groups=mesh['gx'=16,'gy'=8] {'gx'}, dimensions={1}, use_global_device_ids=true | all-gather | bytes 34816 | tf_op jit(solution)/shard_map/all_gather | solution.py:60
  53.7 0.8 broadcast_select_fusion.2
  54.6 0.6 negate_divide_fusion.15
  56.5 0.6 negate_divide_fusion.9
  57.8 0.6 negate_divide_fusion.4
  58.4 44.2 %all-gather.2.cloned.1.call-done = bf16[64,8192]{0,1:T(8,128)(2,1)} async-done(((bf16[64,512]{0,1:T(8,128)(2,1)}), bf16[64,8192]{0,1:T(8,128)(2,1)}) %all-gather.2.cloned.1.call-update) | async-done | bytes 1048592 | tf_op jit(solution)/shard_map/all_gather | solution.py:59
  102.7 108.7 %while.16 = (s32[]{:T(128)}, f32[2,32,16,256]{3,2,1,0:T(8,128)}, s32[1,8192]{1,0:T(1,128)S(1)}, bf16[64,8192]{0,1:T(8,128)(2,1)}, bf16[2,4096,256]{2,1,0:T(8,128...) while((s32[]{:T(128)}, f32[2,32,16,256]{3,2,1,0:T(8,128)}, ...), condition=%wide.region_2.3_spmd.clone, body=%wide.region_0.2_spmd.clone.sunk | while | flops 134809120 | bytes 6952396 | solution.py:78
  103.3 3.1 %scatter_custom_fusion.6 = f32[64,4096]{0,1:T(8,128)S(1)} fusion(s32[512]{0:T(512)S(1)} %bitcast.290, f32[]{:T(128)} %constant.118.clone.3..sunk, bf16[64,8192]{0,1:T(8,128)(2,1)} %get-tuple-element.392, s32[]{:T(128)} %constant.131.clone.1..sunk, s32[]{:T(128)S(6)} %select_n.111), kind=kCustom, calls=%fused_computation.4.clone.1 | custom fusion | flops 65536 | bytes 1180676 | tf_op jit(solution)/shard_map/while/body/eval_jaxpr/scatter-add | solution.py:69
  106.9 2.3 convolution_add_fusion.2
  109.8 3.1 %scatter_custom_fusion.6 = f32[64,4096]{0,1:T(8,128)S(1)} fusion(s32[512]{0:T(512)S(1)} %bitcast.290, f32[]{:T(128)} %constant.118.clone.3..sunk, bf16[64,8192]{0,1:T(8,128)(2,1)} %get-tuple-element.392, s32[]{:T(128)} %constant.131.clone.1..sunk, s32[]{:T(128)S(6)} %select_n.111), kind=kCustom, calls=%fused_computation.4.clone.1 | custom fusion | flops 65536 | bytes 1180676 | tf_op jit(solution)/shard_map/while/body/eval_jaxpr/scatter-add | solution.py:69
  113.3 2.6 convolution_add_fusion.2
  116.6 3.1 %scatter_custom_fusion.6 = f32[64,4096]{0,1:T(8,128)S(1)} fusion(s32[512]{0:T(512)S(1)} %bitcast.290, f32[]{:T(128)} %constant.118.clone.3..sunk, bf16[64,8192]{0,1:T(8,128)(2,1)} %get-tuple-element.392, s32[]{:T(128)} %constant.131.clone.1..sunk, s32[]{:T(128)S(6)} %select_n.111), kind=kCustom, calls=%fused_computation.4.clone.1 | custom fusion | flops 65536 | bytes 1180676 | tf_op jit(solution)/shard_map/while/body/eval_jaxpr/scatter-add | solution.py:69
  120.1 2.6 convolution_add_fusion.2
  123.4 3.1 %scatter_custom_fusion.6 = f32[64,4096]{0,1:T(8,128)S(1)} fusion(s32[512]{0:T(512)S(1)} %bitcast.290, f32[]{:T(128)} %constant.118.clone.3..sunk, bf16[64,8192]{0,1:T(8,128)(2,1)} %get-tuple-element.392, s32[]{:T(128)} %constant.131.clone.1..sunk, s32[]{:T(128)S(6)} %select_n.111), kind=kCustom, calls=%fused_computation.4.clone.1 | custom fusion | flops 65536 | bytes 1180676 | tf_op jit(solution)/shard_map/while/body/eval_jaxpr/scatter-add | solution.py:69
  127.0 2.6 convolution_add_fusion.2
  130.2 3.1 %scatter_custom_fusion.6 = f32[64,4096]{0,1:T(8,128)S(1)} fusion(s32[512]{0:T(512)S(1)} %bitcast.290, f32[]{:T(128)} %constant.118.clone.3..sunk, bf16[64,8192]{0,1:T(8,128)(2,1)} %get-tuple-element.392, s32[]{:T(128)} %constant.131.clone.1..sunk, s32[]{:T(128)S(6)} %select_n.111), kind=kCustom, calls=%fused_computation.4.clone.1 | custom fusion | flops 65536 | bytes 1180676 | tf_op jit(solution)/shard_map/while/body/eval_jaxpr/scatter-add | solution.py:69
  133.8 2.6 convolution_add_fusion.2
  137.0 3.1 %scatter_custom_fusion.6 = f32[64,4096]{0,1:T(8,128)S(1)} fusion(s32[512]{0:T(512)S(1)} %bitcast.290, f32[]{:T(128)} %constant.118.clone.3..sunk, bf16[64,8192]{0,1:T(8,128)(2,1)} %get-tuple-element.392, s32[]{:T(128)} %constant.131.clone.1..sunk, s32[]{:T(128)S(6)} %select_n.111), kind=kCustom, calls=%fused_computation.4.clone.1 | custom fusion | flops 65536 | bytes 1180676 | tf_op jit(solution)/shard_map/while/body/eval_jaxpr/scatter-add | solution.py:69
  140.6 2.6 convolution_add_fusion.2
  143.8 3.1 %scatter_custom_fusion.6 = f32[64,4096]{0,1:T(8,128)S(1)} fusion(s32[512]{0:T(512)S(1)} %bitcast.290, f32[]{:T(128)} %constant.118.clone.3..sunk, bf16[64,8192]{0,1:T(8,128)(2,1)} %get-tuple-element.392, s32[]{:T(128)} %constant.131.clone.1..sunk, s32[]{:T(128)S(6)} %select_n.111), kind=kCustom, calls=%fused_computation.4.clone.1 | custom fusion | flops 65536 | bytes 1180676 | tf_op jit(solution)/shard_map/while/body/eval_jaxpr/scatter-add | solution.py:69
  147.4 2.6 convolution_add_fusion.2
  150.6 3.1 %scatter_custom_fusion.6 = f32[64,4096]{0,1:T(8,128)S(1)} fusion(s32[512]{0:T(512)S(1)} %bitcast.290, f32[]{:T(128)} %constant.118.clone.3..sunk, bf16[64,8192]{0,1:T(8,128)(2,1)} %get-tuple-element.392, s32[]{:T(128)} %constant.131.clone.1..sunk, s32[]{:T(128)S(6)} %select_n.111), kind=kCustom, calls=%fused_computation.4.clone.1 | custom fusion | flops 65536 | bytes 1180676 | tf_op jit(solution)/shard_map/while/body/eval_jaxpr/scatter-add | solution.py:69
  154.2 2.6 convolution_add_fusion.2
  157.5 3.1 %scatter_custom_fusion.6 = f32[64,4096]{0,1:T(8,128)S(1)} fusion(s32[512]{0:T(512)S(1)} %bitcast.290, f32[]{:T(128)} %constant.118.clone.3..sunk, bf16[64,8192]{0,1:T(8,128)(2,1)} %get-tuple-element.392, s32[]{:T(128)} %constant.131.clone.1..sunk, s32[]{:T(128)S(6)} %select_n.111), kind=kCustom, calls=%fused_computation.4.clone.1 | custom fusion | flops 65536 | bytes 1180676 | tf_op jit(solution)/shard_map/while/body/eval_jaxpr/scatter-add | solution.py:69
  161.0 2.6 convolution_add_fusion.2
  164.3 3.1 %scatter_custom_fusion.6 = f32[64,4096]{0,1:T(8,128)S(1)} fusion(s32[512]{0:T(512)S(1)} %bitcast.290, f32[]{:T(128)} %constant.118.clone.3..sunk, bf16[64,8192]{0,1:T(8,128)(2,1)} %get-tuple-element.392, s32[]{:T(128)} %constant.131.clone.1..sunk, s32[]{:T(128)S(6)} %select_n.111), kind=kCustom, calls=%fused_computation.4.clone.1 | custom fusion | flops 65536 | bytes 1180676 | tf_op jit(solution)/shard_map/while/body/eval_jaxpr/scatter-add | solution.py:69
  167.8 2.6 convolution_add_fusion.2
  171.1 3.1 %scatter_custom_fusion.6 = f32[64,4096]{0,1:T(8,128)S(1)} fusion(s32[512]{0:T(512)S(1)} %bitcast.290, f32[]{:T(128)} %constant.118.clone.3..sunk, bf16[64,8192]{0,1:T(8,128)(2,1)} %get-tuple-element.392, s32[]{:T(128)} %constant.131.clone.1..sunk, s32[]{:T(128)S(6)} %select_n.111), kind=kCustom, calls=%fused_computation.4.clone.1 | custom fusion | flops 65536 | bytes 1180676 | tf_op jit(solution)/shard_map/while/body/eval_jaxpr/scatter-add | solution.py:69
  174.7 2.6 convolution_add_fusion.2
  177.9 3.1 %scatter_custom_fusion.6 = f32[64,4096]{0,1:T(8,128)S(1)} fusion(s32[512]{0:T(512)S(1)} %bitcast.290, f32[]{:T(128)} %constant.118.clone.3..sunk, bf16[64,8192]{0,1:T(8,128)(2,1)} %get-tuple-element.392, s32[]{:T(128)} %constant.131.clone.1..sunk, s32[]{:T(128)S(6)} %select_n.111), kind=kCustom, calls=%fused_computation.4.clone.1 | custom fusion | flops 65536 | bytes 1180676 | tf_op jit(solution)/shard_map/while/body/eval_jaxpr/scatter-add | solution.py:69
  181.5 2.6 convolution_add_fusion.2
  184.7 3.1 %scatter_custom_fusion.6 = f32[64,4096]{0,1:T(8,128)S(1)} fusion(s32[512]{0:T(512)S(1)} %bitcast.290, f32[]{:T(128)} %constant.118.clone.3..sunk, bf16[64,8192]{0,1:T(8,128)(2,1)} %get-tuple-element.392, s32[]{:T(128)} %constant.131.clone.1..sunk, s32[]{:T(128)S(6)} %select_n.111), kind=kCustom, calls=%fused_computation.4.clone.1 | custom fusion | flops 65536 | bytes 1180676 | tf_op jit(solution)/shard_map/while/body/eval_jaxpr/scatter-add | solution.py:69
  188.3 2.6 convolution_add_fusion.2
  191.5 3.1 %scatter_custom_fusion.6 = f32[64,4096]{0,1:T(8,128)S(1)} fusion(s32[512]{0:T(512)S(1)} %bitcast.290, f32[]{:T(128)} %constant.118.clone.3..sunk, bf16[64,8192]{0,1:T(8,128)(2,1)} %get-tuple-element.392, s32[]{:T(128)} %constant.131.clone.1..sunk, s32[]{:T(128)S(6)} %select_n.111), kind=kCustom, calls=%fused_computation.4.clone.1 | custom fusion | flops 65536 | bytes 1180676 | tf_op jit(solution)/shard_map/while/body/eval_jaxpr/scatter-add | solution.py:69
  195.1 2.6 convolution_add_fusion.2
  198.3 3.1 %scatter_custom_fusion.6 = f32[64,4096]{0,1:T(8,128)S(1)} fusion(s32[512]{0:T(512)S(1)} %bitcast.290, f32[]{:T(128)} %constant.118.clone.3..sunk, bf16[64,8192]{0,1:T(8,128)(2,1)} %get-tuple-element.392, s32[]{:T(128)} %constant.131.clone.1..sunk, s32[]{:T(128)S(6)} %select_n.111), kind=kCustom, calls=%fused_computation.4.clone.1 | custom fusion | flops 65536 | bytes 1180676 | tf_op jit(solution)/shard_map/while/body/eval_jaxpr/scatter-add | solution.py:69
  201.9 2.6 convolution_add_fusion.2
  205.1 3.1 %scatter_custom_fusion.6 = f32[64,4096]{0,1:T(8,128)S(1)} fusion(s32[512]{0:T(512)S(1)} %bitcast.290, f32[]{:T(128)} %constant.118.clone.3..sunk, bf16[64,8192]{0,1:T(8,128)(2,1)} %get-tuple-element.392, s32[]{:T(128)} %constant.131.clone.1..sunk, s32[]{:T(128)S(6)} %select_n.111), kind=kCustom, calls=%fused_computation.4.clone.1 | custom fusion | flops 65536 | bytes 1180676 | tf_op jit(solution)/shard_map/while/body/eval_jaxpr/scatter-add | solution.py:69
  208.7 2.6 convolution_add_fusion.2
  211.4 2.1 convert_element_type.59
  213.5 6.5 %all-to-all-start.1 = ((bf16[64,16,256]{2,1,0:T(8,128)(2,1)}), bf16[64,16,256]{2,1,0:T(8,128)(2,1)S(1)}, u32[]{:S(2)}, u32[]{:S(2)}) async-start(bf16[64,16,256]{2,1,0:T(8,128)(2,1)} %bitcast.8), calls=%async_computation.1 | async-start | bytes 1048576 | tf_op jit(solution)/shard_map/all_to_all | solution.py:85
  220.0 0.6 negate_divide_fusion.5
  220.8 8.6 %all-to-all-done.1 = bf16[64,16,256]{2,1,0:T(8,128)(2,1)S(1)} async-done(((bf16[64,16,256]{2,1,0:T(8,128)(2,1)}), bf16[64,16,256]{2,1,0:T(8,128)(2,1)S(1)}, u32[]{:S(2)}, u32[]{:S(2)}) %all-to-all-start.1) | async-done | bytes 524320 | tf_op jit(solution)/shard_map/all_to_all | solution.py:85
  229.8 1.1 copy.79
  230.8 4.4 %all-to-all-start.2 = ((bf16[8,128,256]{2,0,1:T(8,128)(2,1)}), bf16[8,128,256]{2,0,1:T(8,128)(2,1)S(1)}, u32[]{:S(2)}, u32[]{:S(2)}) async-start(bf16[8,128,256]{2,0,1:T(8,128)(2,1)} %copy.79), calls=%async_computation.2 | async-start | bytes 1048576 | tf_op jit(solution)/shard_map/all_to_all | solution.py:89
  237.6 7.0 %all-to-all-done.2 = bf16[8,128,256]{2,0,1:T(8,128)(2,1)S(1)} async-done(((bf16[8,128,256]{2,0,1:T(8,128)(2,1)}), bf16[8,128,256]{2,0,1:T(8,128)(2,1)S(1)}, u32[]{:S(2)}, u32[]{:S(2)}) %all-to-all-start.2) | async-done | bytes 524320 | tf_op jit(solution)/shard_map/all_to_all | solution.py:89
  246.3 1.6 fusion.17
  248.1 0.8 constant_dynamic-update-slice_fusion.31
  251.6 1.3 gather_fusion.1
  253.0 0.7 reshape.25776
  253.7 6.0 %all-to-all-start.3 = ((bf16[128,2,128]{2,1,0:T(2,128)(2,1)}), bf16[128,2,128]{2,1,0:T(2,128)(2,1)S(1)}, u32[]{:S(2)}, u32[]{:S(2)}) async-start(bf16[128,2,128]{2,1,0:T(2,128)(2,1)} %reshape.25776), calls=%async_computation.3 | async-start | bytes 131072 | tf_op jit(solution)/shard_map/all_to_all | solution.py:97
  259.7 0.9 fusion.10
  260.6 8.6 %all-to-all-done.3 = bf16[128,2,128]{2,1,0:T(2,128)(2,1)S(1)} async-done(((bf16[128,2,128]{2,1,0:T(2,128)(2,1)}), bf16[128,2,128]{2,1,0:T(2,128)(2,1)S(1)}, u32[]{:S(2)}, u32[]{:S(2)}) %all-to-all-start.3) | async-done | bytes 65568 | tf_op jit(solution)/shard_map/all_to_all | solution.py:97
  269.5 0.7 copy.117
  (338 shorter events, 30.7 us)
Async XLA Ops:
  7.2 222.3 %copy-start = (bf16[2,128,128]{2,1,0:T(8,128)(2,1)S(1)}, bf16[2,128,128]{2,1,0:T(8,128)(2,1)}, u32[]{:S(2)}) copy-start(bf16[2,128,128]{2,1,0:T(8,128)(2,1)} %param.15) | copy-start | bytes 196612
  9.0 12.4 %copy-start.57 = (pred[512]{0:T(512)(128)(4,1)}, pred[512]{0:T(512)(128)(4,1)S(1)}, u32[]{:S(2)}) copy-start(pred[512]{0:T(512)(128)(4,1)S(1)} %lt.82) | copy-start | bytes 1540
  9.9 43.7 %all-to-all-start = ((bf16[128,2,128]{2,1,0:T(2,128)(2,1)}), bf16[128,2,128]{2,1,0:T(2,128)(2,1)S(1)}, u32[]{:S(2)}, u32[]{:S(2)}) async-start(bf16[128,2,128]{2,1,0:T(2,128)(2,1)} %reshape.25774), calls=%async_computation | async-start | bytes 131072 | tf_op jit(solution)/shard_map/all_to_all | solution.py:45
  21.4 81.2 %all-gather.2.cloned.1.call-start = ((), (), s32[]{:S(2)}) async-start(), calls=%async_computation.4 | async-start | bytes 2228224 | tf_op jit(solution)/shard_map/all_gather | solution.py:59
  26.0 8.6 %copy-start.54 = (s32[1024]{0:T(1024)}, s32[1024]{0:T(1024)S(1)}, u32[]{:S(2)}) copy-start(s32[1024]{0:T(1024)S(1)} %pad_clamp_fusion) | copy-start | bytes 12292
  26.2 8.7 %copy-start.56 = (s32[1,512]{1,0:T(1,128)S(1)}, s32[1,512]{1,0:T(1,128)}, u32[]{:S(2)}) copy-start(s32[1,512]{1,0:T(1,128)} %param.10) | copy-start | bytes 6148
  30.1 27.6 %copy-start.1 = (f32[4096]{0:T(1024)}, f32[4096]{0:T(1024)S(1)}, u32[]{:S(2)}) copy-start(f32[4096]{0:T(1024)S(1)} %get-tuple-element.208) | copy-start | bytes 49156
  30.8 25.7 %copy-start.5 = (f32[4096]{0:T(1024)}, f32[4096]{0:T(1024)S(1)}, u32[]{:S(2)}) copy-start(f32[4096]{0:T(1024)S(1)} %get-tuple-element.211) | copy-start | bytes 49156
  30.8 26.3 %copy-start.3 = (f32[4096]{0:T(1024)}, f32[4096]{0:T(1024)S(1)}, u32[]{:S(2)}) copy-start(f32[4096]{0:T(1024)S(1)} %get-tuple-element.210) | copy-start | bytes 49156
  34.6 21.2 %copy-start.7 = (f32[4096]{0:T(1024)}, f32[4096]{0:T(1024)S(1)}, u32[]{:S(2)}) copy-start(f32[4096]{0:T(1024)S(1)} %get-tuple-element.213) | copy-start | bytes 49156
  34.6 68.0 %copy-start.9 = (f32[4096]{0:T(1024)}, f32[4096]{0:T(1024)S(1)}, u32[]{:S(2)}) copy-start(f32[4096]{0:T(1024)S(1)} %get-tuple-element.214) | copy-start | bytes 49156
  34.6 68.0 %copy-start.11 = (f32[4096]{0:T(1024)}, f32[4096]{0:T(1024)S(1)}, u32[]{:S(2)}) copy-start(f32[4096]{0:T(1024)S(1)} %get-tuple-element.216) | copy-start | bytes 49156
  34.6 68.0 %copy-start.13 = (f32[4096]{0:T(1024)}, f32[4096]{0:T(1024)S(1)}, u32[]{:S(2)}) copy-start(f32[4096]{0:T(1024)S(1)} %get-tuple-element.217) | copy-start | bytes 49156
  55.8 46.8 %copy-start.15 = (f32[4096]{0:T(1024)}, f32[4096]{0:T(1024)S(1)}, u32[]{:S(2)}) copy-start(f32[4096]{0:T(1024)S(1)} %get-tuple-element.219) | copy-start | bytes 49156
  55.8 46.8 %copy-start.17 = (f32[4096]{0:T(1024)}, f32[4096]{0:T(1024)S(1)}, u32[]{:S(2)}) copy-start(f32[4096]{0:T(1024)S(1)} %get-tuple-element.220) | copy-start | bytes 49156
  56.5 46.2 %copy-start.19 = (f32[4096]{0:T(1024)}, f32[4096]{0:T(1024)S(1)}, u32[]{:S(2)}) copy-start(f32[4096]{0:T(1024)S(1)} %get-tuple-element.222) | copy-start | bytes 49156
  56.5 46.2 %copy-start.21 = (f32[4096]{0:T(1024)}, f32[4096]{0:T(1024)S(1)}, u32[]{:S(2)}) copy-start(f32[4096]{0:T(1024)S(1)} %get-tuple-element.223) | copy-start | bytes 49156
  57.1 45.5 %copy-start.23 = (f32[4096]{0:T(1024)}, f32[4096]{0:T(1024)S(1)}, u32[]{:S(2)}) copy-start(f32[4096]{0:T(1024)S(1)} %get-tuple-element.225) | copy-start | bytes 49156
  57.2 45.5 %copy-start.25 = (f32[4096]{0:T(1024)}, f32[4096]{0:T(1024)S(1)}, u32[]{:S(2)}) copy-start(f32[4096]{0:T(1024)S(1)} %get-tuple-element.226) | copy-start | bytes 49156
  106.9 2.3 copy-start.53
  113.3 2.6 copy-start.53
  120.1 2.6 copy-start.53
  127.0 2.6 copy-start.53
  133.8 2.6 copy-start.53
  140.6 2.6 copy-start.53
  147.4 2.6 copy-start.53
  154.2 2.6 copy-start.53
  161.0 2.6 copy-start.53
  167.8 2.6 copy-start.53
  174.6 2.6 copy-start.53
  181.5 2.6 copy-start.53
  188.3 2.6 copy-start.53
  195.1 2.6 copy-start.53
  201.9 2.6 copy-start.53
  208.7 2.6 copy-start.53
  211.3 8.7 %copy-start.28 = (f32[4096]{0:T(1024)S(1)}, f32[4096]{0:T(1024)}, u32[]{:S(2)}) copy-start(f32[4096]{0:T(1024)} %get-tuple-element.229) | copy-start | bytes 49156
  211.3 9.3 %copy-start.49 = (f32[2,2,8,128]{3,2,1,0:T(8,128)S(1)}, f32[2,2,8,128]{3,2,1,0:T(8,128)}, u32[]{:S(2)}) copy-start(f32[2,2,8,128]{3,2,1,0:T(8,128)} %get-tuple-element.296) | copy-start | bytes 49156
  211.3 9.3 %copy-start.48 = (f32[2,2,8,128]{3,2,1,0:T(8,128)S(1)}, f32[2,2,8,128]{3,2,1,0:T(8,128)}, u32[]{:S(2)}) copy-start(f32[2,2,8,128]{3,2,1,0:T(8,128)} %get-tuple-element.297) | copy-start | bytes 49156
  211.4 9.3 %copy-start.51 = (f32[2,2,8,128]{3,2,1,0:T(8,128)S(1)}, f32[2,2,8,128]{3,2,1,0:T(8,128)}, u32[]{:S(2)}) copy-start(f32[2,2,8,128]{3,2,1,0:T(8,128)} %get-tuple-element.314) | copy-start | bytes 49156
  211.4 9.3 %copy-start.47 = (f32[2,2,8,128]{3,2,1,0:T(8,128)S(1)}, f32[2,2,8,128]{3,2,1,0:T(8,128)}, u32[]{:S(2)}) copy-start(f32[2,2,8,128]{3,2,1,0:T(8,128)} %get-tuple-element.295) | copy-start | bytes 49156
  211.4 9.4 %copy-start.27 = (f32[4096]{0:T(1024)S(1)}, f32[4096]{0:T(1024)}, u32[]{:S(2)}) copy-start(f32[4096]{0:T(1024)} %get-tuple-element.228) | copy-start | bytes 49156
  213.5 15.9 %all-to-all-start.1 = ((bf16[64,16,256]{2,1,0:T(8,128)(2,1)}), bf16[64,16,256]{2,1,0:T(8,128)(2,1)S(1)}, u32[]{:S(2)}, u32[]{:S(2)}) async-start(bf16[64,16,256]{2,1,0:T(8,128)(2,1)} %bitcast.8), calls=%async_computation.1 | async-start | bytes 1048576 | tf_op jit(solution)/shard_map/all_to_all | solution.py:85
  229.4 6.4 %copy-start.50 = (s32[16,256]{1,0:T(8,128)S(1)}, s32[16,256]{1,0:T(8,128)}, u32[]{:S(2)}) copy-start(s32[16,256]{1,0:T(8,128)} %param.12) | copy-start | bytes 49156
  230.8 13.7 %all-to-all-start.2 = ((bf16[8,128,256]{2,0,1:T(8,128)(2,1)}), bf16[8,128,256]{2,0,1:T(8,128)(2,1)S(1)}, u32[]{:S(2)}, u32[]{:S(2)}) async-start(bf16[8,128,256]{2,0,1:T(8,128)(2,1)} %copy.79), calls=%async_computation.2 | async-start | bytes 1048576 | tf_op jit(solution)/shard_map/all_to_all | solution.py:89
  244.7 1.4 copy-start.2
  245.4 2.5 copy-start.29
  245.4 2.5 copy-start.30
  245.5 2.5 copy-start.31
  245.5 2.5 copy-start.32
  245.5 2.5 copy-start.33
  245.5 2.5 copy-start.34
  245.5 2.5 copy-start.35
  245.5 2.5 copy-start.36
  245.5 2.5 copy-start.37
  245.5 2.5 copy-start.38
  245.5 2.5 copy-start.39
  245.5 2.5 copy-start.40
  245.6 2.5 copy-start.41
  245.6 2.5 copy-start.42
  245.6 2.5 copy-start.43
  245.6 2.5 copy-start.46
  250.9 8.7 %copy-start.44 = (f32[16,256]{1,0:T(8,128)S(1)}, f32[16,256]{1,0:T(8,128)}, u32[]{:S(2)}) copy-start(f32[16,256]{1,0:T(8,128)} %convert_element_type.66) | copy-start | bytes 49156
  251.0 18.3 %copy-start.58 = (pred[512]{0:T(512)(128)(4,1)S(1)}, pred[512]{0:T(512)(128)(4,1)}, u32[]{:S(2)}) copy-start(pred[512]{0:T(512)(128)(4,1)} %copy-done.57) | copy-start | bytes 1540
  253.7 15.6 %all-to-all-start.3 = ((bf16[128,2,128]{2,1,0:T(2,128)(2,1)}), bf16[128,2,128]{2,1,0:T(2,128)(2,1)S(1)}, u32[]{:S(2)}, u32[]{:S(2)}) async-start(bf16[128,2,128]{2,1,0:T(2,128)(2,1)} %reshape.25776), calls=%async_computation.3 | async-start | bytes 131072 | tf_op jit(solution)/shard_map/all_to_all | solution.py:97
  (30 other events, 28.8 us)
Sparse Core Ops, SparseCore 0:
  54.7 47.8 all-gather.1
where the time goes:
time: 278 us; the launch traced here: 277 us
  other arithmetic  72.2 us (26%)
  waiting for transfers between devices  68.4 us (25%)
  matrix products  41.8 us (15%)
  local copies, waits for them, and re-layouts  31.4 us (11%)
  starting transfers between devices  28.4 us (10%)
  blocking collectives  18.8 us (7%)
  between operations  15.4 us (6%)
    scatter-add x16, other arithmetic, one_source(): dense = jnp.zeros((layers, cell_count), jnp.float32).at[:, block_columns]...  49.9 us
    all_gather x1, waiting for transfers between devices, body(): values_piece = lax.all_gather(line_values, 'gx', axis=1, tiled=True)  44.2 us
    dot_general x16, matrix products, one_source(): jnp.einsum('tkjn,tnm->tkjm', dense, kernel_rows, preferred_element_type=j...  41.5 us
    all_gather x1, blocking collectives, body(): columns_piece = lax.all_gather(line_columns, 'gx', axis=1, tiled=True)  18.8 us
    all_to_all x1, starting transfers between devices, body(): lax.all_to_all(outgoing.reshape(layers, 1, devices_all, capacity), ('gx',...  11.5 us
    while x80, local copies, waits for them, and re-layouts  11.4 us
    div x30, other arithmetic, vertical_solve(): ratios.append(-upper_coef / denominator)  10.7 us
    all_to_all x1, waiting for transfers between devices, body(): lax.all_to_all(picked.reshape(layers, 1, devices_all, capacity), ('gx', '...  8.63 us
  transfers between devices with their start and end apart: 5, of which 4 were waited for; matrix products, arithmetic and copies ran while one was open for 7% of the time, Pallas kernels for 0%

commit v1 on v0

v1 whole, which is shorter than its diff:
```python
import functools
import jax
import jax.numpy as jnp
from jax import lax
from jax.experimental import pallas as pl
from jax.experimental.pallas import tpu as pltpu
from jax.sharding import PartitionSpec as P

LEV = 32
CAP = 4
CY = 16
CX = 256
LAYERS = 64
NY = 128
N_GX = 16
N_GY = 8
DEV = 128
SLOTS = DEV * CAP
SHARE = LAYERS // N_GY
ROWS = 40
BF = jnp.bfloat16
F32 = jnp.float32
I32 = jnp.int32


def iota(shape, dim):
    return lax.broadcasted_iota(I32, shape, dim)


def one_hot(cond):
    return jnp.where(cond, 1.0, 0.0).astype(BF)


def dot(a, b, dims=((1,), (0,))):
    return lax.dot_general(a, b, (dims, ((), ())), preferred_element_type=F32)


def send_kernel(inn_ref, col_ref, cnt_ref, mask_ref, out_ref):
    counts = jnp.broadcast_to(cnt_ref[...], (8, DEV)).astype(F32).astype(BF)
    spread = one_hot(iota((DEV, SLOTS), 1) // CAP == iota((DEV, SLOTS), 0))
    count_lane = dot(counts, spread)[0:1, :]
    slot_lane = (iota((1, SLOTS), 1) % CAP).astype(F32)
    live = slot_lane < count_lane
    values = jnp.where(live, inn_ref[0].astype(F32), 0.0).astype(BF)
    cells = col_ref[...]
    row = cells // CX
    col = cells % CX
    pick_col = one_hot(iota((CX, SLOTS), 0) == col)
    sea_rows = dot(mask_ref[...].astype(F32).astype(BF), pick_col)
    sea = jnp.sum(jnp.where(iota((CY, SLOTS), 0) == row, sea_rows, 0.0), axis=0, keepdims=True)
    row_code = jnp.where(sea > 0.5, row.astype(F32), 255.0)
    codes = jnp.where(
        iota((8, SLOTS), 0) == 0,
        jnp.broadcast_to(row_code, (8, SLOTS)),
        jnp.broadcast_to(col.astype(F32), (8, SLOTS)),
    ).astype(BF)
    source = iota((SLOTS, SLOTS), 0)
    target = iota((SLOTS, SLOTS), 1)
    permute = one_hot((source % CAP) * DEV + source // CAP == target)
    moved = dot(codes, permute)
    tile = jnp.concatenate(
        [moved[0:1, c * DEV : (c + 1) * DEV] for c in range(CAP)]
        + [moved[1:2, c * DEV : (c + 1) * DEV] for c in range(CAP)],
        axis=0,
    ).astype(BF)
    for b in range(N_GY):
        block = values[b * SHARE : (b + 1) * SHARE, :]
        message = jnp.concatenate(
            [block[:, q * DEV : (q + 1) * DEV] for q in range(CAP)] + [tile], axis=0
        )
        for a in range(N_GX):
            out_ref[a * N_GY + b] = message


def smooth_kernel(tracer_ref, got_ref, kx_ref, ky_ref, out_ref, wide_ref, turned_ref, dense_ref, acc_ref):
    step = pl.program_id(0)

    @pl.when(step == 0)
    def _():
        acc_ref[...] = jnp.zeros_like(acc_ref)

        def widen(s, carry):
            wide_ref[pl.ds(pl.multiple_of(s * 32, 32), 32), :] = got_ref[s, 0:32, :].astype(F32)
            return carry

        lax.fori_loop(0, DEV, widen, 0, unroll=8)
        for q in range(CAP):
            for l in range(SHARE):
                block = wide_ref[pl.ds(q * SHARE + l, DEV, stride=32), :]
                turned_ref[pl.ds(q * DEV * SHARE + l, DEV, stride=SHARE), :] = block.T

    col_iota = iota((CX, DEV), 0).astype(F32).astype(BF)
    half_iota = (iota((2 * SHARE, DEV), 0) // SHARE).astype(F32).astype(BF)
    zero = jnp.zeros((), BF)
    one = jnp.ones((), BF)
    for b in range(N_GY):
        owner = step * N_GY + b
        codes = got_ref[owner, 32:40, :].astype(F32)
        left = [[] for _ in range(N_GY)]
        right = []
        for c in range(CAP):
            base = pl.multiple_of(owner * (CAP * SHARE) + c * SHARE, SHARE)
            v = turned_ref[pl.ds(base, SHARE), :]
            twice = jnp.concatenate([v, v], axis=0).astype(BF)
            row = jnp.broadcast_to(codes[c : c + 1, :], (2 * SHARE, DEV)).astype(BF)
            pair = row - half_iota
            for k in range(CY // 2):
                left[k].append(jnp.where(pair == jnp.asarray(2 * k, BF), twice, zero))
            col = jnp.broadcast_to(codes[CAP + c : CAP + c + 1, :], (CX, DEV)).astype(BF)
            right.append(jnp.where(col == col_iota, one, zero))
        lhs = jnp.concatenate([jnp.concatenate(x, axis=1) for x in left], axis=0)
        rhs = jnp.concatenate(right, axis=1)
        dense = dot(lhs, rhs, ((1,), (1,)))
        dense_ref[b * 128 : (b + 1) * 128, :] = dense.astype(BF)
    gain = dot(dense_ref[...], kx_ref[0])
    for h in range(2):
        acc_ref[h * 1024 : (h + 1) * 1024, :] += gain[:, h * 128 : (h + 1) * 128]

    @pl.when(step == N_GX - 1)
    def _():
        for l in range(SHARE):
            along_x = jnp.concatenate(
                [acc_ref[pl.ds(h * 1024 + l, NY, stride=SHARE), :] for h in range(2)], axis=1
            ).astype(BF)
            along_y = dot(ky_ref[0], along_x, ((0,), (0,))).astype(BF)
            for b in range(N_GY):
                out_ref[b, l] = along_y[b * CY : (b + 1) * CY, :]


def solve_kernel(field_ref, coef_ref, mask_ref, col_ref, inc_ref, pick_ref, part_ref, ratio_ref):
    mask = mask_ref[...].astype(F32)
    prev0 = prev1 = ratio = None
    for k in range(LEV):
        here = coef_ref[k]
        below = coef_ref[k + 1] if k + 1 < LEV else jnp.zeros_like(here)
        f0 = field_ref[k].astype(F32)
        f1 = field_ref[LEV + k].astype(F32)
        diagonal = 1.0 + here + below
        if k == 0:
            inv = 1.0 / diagonal
            prev0 = f0 * inv
            prev1 = f1 * inv
        else:
            inv = 1.0 / (diagonal + here * ratio)
            prev0 = (f0 + here * prev0) * inv
            prev1 = (f1 + here * prev1) * inv
        ratio = -below * inv
        ratio_ref[k] = ratio
        part_ref[k] = prev0
        part_ref[LEV + k] = prev1
    x0 = x1 = None
    for k in range(LEV - 1, -1, -1):
        if k == LEV - 1:
            x0 = part_ref[k]
            x1 = part_ref[LEV + k]
        else:
            x0 = part_ref[k] - ratio_ref[k] * x0
            x1 = part_ref[LEV + k] - ratio_ref[k] * x1
        inc_ref[k] = (x0 * mask).astype(BF)
        inc_ref[LEV + k] = (x1 * mask).astype(BF)
    cells = col_ref[...]
    row = cells // CX
    col = cells % CX
    pick_col = one_hot(iota((CX, SLOTS), 0) == col)
    row_iota = iota((LAYERS * CY, SLOTS), 0) % CY
    found = dot(inc_ref[...].reshape(LAYERS * CY, CX), pick_col)
    chosen = jnp.where(row_iota == row, found, 0.0).astype(BF)
    total = one_hot(iota((LAYERS, LAYERS * CY), 1) // CY == iota((LAYERS, LAYERS * CY), 0))
    pick_ref[...] = dot(chosen, total, ((0,), (1,))).astype(BF)


def call(kernel, out_shape, n_in, name, scratch=()):
    return pl.pallas_call(
        kernel,
        out_shape=out_shape,
        in_specs=[pl.BlockSpec(memory_space=pltpu.VMEM)] * n_in,
        out_specs=jax.tree.map(lambda _: pl.BlockSpec(memory_space=pltpu.VMEM), out_shape),
        scratch_shapes=list(scratch),
        name=name,
    )


def body(innovations, station_columns, profile_counts, land_mask, vertical_coef, inverse_x, inverse_y):
    everyone = ("gx", "gy")
    message = call(send_kernel, jax.ShapeDtypeStruct((DEV, ROWS, DEV), BF), 4, "send")(
        innovations, station_columns, profile_counts, land_mask
    )
    got = lax.all_to_all(message, everyone, split_axis=0, concat_axis=0, tiled=True)
    tracer = (lax.axis_index("gy") * SHARE // LEV).reshape(1).astype(I32)
    product = pl.pallas_call(
        smooth_kernel,
        out_shape=jax.ShapeDtypeStruct((N_GY, SHARE, CY, CX), BF),
        grid_spec=pltpu.PrefetchScalarGridSpec(
            num_scalar_prefetch=1,
            grid=(N_GX,),
            in_specs=[
                pl.BlockSpec((DEV, ROWS, DEV), lambda i, t: (0, 0, 0), pipeline_mode=pl.Buffered(1)),
                pl.BlockSpec((1, CX, CX), lambda i, t: (t[0], i, 0)),
                pl.BlockSpec((1, NY, NY), lambda i, t: (t[0], 0, 0)),
            ],
            out_specs=pl.BlockSpec((N_GY, SHARE, CY, CX), lambda i, t: (0, 0, 0, 0)),
            scratch_shapes=[
                pltpu.VMEM((DEV * 32, DEV), F32),
                pltpu.VMEM((SLOTS * SHARE, DEV), F32),
                pltpu.VMEM((NY * SHARE, CX), BF),
                pltpu.VMEM((2 * NY * SHARE, 128), F32),
            ],
        ),
        compiler_params=pltpu.CompilerParams(dimension_semantics=("arbitrary",)),
        name="smooth",
    )(tracer, got, inverse_x, inverse_y)
    along_y = lax.all_to_all(product, "gy", split_axis=0, concat_axis=0, tiled=True)
    increment, picked = call(
        solve_kernel,
        (jax.ShapeDtypeStruct((LAYERS, CY, CX), BF), jax.ShapeDtypeStruct((SLOTS, LAYERS), BF)),
        4,
        "solve",
        [pltpu.VMEM((LAYERS, CY, CX), F32), pltpu.VMEM((LEV, CY, CX), F32)],
    )(along_y.reshape(LAYERS, CY, CX), vertical_coef, land_mask, station_columns)
    returned = lax.all_to_all(
        picked.reshape(DEV, 2, 128), everyone, split_axis=0, concat_axis=0, tiled=True
    )
    returned = returned.reshape(SLOTS, LAYERS).T.reshape(1, LAYERS, SLOTS)
    slot_index = lax.broadcasted_iota(I32, (DEV, CAP), 1)
    live = (slot_index < profile_counts[0][:, None]).reshape(SLOTS)
    equivalents = jnp.where(live[None, None, :], returned, jnp.zeros((), BF))
    return increment, equivalents


def solution(mesh):
    in_specs = (
        P(("gx", "gy"), None, None),
        P(("gx", "gy"), None),
        P(("gx", "gy"), None),
        P("gy", "gx"),
        P(None, "gy", "gx"),
        P(None, None, "gx"),
        P(),
    )
    out_specs = (P(None, "gy", "gx"), P(("gx", "gy"), None, None))
    return jax.shard_map(body, mesh=mesh, in_specs=in_specs, out_specs=out_specs, check_vma=False)
```

time: 278 us -> 92.8 us (0.33)
  other arithmetic: 72.2 us -> 0.22 us
  matrix products: 41.8 us -> 0 us
  waiting for transfers between devices: 68.4 us -> 31 us
  local copies, waits for them, and re-layouts: 31.4 us -> 3.68 us
  Pallas kernels: 0 us -> 25.8 us
  between operations: 15.4 us -> 0.7 us
  starting transfers between devices: 28.4 us -> 15.9 us
  blocking collectives: 18.8 us -> 15 us
    scatter-add x16 -> x0, other arithmetic: 49.9 us -> none  [one_source(): dense = jnp.zeros((layers, cell_count), jnp.float32).at[:, block_columns]...]
    all_gather x1 -> x0, waiting for transfers between devices: 44.2 us -> none  [body(): values_piece = lax.all_gather(line_values, 'gx', axis=1, tiled=True)]
    dot_general x17 -> x0, matrix products: 41.8 us -> none  [the longest x16 41.5 us: one_source(): jnp.einsum('tkjn,tnm->tkjm', dense, kernel_rows, preferred_element_type=j...]
    pallas_call x0 -> x3, Pallas kernels: none -> 25.8 us  [the longest x1 20 us: body(): pl.pallas_call(smooth_kernel, out_shape=jax.ShapeDtypeStruct((N_GY, SHARE...]
    all_gather x1 -> x0, blocking collectives: 18.8 us -> none  [body(): columns_piece = lax.all_gather(line_columns, 'gx', axis=1, tiled=True)]
    all_to_all x0 -> x1, blocking collectives: none -> 15 us  [body(): lax.all_to_all(product, 'gy', split_axis=0, concat_axis=0, tiled=True)]
    all_to_all x4 -> x2, starting transfers between devices: 28.3 us -> 15.9 us  [the longest x1 11.5 us: body(): lax.all_to_all(message, everyone, split_axis=0, concat_axis=0, tiled=True)]
    div x31 -> x0, other arithmetic: 12.3 us -> none  [the longest x30 10.7 us: vertical_solve(): ratios.append(-upper_coef / denominator)]
  transfers between devices with their start and end apart: 5 -> 2, of which waited for: 4 -> 2; matrix products, arithmetic and copies ran while one was open for 7% -> 0% of each run, Pallas kernels for 0% -> 0%
where the time goes in v1:
time: 92.8 us; the launch traced here: 92.3 us
  waiting for transfers between devices  31 us (33%)
  Pallas kernels  25.8 us (28%)
  starting transfers between devices  15.9 us (17%)
  blocking collectives  15 us (16%)
  local copies, waits for them, and re-layouts  3.68 us (4%)
    all_to_all x1, waiting for transfers between devices, body(): lax.all_to_all(message, everyone, split_axis=0, concat_axis=0, tiled=True)  21.5 us
    pallas_call x1, Pallas kernels, body(): pl.pallas_call(smooth_kernel, out_shape=jax.ShapeDtypeStruct((N_GY, SHARE...  20 us
    all_to_all x1, blocking collectives, body(): lax.all_to_all(product, 'gy', split_axis=0, concat_axis=0, tiled=True)  15 us
    all_to_all x1, starting transfers between devices, body(): lax.all_to_all(message, everyone, split_axis=0, concat_axis=0, tiled=True)  11.5 us
    all_to_all x1, waiting for transfers between devices, body(): lax.all_to_all(picked.reshape(DEV, 2, 128), everyone, split_axis=0, conca...  9.48 us
    all_to_all x1, starting transfers between devices, body(): lax.all_to_all(picked.reshape(DEV, 2, 128), everyone, split_axis=0, conca...  4.42 us
    pallas_call x1, Pallas kernels, body(): call(solve_kernel, (jax.ShapeDtypeStruct((LAYERS, CY, CX), BF), jax.Shape...  3.31 us
    pallas_call x1, Pallas kernels, body(): call(send_kernel, jax.ShapeDtypeStruct((DEV, ROWS, DEV), BF), 4, 'send')  2.46 us
  transfers between devices with their start and end apart: 2, of which 2 were waited for; matrix products, arithmetic and copies ran while one was open for 0% of the time, Pallas kernels for 0%

profile of v1, /device:TPU:1, one launch (start us, length us, event | category | flops | bytes accessed | tf_op | source)
XLA Modules:
  0.0 92.3 jit_solution(8342252573155829683)
XLA Ops:
  0.6 2.5 %send.1 = bf16[128,40,128]{2,1,0:T(8,128)(2,1)} custom-call(bf16[1,64,512]{2,1,0:T(8,128)(2,1)} %inn_ref.1, s32[1,512]{1,0:T(1,128)} %col_ref.3, s32[1,128]{1,0:T(1,128)} %cnt_ref.1, s32[16,256]{1,0:T(8,128)} %mask_ref.3), custom_call_target="tpu_custom_call" | custom-call | tf_op jit(solution)/shard_map/send/pallas_call | solution.py:185
  3.1 11.5 %all-to-all-start = ((bf16[128,40,128]{2,1,0:T(8,128)(2,1)}), bf16[128,40,128]{2,1,0:T(8,128)(2,1)S(1)}, u32[]{:S(2)}, u32[]{:S(2)}) async-start(bf16[128,40,128]{2,1,0:T(8,128)(2,1)} %send.1), calls=%async_computation | async-start | bytes 2621440 | tf_op jit(solution)/shard_map/all_to_all | solution.py:188
  14.6 21.5 %all-to-all-done.got_ref = bf16[128,40,128]{2,1,0:T(8,128)(2,1)S(1)} async-done(((bf16[128,40,128]{2,1,0:T(8,128)(2,1)}), bf16[128,40,128]{2,1,0:T(8,128)(2,1)S(1)}, u32[]{:S(2)}, u32[]{:S(2)}) %all-to-all-start) | async-done | bytes 1310752 | tf_op jit(solution)/shard_map/all_to_all | solution.py:188
  36.1 0.0 copy-start
  36.1 1.1 %copy-done = bf16[128,40,128]{2,1,0:T(8,128)(2,1)} copy-done((bf16[128,40,128]{2,1,0:T(8,128)(2,1)}, bf16[128,40,128]{2,1,0:T(8,128)(2,1)S(1)}, u32[]{:S(2)}) %copy-start) | copy-done | bytes 1310744
  37.2 20.0 %smooth.1 = bf16[8,8,16,256]{3,2,1,0:T(8,128)(2,1)} custom-call(s32[1]{0:T(128)} %bitcast.tracer_ref, bf16[128,40,128]{2,1,0:T(8,128)(2,1)} %copy-done, bf16[2,4096,256]{2,1,0:T(8,128)(2,1)} %kx_ref.1, bf16[2,128,128]{2,1,0:T(8,128)(2,1)} %ky_ref.1), custom_call_target="tpu_custom_call" | custom-call | tf_op jit(solution)/shard_map/smooth/pallas_call | solution.py:190
  57.2 0.0 copy-start.1
  57.2 15.0 %all_to_all.15 = bf16[8,8,16,256]{3,2,1,0:T(8,128)(2,1)} all-to-all(bf16[8,8,16,256]{3,2,1,0:T(8,128)(2,1)} %smooth.1), channel_id=1, replica_groups=mesh['gx'=16,'gy'=8] {'gy'}, dimensions={0} | all-to-all | bytes 1048576 | tf_op jit(solution)/shard_map/all_to_all | solution.py:212
  72.2 3.3 %solve.1 = (bf16[64,16,256]{2,1,0:T(8,128)(2,1)}, bf16[512,64]{1,0:T(8,128)(2,1)}) custom-call(bf16[64,16,256]{2,1,0:T(8,128)(2,1)} %bitcast.7, f32[32,16,256]{2,1,0:T(8,128)} %coef_ref.1, s32[16,256]{1,0:T(8,128)} %mask_ref.3, s32[1,512]{1,0:T(1,128)} %col_ref.3), custom_call_target="tpu_custom_call" | custom-call | tf_op jit(solution)/shard_map/solve/pallas_call | solution.py:213
  75.6 1.7 %reshape.37 = bf16[128,2,128]{2,1,0:T(2,128)(2,1)} reshape(bf16[512,64]{1,0:T(8,128)(2,1)} %get-tuple-element.5) | data formatting | bytes 131072 | tf_op jit(solution)/shard_map/reshape | solution.py:221
  77.2 4.4 %all-to-all-start.2 = ((bf16[128,2,128]{2,1,0:T(2,128)(2,1)}), bf16[128,2,128]{2,1,0:T(2,128)(2,1)S(1)}, u32[]{:S(2)}, u32[]{:S(2)}) async-start(bf16[128,2,128]{2,1,0:T(2,128)(2,1)} %reshape.37), calls=%async_computation.2 | async-start | bytes 131072 | tf_op jit(solution)/shard_map/all_to_all | solution.py:220
  81.6 0.0 copy-done.1
  81.7 0.1 iota_compare_fusion
  81.7 0.1 lt.20
  81.9 9.5 %all-to-all-done.2 = bf16[128,2,128]{2,1,0:T(2,128)(2,1)S(1)} async-done(((bf16[128,2,128]{2,1,0:T(2,128)(2,1)}), bf16[128,2,128]{2,1,0:T(2,128)(2,1)S(1)}, u32[]{:S(2)}, u32[]{:S(2)}) %all-to-all-start.2) | async-done | bytes 65568 | tf_op jit(solution)/shard_map/all_to_all | solution.py:220
  91.3 0.1 reshape.38
  91.5 0.1 select_bitcast_fusion
  91.6 0.7 copy.9
Async XLA Ops:
  3.1 33.0 %all-to-all-start = ((bf16[128,40,128]{2,1,0:T(8,128)(2,1)}), bf16[128,40,128]{2,1,0:T(8,128)(2,1)S(1)}, u32[]{:S(2)}, u32[]{:S(2)}) async-start(bf16[128,40,128]{2,1,0:T(8,128)(2,1)} %send.1), calls=%async_computation | async-start | bytes 2621440 | tf_op jit(solution)/shard_map/all_to_all | solution.py:188
  36.1 1.1 %copy-start = (bf16[128,40,128]{2,1,0:T(8,128)(2,1)}, bf16[128,40,128]{2,1,0:T(8,128)(2,1)S(1)}, u32[]{:S(2)}) copy-start(bf16[128,40,128]{2,1,0:T(8,128)(2,1)S(1)} %all-to-all-done.got_ref) | copy-start | bytes 3932164
  57.2 24.4 %copy-start.1 = (s32[1,128]{1,0:T(1,128)S(1)}, s32[1,128]{1,0:T(1,128)}, u32[]{:S(2)}) copy-start(s32[1,128]{1,0:T(1,128)} %cnt_ref.1) | copy-start | bytes 1540
  77.2 14.1 %all-to-all-start.2 = ((bf16[128,2,128]{2,1,0:T(2,128)(2,1)}), bf16[128,2,128]{2,1,0:T(2,128)(2,1)S(1)}, u32[]{:S(2)}, u32[]{:S(2)}) async-start(bf16[128,2,128]{2,1,0:T(2,128)(2,1)} %reshape.37), calls=%async_computation.2 | async-start | bytes 131072 | tf_op jit(solution)/shard_map/all_to_all | solution.py:220

commit v2 on v1

v2 whole, which is shorter than its diff:
```python
import functools
import jax
import jax.numpy as jnp
from jax import lax
from jax.experimental import pallas as pl
from jax.experimental.pallas import tpu as pltpu
from jax.sharding import PartitionSpec as P

LEV = 32
CAP = 4
CY = 16
CX = 256
LAYERS = 64
NY = 128
N_GX = 16
N_GY = 8
DEV = 128
SLOTS = DEV * CAP
SHARE = LAYERS // N_GY
ROWS = 40
BF = jnp.bfloat16
F32 = jnp.float32
I32 = jnp.int32


def iota(shape, dim):
    return lax.broadcasted_iota(I32, shape, dim)


def one_hot(cond):
    return jnp.where(cond, 1.0, 0.0).astype(BF)


def dot(a, b, dims=((1,), (0,))):
    return lax.dot_general(a, b, (dims, ((), ())), preferred_element_type=F32)


def send_kernel(inn_ref, col_ref, cnt_ref, mask_ref, out_ref):
    counts = jnp.broadcast_to(cnt_ref[...], (8, DEV)).astype(F32).astype(BF)
    spread = one_hot(iota((DEV, SLOTS), 1) // CAP == iota((DEV, SLOTS), 0))
    count_lane = dot(counts, spread)[0:1, :]
    slot_lane = (iota((1, SLOTS), 1) % CAP).astype(F32)
    live = slot_lane < count_lane
    values = jnp.where(live, inn_ref[0].astype(F32), 0.0).astype(BF)
    cells = col_ref[...]
    row = cells // CX
    col = cells % CX
    pick_col = one_hot(iota((CX, SLOTS), 0) == col)
    sea_rows = dot(mask_ref[...].astype(F32).astype(BF), pick_col)
    sea = jnp.sum(jnp.where(iota((CY, SLOTS), 0) == row, sea_rows, 0.0), axis=0, keepdims=True)
    row_code = jnp.where(sea > 0.5, row.astype(F32), 255.0)
    codes = jnp.where(
        iota((8, SLOTS), 0) == 0,
        jnp.broadcast_to(row_code, (8, SLOTS)),
        jnp.broadcast_to(col.astype(F32), (8, SLOTS)),
    ).astype(BF)
    source = iota((SLOTS, SLOTS), 0)
    target = iota((SLOTS, SLOTS), 1)
    permute = one_hot((source % CAP) * DEV + source // CAP == target)
    moved = dot(codes, permute)
    tile = jnp.concatenate(
        [moved[0:1, c * DEV : (c + 1) * DEV] for c in range(CAP)]
        + [moved[1:2, c * DEV : (c + 1) * DEV] for c in range(CAP)],
        axis=0,
    ).astype(BF)
    for b in range(N_GY):
        block = values[b * SHARE : (b + 1) * SHARE, :]
        message = jnp.concatenate(
            [block[:, q * DEV : (q + 1) * DEV] for q in range(CAP)] + [tile], axis=0
        )
        for a in range(N_GX):
            out_ref[a * N_GY + b] = message


def smooth_kernel(
    tracer_ref, got_ref, kx_ref, ky_ref, *refs
):
    out_refs = refs[:N_GY]
    wide_ref, turned_ref, dense_ref, acc_ref, along_ref, kx_vmem, sem = refs[N_GY:]
    fetch = pltpu.make_async_copy(kx_ref.at[tracer_ref[0]], kx_vmem, sem)
    fetch.start()
    acc_ref[...] = jnp.zeros_like(acc_ref)

    def widen(s, carry):
        wide_ref[pl.ds(pl.multiple_of(s * 32, 32), 32), :] = got_ref[s, 0:32, :].astype(F32)
        return carry

    lax.fori_loop(0, DEV, widen, 0, unroll=8)
    for q in range(CAP):
        for l in range(SHARE):
            block = wide_ref[pl.ds(q * SHARE + l, DEV, stride=32), :]
            turned_ref[pl.ds(q * DEV * SHARE + l, DEV, stride=SHARE), :] = block.T
    fetch.wait()

    col_iota = iota((CX, DEV), 0).astype(F32).astype(BF)
    half_iota = (iota((2 * SHARE, DEV), 0) // SHARE).astype(F32).astype(BF)
    zero = jnp.zeros((), BF)
    one = jnp.ones((), BF)

    def column_block(step, carry):
        for b in range(N_GY):
            owner = step * N_GY + b
            codes = got_ref[owner, 32:40, :].astype(F32)
            left = [[] for _ in range(N_GY)]
            right = []
            for c in range(CAP):
                base = pl.multiple_of(owner * (CAP * SHARE) + c * SHARE, SHARE)
                v = turned_ref[pl.ds(base, SHARE), :]
                twice = jnp.concatenate([v, v], axis=0).astype(BF)
                row = jnp.broadcast_to(codes[c : c + 1, :], (2 * SHARE, DEV)).astype(BF)
                pair = row - half_iota
                for k in range(CY // 2):
                    left[k].append(jnp.where(pair == jnp.asarray(2 * k, BF), twice, zero))
                col = jnp.broadcast_to(codes[CAP + c : CAP + c + 1, :], (CX, DEV)).astype(BF)
                right.append(jnp.where(col == col_iota, one, zero))
            lhs = jnp.concatenate([jnp.concatenate(x, axis=1) for x in left], axis=0)
            rhs = jnp.concatenate(right, axis=1)
            dense = dot(lhs, rhs, ((1,), (1,)))
            dense_ref[b * 128 : (b + 1) * 128, :] = dense.astype(BF)
        gain = dot(dense_ref[...], kx_vmem[pl.ds(pl.multiple_of(step * CX, CX), CX), :])
        for h in range(2):
            acc_ref[h * 1024 : (h + 1) * 1024, :] += gain[:, h * 128 : (h + 1) * 128]
        return carry

    lax.fori_loop(0, N_GX, column_block, 0)
    for l in range(SHARE):
        along_x = jnp.concatenate(
            [acc_ref[pl.ds(h * 1024 + l, NY, stride=SHARE), :] for h in range(2)], axis=1
        ).astype(BF)
        along_y = dot(ky_ref[tracer_ref[0]], along_x, ((0,), (0,))).astype(BF)
        along_ref[l] = along_y
    mine = tracer_ref[1]
    for k in range(N_GY):
        row = pl.multiple_of((mine ^ k) * CY, CY)
        out_refs[k][...] = along_ref[:, pl.ds(row, CY), :]


def smooth_call(tracer, got, inverse_x, inverse_y):
    vmem = pl.BlockSpec(memory_space=pltpu.VMEM)
    return pl.pallas_call(
        smooth_kernel,
        out_shape=[pltpu.VMEM((SHARE, CY, CX), BF)] * N_GY,
        in_specs=[
            pl.BlockSpec(memory_space=pltpu.SMEM),
            vmem,
            pl.BlockSpec(memory_space=pl.ANY),
            vmem,
        ],
        out_specs=[vmem] * N_GY,
        scratch_shapes=[
            pltpu.VMEM((DEV * 32, DEV), F32),
            pltpu.VMEM((SLOTS * SHARE, DEV), F32),
            pltpu.VMEM((NY * SHARE, CX), BF),
            pltpu.VMEM((2 * NY * SHARE, 128), F32),
            pltpu.VMEM((SHARE, NY, CX), BF),
            pltpu.VMEM((N_GX * CX, CX), BF),
            pltpu.SemaphoreType.DMA(()),
        ],
        name="smooth",
    )(tracer, got, inverse_x, inverse_y)


def coef_kernel(coef_ref, inv_ref, gain_ref, ratio_ref):
    ratio = None
    for k in range(LEV):
        here = coef_ref[k]
        below = coef_ref[k + 1] if k + 1 < LEV else jnp.zeros_like(here)
        diagonal = 1.0 + here + below
        if k > 0:
            diagonal = diagonal + here * ratio
        inv = 1.0 / diagonal
        ratio = -below * inv
        inv_ref[k] = inv
        gain_ref[k] = here * inv
        ratio_ref[k] = ratio


def solve_kernel(where_ref, *refs):
    parts = refs[:N_GY]
    inv_ref, gain_ref, ratio_ref, mask_ref, col_ref, inc_ref, pick_ref, field_ref, part_ref = refs[N_GY:]
    mine = where_ref[1]
    for k in range(N_GY):
        field_ref[pl.ds((mine ^ k) * SHARE, SHARE)] = parts[k][...]
    mask = mask_ref[...].astype(F32)
    prev0 = prev1 = None
    for k in range(LEV):
        f0 = field_ref[k].astype(F32) * inv_ref[k]
        f1 = field_ref[LEV + k].astype(F32) * inv_ref[k]
        if k == 0:
            prev0, prev1 = f0, f1
        else:
            prev0 = f0 + gain_ref[k] * prev0
            prev1 = f1 + gain_ref[k] * prev1
        part_ref[k] = prev0
        part_ref[LEV + k] = prev1
    x0, x1 = prev0, prev1
    for k in range(LEV - 1, -1, -1):
        if k < LEV - 1:
            x0 = part_ref[k] - ratio_ref[k] * x0
            x1 = part_ref[LEV + k] - ratio_ref[k] * x1
        inc_ref[k] = (x0 * mask).astype(BF)
        inc_ref[LEV + k] = (x1 * mask).astype(BF)
    cells = col_ref[...]
    row = cells // CX
    col = cells % CX
    packed = jnp.concatenate([row.astype(F32), col.astype(F32)] + [jnp.zeros((6, SLOTS), F32)], axis=0).astype(BF)
    source = iota((SLOTS, SLOTS), 0)
    target = iota((SLOTS, SLOTS), 1)
    moved = dot(packed, one_hot((source % CAP) * DEV + source // CAP == target))
    row = moved[0:1, :].astype(I32)
    col = moved[1:2, :].astype(I32)
    pick_col = one_hot(iota((CX, SLOTS), 0) == col)
    row_iota = iota((LAYERS * CY, SLOTS), 0) % CY
    found = dot(inc_ref[...].reshape(LAYERS * CY, CX), pick_col)
    chosen = jnp.where(row_iota == row, found, 0.0).astype(BF)
    total = one_hot(iota((LAYERS, LAYERS * CY), 1) // CY == iota((LAYERS, LAYERS * CY), 0))
    picked = dot(chosen, total, ((0,), (1,))).astype(BF)
    for r in range(2):
        pair = [picked[(2 * r + h) * DEV : (2 * r + h + 1) * DEV, :] for h in range(2)]
        pick_ref[:, r, :] = jnp.concatenate(pair, axis=1)


def in_vmem(x):
    return pltpu.with_memory_space_constraint(x, pltpu.VMEM)


def call(kernel, out_shape, n_in, name, scratch=()):
    return pl.pallas_call(
        kernel,
        out_shape=out_shape,
        in_specs=[pl.BlockSpec(memory_space=pltpu.VMEM)] * n_in,
        out_specs=jax.tree.map(lambda _: pl.BlockSpec(memory_space=pltpu.VMEM), out_shape),
        scratch_shapes=list(scratch),
        name=name,
    )


def body(innovations, station_columns, profile_counts, land_mask, vertical_coef, inverse_x, inverse_y):
    everyone = ("gx", "gy")
    message = call(send_kernel, pltpu.VMEM((DEV, ROWS, DEV), BF), 4, "send")(
        innovations, station_columns, profile_counts, land_mask
    )
    got = lax.all_to_all(message, everyone, split_axis=0, concat_axis=0, tiled=True)
    mine = lax.axis_index("gy").astype(I32)
    where = jnp.stack([mine * SHARE // LEV, mine])
    products = smooth_call(where, in_vmem(got), inverse_x, inverse_y)
    parts = [products[0]] + [
        lax.ppermute(products[k], "gy", [(i, i ^ k) for i in range(N_GY)]) for k in range(1, N_GY)
    ]
    plane = pltpu.VMEM((LEV, CY, CX), F32)
    inv, gain, ratio = call(coef_kernel, (plane, plane, plane), 1, "coef")(vertical_coef)
    vmem = pl.BlockSpec(memory_space=pltpu.VMEM)
    increment, picked = pl.pallas_call(
        solve_kernel,
        out_shape=(jax.ShapeDtypeStruct((LAYERS, CY, CX), BF), pltpu.VMEM((DEV, 2, DEV), BF)),
        in_specs=[pl.BlockSpec(memory_space=pltpu.SMEM)] + [vmem] * (N_GY + 5),
        out_specs=(vmem, vmem),
        scratch_shapes=[pltpu.VMEM((LAYERS, CY, CX), BF), pltpu.VMEM((LAYERS, CY, CX), F32)],
        name="solve",
    )(where, *[in_vmem(p) for p in parts], in_vmem(inv), in_vmem(gain), in_vmem(ratio), land_mask, station_columns)
    returned = lax.all_to_all(picked, everyone, split_axis=0, concat_axis=0, tiled=True)
    returned = returned.reshape(SLOTS, LAYERS).T.reshape(1, LAYERS, SLOTS)
    slot_index = lax.broadcasted_iota(I32, (DEV, CAP), 1)
    live = (slot_index < profile_counts[0][:, None]).reshape(SLOTS)
    equivalents = jnp.where(live[None, None, :], returned, jnp.zeros((), BF))
    return increment, equivalents


def solution(mesh):
    in_specs = (
        P(("gx", "gy"), None, None),
        P(("gx", "gy"), None),
        P(("gx", "gy"), None),
        P("gy", "gx"),
        P(None, "gy", "gx"),
        P(None, None, "gx"),
        P(),
    )
    out_specs = (P(None, "gy", "gx"), P(("gx", "gy"), None, None))
    return jax.shard_map(body, mesh=mesh, in_specs=in_specs, out_specs=out_specs, check_vma=False)
```

time: 92.8 us -> 85.6 us (0.922)
  blocking collectives: 15 us -> 0 us
  starting transfers between devices: 15.9 us -> 25.2 us
  local copies, waits for them, and re-layouts: 3.68 us -> 0.95 us
  waiting for transfers between devices: 31 us -> 32.4 us
    all_to_all x1 -> x0, blocking collectives: 15 us -> none  [body(): lax.all_to_all(product, 'gy', split_axis=0, concat_axis=0, tiled=True)]
    ppermute x0 -> x7, starting transfers between devices: none -> 9.41 us  [body(): lax.ppermute(products[k], 'gy', [(i, i ^ k) for i in range(N_GY)])]
    ppermute x0 -> x7, waiting for transfers between devices: none -> 2.14 us  [body(): lax.ppermute(products[k], 'gy', [(i, i ^ k) for i in range(N_GY)])]
    reshape x1 -> x0, local copies, waits for them, and re-layouts: 1.66 us -> none  [body(): picked.reshape(DEV, 2, 128)]
    unnamed x5 -> x3, local copies, waits for them, and re-layouts: 1.81 us -> 0.73 us
    pallas_call x3 -> x4, Pallas kernels: 25.8 us -> 25.1 us  [the longest x1 18.5 us: smooth_call(): pl.pallas_call(smooth_kernel, out_shape=[pltpu.VMEM((SHARE, CY, CX), BF)]...]
  transfers between devices with their start and end apart: 2 -> 9, of which waited for: 2 -> 4; matrix products, arithmetic and copies ran while one was open for 0% -> 1% of each run, Pallas kernels for 0% -> 2%
where the time goes in v2:
time: 85.6 us; the launch traced here: 85.2 us
  waiting for transfers between devices  32.4 us (38%)
  starting transfers between devices  25.2 us (29%)
  Pallas kernels  25.1 us (29%)
  local copies, waits for them, and re-layouts  0.95 us (1%)
    all_to_all x1, waiting for transfers between devices, body(): lax.all_to_all(message, everyone, split_axis=0, concat_axis=0, tiled=True)  21 us
    pallas_call x1, Pallas kernels, smooth_call(): pl.pallas_call(smooth_kernel, out_shape=[pltpu.VMEM((SHARE, CY, CX), BF)]...  18.5 us
    all_to_all x1, starting transfers between devices, body(): lax.all_to_all(message, everyone, split_axis=0, concat_axis=0, tiled=True)  11.5 us
    ppermute x7, starting transfers between devices, body(): lax.ppermute(products[k], 'gy', [(i, i ^ k) for i in range(N_GY)])  9.41 us
    all_to_all x1, waiting for transfers between devices, body(): lax.all_to_all(picked, everyone, split_axis=0, concat_axis=0, tiled=True)  9.34 us
    all_to_all x1, starting transfers between devices, body(): lax.all_to_all(picked, everyone, split_axis=0, concat_axis=0, tiled=True)  4.28 us
    pallas_call x1, Pallas kernels, body(): pl.pallas_call(solve_kernel, out_shape=(jax.ShapeDtypeStruct((LAYERS, CY,...  2.86 us
    pallas_call x1, Pallas kernels, body(): call(send_kernel, pltpu.VMEM((DEV, ROWS, DEV), BF), 4, 'send')  2.45 us
  transfers between devices with their start and end apart: 9, of which 4 were waited for; matrix products, arithmetic and copies ran while one was open for 1% of the time, Pallas kernels for 2%

profile of v2, /device:TPU:1, one launch (start us, length us, event | category | flops | bytes accessed | tf_op | source)
XLA Modules:
  0.0 85.2 jit_solution(11538585008084976843)
XLA Ops:
  0.6 2.5 %send.1 = bf16[128,40,128]{2,1,0:T(8,128)(2,1)} custom-call(bf16[1,64,512]{2,1,0:T(8,128)(2,1)} %inn_ref.1, s32[1,512]{1,0:T(1,128)} %refs_12_.1, s32[1,128]{1,0:T(1,128)} %cnt_ref.1, s32[16,256]{1,0:T(8,128)} %refs_11_.1), custom_call_target="tpu_custom_call" | custom-call | tf_op jit(solution)/shard_map/send/pallas_call | solution.py:240
  3.1 11.5 %all-to-all-start = ((bf16[128,40,128]{2,1,0:T(8,128)(2,1)}), bf16[128,40,128]{2,1,0:T(8,128)(2,1)S(1)}, u32[]{:S(2)}, u32[]{:S(2)}) async-start(bf16[128,40,128]{2,1,0:T(8,128)(2,1)} %send.1), calls=%async_computation | async-start | bytes 2621440 | tf_op jit(solution)/shard_map/all_to_all | solution.py:243
  14.6 0.6 pad_add_fusion.tracer_ref.where_ref
  15.2 21.0 %all-to-all-done.got_ref = bf16[128,40,128]{2,1,0:T(8,128)(2,1)S(1)} async-done(((bf16[128,40,128]{2,1,0:T(8,128)(2,1)}), bf16[128,40,128]{2,1,0:T(8,128)(2,1)S(1)}, u32[]{:S(2)}, u32[]{:S(2)}) %all-to-all-start) | async-done | bytes 1310752 | tf_op jit(solution)/shard_map/all_to_all | solution.py:243
  36.1 18.5 %smooth.1 = (bf16[8,16,256]{2,1,0:T(8,128)(2,1)S(1)}, bf16[8,16,256]{2,1,0:T(8,128)(2,1)S(1)}, bf16[8,16,256]{2,1,0:T(8,128)(2,1)S(1)}, bf16[8,16,256]{2,1,0:T(8...) custom-call(s32[2]{0:T(128)} %pad_add_fusion.tracer_ref.where_ref, ...), custom_call_target="tpu_custom_call" | custom-call | tf_op jit(solution)/shard_map/smooth/pallas_call | solution.py:140
  54.6 1.5 %collective-permute-start = (bf16[8,16,256]{2,1,0:T(8,128)(2,1)S(1)}, bf16[8,16,256]{2,1,0:T(8,128)(2,1)S(1)}, u32[]{:S(2)}, u32[]{:S(2)}) collective-permute-start(bf16[8,16,256]{2,1,0:T(8,128)(2,1)S(1)} %get-tuple-element.16), channel_id=1, source_target_pairs={{0,1},{1,0},{2,3},{3,2},{4,5},{5,4},{6,7},{7,6},{8,9},{9,8},{10,11... | collective-permute-start | bytes 196616 | tf_op jit(solution)/shard_map/ppermute | solution.py:248
  56.1 0.1 collective-permute-start.1
  56.2 1.6 %collective-permute-start.2 = (bf16[8,16,256]{2,1,0:T(8,128)(2,1)S(1)}, bf16[8,16,256]{2,1,0:T(8,128)(2,1)S(1)}, u32[]{:S(2)}, u32[]{:S(2)}) collective-permute-start(bf16[8,16,256]{2,1,0:T(8,128)(2,1)S(1)} %get-tuple-element.18), channel_id=1, source_target_pairs={{0,3},{1,2},{2,1},{3,0},{4,7},{5,6},{6,5},{7,4},{8,11},{9,10},{10,... | collective-permute-start | bytes 196616 | tf_op jit(solution)/shard_map/ppermute | solution.py:248
  57.8 0.1 collective-permute-start.3
  57.9 3.2 %collective-permute-start.4 = (bf16[8,16,256]{2,1,0:T(8,128)(2,1)S(1)}, bf16[8,16,256]{2,1,0:T(8,128)(2,1)S(1)}, u32[]{:S(2)}, u32[]{:S(2)}) collective-permute-start(bf16[8,16,256]{2,1,0:T(8,128)(2,1)S(1)} %get-tuple-element.20), channel_id=1, source_target_pairs={{0,5},{1,4},{2,7},{3,6},{4,1},{5,0},{6,3},{7,2},{8,13},{9,12},{10,... | collective-permute-start | bytes 196616 | tf_op jit(solution)/shard_map/ppermute | solution.py:248
  61.1 0.0 collective-permute-done.refs_1_
  61.1 0.0 collective-permute-start.5
  61.1 0.0 collective-permute-done.1.refs_2_
  61.1 0.0 copy-start
  61.1 2.9 %collective-permute-start.6 = (bf16[8,16,256]{2,1,0:T(8,128)(2,1)S(1)}, bf16[8,16,256]{2,1,0:T(8,128)(2,1)S(1)}, u32[]{:S(2)}, u32[]{:S(2)}) collective-permute-start(bf16[8,16,256]{2,1,0:T(8,128)(2,1)S(1)} %get-tuple-element.22), channel_id=1, source_target_pairs={{0,7},{1,6},{2,5},{3,4},{4,3},{5,2},{6,1},{7,0},{8,15},{9,14},{10,... | collective-permute-start | bytes 196616 | tf_op jit(solution)/shard_map/ppermute | solution.py:248
  64.0 1.3 %coef.1 = (f32[32,16,256]{2,1,0:T(8,128)S(1)}, f32[32,16,256]{2,1,0:T(8,128)S(1)}, f32[32,16,256]{2,1,0:T(8,128)S(1)}) custom-call(f32[32,16,256]{2,1,0:T(8,128)} %coef_ref.1), custom_call_target="tpu_custom_call" | custom-call | tf_op jit(solution)/shard_map/coef/pallas_call | solution.py:251
  65.4 0.0 collective-permute-done.2.refs_3_
  65.4 0.0 collective-permute-done.3.refs_4_
  65.4 0.0 collective-permute-done.4.refs_5_
  65.4 0.5 collective-permute-done.5.refs_6_
  65.9 1.7 %collective-permute-done.6.refs_7_ = bf16[8,16,256]{2,1,0:T(8,128)(2,1)S(1)} collective-permute-done((bf16[8,16,256]{2,1,0:T(8,128)(2,1)S(1)}, bf16[8,16,256]{2,1,0:T(8,128)(2,1)S(1)}, u32[]{:S(2)}, u32[]{:S(2)}) %collective-permute-start.6) | collective-permute-done | bytes 65568 | tf_op jit(solution)/shard_map/ppermute | solution.py:248
  67.5 2.9 %solve.1 = (bf16[64,16,256]{2,1,0:T(8,128)(2,1)}, bf16[128,2,128]{2,1,0:T(2,128)(2,1)}) custom-call(s32[2]{0:T(128)} %pad_add_fusion.tracer_ref.where_ref, bf16[8,16,256]{2,1,0:T(8,128)(2,1)S(1)} %get-tuple-element.15.refs_0_, bf16[8,16,256]{2,1,0:T(8,128)(2,1)S(1)} %collective-permute-done.refs_1_, bf16[8,16,256]{2,1,0:T(8,128)(2,1)S(1)} %collective-permute-done.1.refs_2_, ...), custom_call_target="tpu_custom_call" | custom-call | tf_op jit(solution)/shard_map/solve/pallas_call | solution.py:253
  70.4 4.3 %all-to-all-start.1 = ((bf16[128,2,128]{2,1,0:T(2,128)(2,1)}), bf16[128,2,128]{2,1,0:T(2,128)(2,1)S(1)}, u32[]{:S(2)}, u32[]{:S(2)}) async-start(bf16[128,2,128]{2,1,0:T(2,128)(2,1)} %get-tuple-element.27), calls=%async_computation.1 | async-start | bytes 131072 | tf_op jit(solution)/shard_map/all_to_all | solution.py:261
  74.7 0.0 copy-done
  74.7 0.1 iota_compare_fusion
  74.8 0.1 lt.20
  74.9 9.3 %all-to-all-done.1 = bf16[128,2,128]{2,1,0:T(2,128)(2,1)S(1)} async-done(((bf16[128,2,128]{2,1,0:T(2,128)(2,1)}), bf16[128,2,128]{2,1,0:T(2,128)(2,1)S(1)}, u32[]{:S(2)}, u32[]{:S(2)}) %all-to-all-start.1) | async-done | bytes 65568 | tf_op jit(solution)/shard_map/all_to_all | solution.py:261
  84.2 0.1 reshape.26
  84.3 0.1 select_bitcast_fusion
  84.5 0.7 copy.10
Async XLA Ops:
  3.1 33.0 %all-to-all-start = ((bf16[128,40,128]{2,1,0:T(8,128)(2,1)}), bf16[128,40,128]{2,1,0:T(8,128)(2,1)S(1)}, u32[]{:S(2)}, u32[]{:S(2)}) async-start(bf16[128,40,128]{2,1,0:T(8,128)(2,1)} %send.1), calls=%async_computation | async-start | bytes 2621440 | tf_op jit(solution)/shard_map/all_to_all | solution.py:243
  54.6 6.5 %collective-permute-start = (bf16[8,16,256]{2,1,0:T(8,128)(2,1)S(1)}, bf16[8,16,256]{2,1,0:T(8,128)(2,1)S(1)}, u32[]{:S(2)}, u32[]{:S(2)}) collective-permute-start(bf16[8,16,256]{2,1,0:T(8,128)(2,1)S(1)} %get-tuple-element.16), channel_id=1, source_target_pairs={{0,1},{1,0},{2,3},{3,2},{4,5},{5,4},{6,7},{7,6},{8,9},{9,8},{10,11... | collective-permute-start | bytes 196616 | tf_op jit(solution)/shard_map/ppermute | solution.py:248
  56.1 5.0 %collective-permute-start.1 = (bf16[8,16,256]{2,1,0:T(8,128)(2,1)S(1)}, bf16[8,16,256]{2,1,0:T(8,128)(2,1)S(1)}, u32[]{:S(2)}, u32[]{:S(2)}) collective-permute-start(bf16[8,16,256]{2,1,0:T(8,128)(2,1)S(1)} %get-tuple-element.17), channel_id=1, source_target_pairs={{0,2},{1,3},{2,0},{3,1},{4,6},{5,7},{6,4},{7,5},{8,10},{9,11},{10,... | collective-permute-start | bytes 196616 | tf_op jit(solution)/shard_map/ppermute | solution.py:248
  56.2 9.2 %collective-permute-start.2 = (bf16[8,16,256]{2,1,0:T(8,128)(2,1)S(1)}, bf16[8,16,256]{2,1,0:T(8,128)(2,1)S(1)}, u32[]{:S(2)}, u32[]{:S(2)}) collective-permute-start(bf16[8,16,256]{2,1,0:T(8,128)(2,1)S(1)} %get-tuple-element.18), channel_id=1, source_target_pairs={{0,3},{1,2},{2,1},{3,0},{4,7},{5,6},{6,5},{7,4},{8,11},{9,10},{10,... | collective-permute-start | bytes 196616 | tf_op jit(solution)/shard_map/ppermute | solution.py:248
  57.8 7.6 %collective-permute-start.3 = (bf16[8,16,256]{2,1,0:T(8,128)(2,1)S(1)}, bf16[8,16,256]{2,1,0:T(8,128)(2,1)S(1)}, u32[]{:S(2)}, u32[]{:S(2)}) collective-permute-start(bf16[8,16,256]{2,1,0:T(8,128)(2,1)S(1)} %get-tuple-element.19), channel_id=1, source_target_pairs={{0,4},{1,5},{2,6},{3,7},{4,0},{5,1},{6,2},{7,3},{8,12},{9,13},{10,... | collective-permute-start | bytes 196616 | tf_op jit(solution)/shard_map/ppermute | solution.py:248
  57.9 7.5 %collective-permute-start.4 = (bf16[8,16,256]{2,1,0:T(8,128)(2,1)S(1)}, bf16[8,16,256]{2,1,0:T(8,128)(2,1)S(1)}, u32[]{:S(2)}, u32[]{:S(2)}) collective-permute-start(bf16[8,16,256]{2,1,0:T(8,128)(2,1)S(1)} %get-tuple-element.20), channel_id=1, source_target_pairs={{0,5},{1,4},{2,7},{3,6},{4,1},{5,0},{6,3},{7,2},{8,13},{9,12},{10,... | collective-permute-start | bytes 196616 | tf_op jit(solution)/shard_map/ppermute | solution.py:248
  61.1 4.8 %collective-permute-start.5 = (bf16[8,16,256]{2,1,0:T(8,128)(2,1)S(1)}, bf16[8,16,256]{2,1,0:T(8,128)(2,1)S(1)}, u32[]{:S(2)}, u32[]{:S(2)}) collective-permute-start(bf16[8,16,256]{2,1,0:T(8,128)(2,1)S(1)} %get-tuple-element.21), channel_id=1, source_target_pairs={{0,6},{1,7},{2,4},{3,5},{4,2},{5,3},{6,0},{7,1},{8,14},{9,15},{10,... | collective-permute-start | bytes 196616 | tf_op jit(solution)/shard_map/ppermute | solution.py:248
  61.1 13.6 %copy-start = (s32[1,128]{1,0:T(1,128)S(1)}, s32[1,128]{1,0:T(1,128)}, u32[]{:S(2)}) copy-start(s32[1,128]{1,0:T(1,128)} %cnt_ref.1) | copy-start | bytes 1540
  61.1 6.4 %collective-permute-start.6 = (bf16[8,16,256]{2,1,0:T(8,128)(2,1)S(1)}, bf16[8,16,256]{2,1,0:T(8,128)(2,1)S(1)}, u32[]{:S(2)}, u32[]{:S(2)}) collective-permute-start(bf16[8,16,256]{2,1,0:T(8,128)(2,1)S(1)} %get-tuple-element.22), channel_id=1, source_target_pairs={{0,7},{1,6},{2,5},{3,4},{4,3},{5,2},{6,1},{7,0},{8,15},{9,14},{10,... | collective-permute-start | bytes 196616 | tf_op jit(solution)/shard_map/ppermute | solution.py:248
  70.4 13.8 %all-to-all-start.1 = ((bf16[128,2,128]{2,1,0:T(2,128)(2,1)}), bf16[128,2,128]{2,1,0:T(2,128)(2,1)S(1)}, u32[]{:S(2)}, u32[]{:S(2)}) async-start(bf16[128,2,128]{2,1,0:T(2,128)(2,1)} %get-tuple-element.27), calls=%async_computation.1 | async-start | bytes 131072 | tf_op jit(solution)/shard_map/all_to_all | solution.py:261

commit v3 on v2

--- a/solution.py
+++ b/solution.py
@@ -76,23 +76,25 @@
     tracer_ref, got_ref, kx_ref, ky_ref, *refs
 ):
     out_refs = refs[:N_GY]
-    wide_ref, turned_ref, dense_ref, acc_ref, along_ref, kx_vmem, sem = refs[N_GY:]
+    wide_ref, turned_ref, column_ref, dense_ref, acc_ref, along_ref, kx_vmem, sem = refs[N_GY:]
     fetch = pltpu.make_async_copy(kx_ref.at[tracer_ref[0]], kx_vmem, sem)
     fetch.start()
     acc_ref[...] = jnp.zeros_like(acc_ref)
 
     def widen(s, carry):
-        wide_ref[pl.ds(pl.multiple_of(s * 32, 32), 32), :] = got_ref[s, 0:32, :].astype(F32)
+        wide_ref[pl.ds(pl.multiple_of(s * ROWS, 8), ROWS), :] = got_ref[s].astype(F32)
         return carry
 
     lax.fori_loop(0, DEV, widen, 0, unroll=8)
     for q in range(CAP):
         for l in range(SHARE):
-            block = wide_ref[pl.ds(q * SHARE + l, DEV, stride=32), :]
+            block = wide_ref[pl.ds(q * SHARE + l, DEV, stride=ROWS), :]
             turned_ref[pl.ds(q * DEV * SHARE + l, DEV, stride=SHARE), :] = block.T
+    for c in range(CAP):
+        column_ref[c] = wide_ref[pl.ds(36 + c, DEV, stride=ROWS), :].T
     fetch.wait()
 
-    col_iota = iota((CX, DEV), 0).astype(F32).astype(BF)
+    col_iota = [(iota((DEV, DEV), 1) + h * DEV).astype(F32).astype(BF) for h in range(2)]
     half_iota = (iota((2 * SHARE, DEV), 0) // SHARE).astype(F32).astype(BF)
     zero = jnp.zeros((), BF)
     one = jnp.ones((), BF)
@@ -111,18 +113,18 @@
                 pair = row - half_iota
                 for k in range(CY // 2):
                     left[k].append(jnp.where(pair == jnp.asarray(2 * k, BF), twice, zero))
-                col = jnp.broadcast_to(codes[CAP + c : CAP + c + 1, :], (CX, DEV)).astype(BF)
-                right.append(jnp.where(col == col_iota, one, zero))
+                col = jnp.take_along_axis(column_ref[c], jnp.full((DEV, DEV), owner, I32), axis=1).astype(BF)
+                right.append(jnp.concatenate([jnp.where(col == x, one, zero) for x in col_iota], axis=1))
             lhs = jnp.concatenate([jnp.concatenate(x, axis=1) for x in left], axis=0)
-            rhs = jnp.concatenate(right, axis=1)
-            dense = dot(lhs, rhs, ((1,), (1,)))
+            rhs = jnp.concatenate(right, axis=0)
+            dense = dot(lhs, rhs)
             dense_ref[b * 128 : (b + 1) * 128, :] = dense.astype(BF)
         gain = dot(dense_ref[...], kx_vmem[pl.ds(pl.multiple_of(step * CX, CX), CX), :])
         for h in range(2):
             acc_ref[h * 1024 : (h + 1) * 1024, :] += gain[:, h * 128 : (h + 1) * 128]
         return carry
 
-    lax.fori_loop(0, N_GX, column_block, 0)
+    lax.fori_loop(0, N_GX, column_block, 0, unroll=16)
     for l in range(SHARE):
         along_x = jnp.concatenate(
             [acc_ref[pl.ds(h * 1024 + l, NY, stride=SHARE), :] for h in range(2)], axis=1
@@ -148,8 +150,9 @@
         ],
         out_specs=[vmem] * N_GY,
         scratch_shapes=[
-            pltpu.VMEM((DEV * 32, DEV), F32),
+            pltpu.VMEM((DEV * ROWS, DEV), F32),
             pltpu.VMEM((SLOTS * SHARE, DEV), F32),
+            pltpu.VMEM((CAP, DEV, DEV), F32),
             pltpu.VMEM((NY * SHARE, CX), BF),
             pltpu.VMEM((2 * NY * SHARE, 128), F32),
             pltpu.VMEM((SHARE, NY, CX), BF),

time: 85.6 us -> 77.2 us (0.902)
  Pallas kernels: 25.1 us -> 16.7 us
    pallas_call x1, Pallas kernels: 18.5 us -> 10.1 us  [smooth_call(): pl.pallas_call(smooth_kernel, out_shape=[pltpu.VMEM((SHARE, CY, CX), BF)]...]
where the time goes in v3:
time: 77.2 us; the launch traced here: 76.8 us
  waiting for transfers between devices  32.4 us (42%)
  starting transfers between devices  25.2 us (33%)
  Pallas kernels  16.7 us (22%)
  local copies, waits for them, and re-layouts  0.95 us (1%)
  other arithmetic  0.8 us (1%)
    all_to_all x1, waiting for transfers between devices, body(): lax.all_to_all(message, everyone, split_axis=0, concat_axis=0, tiled=True)  21 us
    all_to_all x1, starting transfers between devices, body(): lax.all_to_all(message, everyone, split_axis=0, concat_axis=0, tiled=True)  11.5 us
    pallas_call x1, Pallas kernels, smooth_call(): pl.pallas_call(smooth_kernel, out_shape=[pltpu.VMEM((SHARE, CY, CX), BF)]...  10.1 us
    ppermute x7, starting transfers between devices, body(): lax.ppermute(products[k], 'gy', [(i, i ^ k) for i in range(N_GY)])  9.42 us
    all_to_all x1, waiting for transfers between devices, body(): lax.all_to_all(picked, everyone, split_axis=0, concat_axis=0, tiled=True)  9.34 us
    all_to_all x1, starting transfers between devices, body(): lax.all_to_all(picked, everyone, split_axis=0, concat_axis=0, tiled=True)  4.27 us
    pallas_call x1, Pallas kernels, body(): pl.pallas_call(solve_kernel, out_shape=(jax.ShapeDtypeStruct((LAYERS, CY,...  2.86 us
    pallas_call x1, Pallas kernels, body(): call(send_kernel, pltpu.VMEM((DEV, ROWS, DEV), BF), 4, 'send')  2.45 us
  transfers between devices with their start and end apart: 9, of which 4 were waited for; matrix products, arithmetic and copies ran while one was open for 1% of the time, Pallas kernels for 2%

profile of v3, /device:TPU:1, one launch (start us, length us, event | category | flops | bytes accessed | tf_op | source)
XLA Modules:
  0.0 76.8 jit_solution(4221881927303526286)
XLA Ops:
  0.6 2.5 %send.1 = bf16[128,40,128]{2,1,0:T(8,128)(2,1)} custom-call(bf16[1,64,512]{2,1,0:T(8,128)(2,1)} %inn_ref.1, s32[1,512]{1,0:T(1,128)} %refs_12_.1, s32[1,128]{1,0:T(1,128)} %cnt_ref.1, s32[16,256]{1,0:T(8,128)} %refs_11_.1), custom_call_target="tpu_custom_call" | custom-call | tf_op jit(solution)/shard_map/send/pallas_call | solution.py:243
  3.1 11.5 %all-to-all-start = ((bf16[128,40,128]{2,1,0:T(8,128)(2,1)}), bf16[128,40,128]{2,1,0:T(8,128)(2,1)S(1)}, u32[]{:S(2)}, u32[]{:S(2)}) async-start(bf16[128,40,128]{2,1,0:T(8,128)(2,1)} %send.1), calls=%async_computation | async-start | bytes 2621440 | tf_op jit(solution)/shard_map/all_to_all | solution.py:246
  14.6 0.6 pad_add_fusion.tracer_ref.where_ref
  15.2 21.0 %all-to-all-done.got_ref = bf16[128,40,128]{2,1,0:T(8,128)(2,1)S(1)} async-done(((bf16[128,40,128]{2,1,0:T(8,128)(2,1)}), bf16[128,40,128]{2,1,0:T(8,128)(2,1)S(1)}, u32[]{:S(2)}, u32[]{:S(2)}) %all-to-all-start) | async-done | bytes 1310752 | tf_op jit(solution)/shard_map/all_to_all | solution.py:246
  36.1 10.1 %smooth.1 = (bf16[8,16,256]{2,1,0:T(8,128)(2,1)S(1)}, bf16[8,16,256]{2,1,0:T(8,128)(2,1)S(1)}, bf16[8,16,256]{2,1,0:T(8,128)(2,1)S(1)}, bf16[8,16,256]{2,1,0:T(8...) custom-call(s32[2]{0:T(128)} %pad_add_fusion.tracer_ref.where_ref, ...), custom_call_target="tpu_custom_call" | custom-call | tf_op jit(solution)/shard_map/smooth/pallas_call | solution.py:142
  46.2 1.5 %collective-permute-start = (bf16[8,16,256]{2,1,0:T(8,128)(2,1)S(1)}, bf16[8,16,256]{2,1,0:T(8,128)(2,1)S(1)}, u32[]{:S(2)}, u32[]{:S(2)}) collective-permute-start(bf16[8,16,256]{2,1,0:T(8,128)(2,1)S(1)} %get-tuple-element.16), channel_id=1, source_target_pairs={{0,1},{1,0},{2,3},{3,2},{4,5},{5,4},{6,7},{7,6},{8,9},{9,8},{10,11... | collective-permute-start | bytes 196616 | tf_op jit(solution)/shard_map/ppermute | solution.py:251
  47.7 0.1 collective-permute-start.1
  47.8 1.6 %collective-permute-start.2 = (bf16[8,16,256]{2,1,0:T(8,128)(2,1)S(1)}, bf16[8,16,256]{2,1,0:T(8,128)(2,1)S(1)}, u32[]{:S(2)}, u32[]{:S(2)}) collective-permute-start(bf16[8,16,256]{2,1,0:T(8,128)(2,1)S(1)} %get-tuple-element.18), channel_id=1, source_target_pairs={{0,3},{1,2},{2,1},{3,0},{4,7},{5,6},{6,5},{7,4},{8,11},{9,10},{10,... | collective-permute-start | bytes 196616 | tf_op jit(solution)/shard_map/ppermute | solution.py:251
  49.4 0.1 collective-permute-start.3
  49.5 3.2 %collective-permute-start.4 = (bf16[8,16,256]{2,1,0:T(8,128)(2,1)S(1)}, bf16[8,16,256]{2,1,0:T(8,128)(2,1)S(1)}, u32[]{:S(2)}, u32[]{:S(2)}) collective-permute-start(bf16[8,16,256]{2,1,0:T(8,128)(2,1)S(1)} %get-tuple-element.20), channel_id=1, source_target_pairs={{0,5},{1,4},{2,7},{3,6},{4,1},{5,0},{6,3},{7,2},{8,13},{9,12},{10,... | collective-permute-start | bytes 196616 | tf_op jit(solution)/shard_map/ppermute | solution.py:251
  52.7 0.0 collective-permute-done.refs_1_
  52.7 0.0 collective-permute-start.5
  52.7 0.0 collective-permute-done.1.refs_2_
  52.7 0.0 copy-start
  52.7 2.9 %collective-permute-start.6 = (bf16[8,16,256]{2,1,0:T(8,128)(2,1)S(1)}, bf16[8,16,256]{2,1,0:T(8,128)(2,1)S(1)}, u32[]{:S(2)}, u32[]{:S(2)}) collective-permute-start(bf16[8,16,256]{2,1,0:T(8,128)(2,1)S(1)} %get-tuple-element.22), channel_id=1, source_target_pairs={{0,7},{1,6},{2,5},{3,4},{4,3},{5,2},{6,1},{7,0},{8,15},{9,14},{10,... | collective-permute-start | bytes 196616 | tf_op jit(solution)/shard_map/ppermute | solution.py:251
  55.6 1.3 %coef.1 = (f32[32,16,256]{2,1,0:T(8,128)S(1)}, f32[32,16,256]{2,1,0:T(8,128)S(1)}, f32[32,16,256]{2,1,0:T(8,128)S(1)}) custom-call(f32[32,16,256]{2,1,0:T(8,128)} %coef_ref.1), custom_call_target="tpu_custom_call" | custom-call | tf_op jit(solution)/shard_map/coef/pallas_call | solution.py:254
  57.0 0.0 collective-permute-done.2.refs_3_
  57.0 0.0 collective-permute-done.3.refs_4_
  57.0 0.0 collective-permute-done.4.refs_5_
  57.0 0.5 collective-permute-done.5.refs_6_
  57.5 1.7 %collective-permute-done.6.refs_7_ = bf16[8,16,256]{2,1,0:T(8,128)(2,1)S(1)} collective-permute-done((bf16[8,16,256]{2,1,0:T(8,128)(2,1)S(1)}, bf16[8,16,256]{2,1,0:T(8,128)(2,1)S(1)}, u32[]{:S(2)}, u32[]{:S(2)}) %collective-permute-start.6) | collective-permute-done | bytes 65568 | tf_op jit(solution)/shard_map/ppermute | solution.py:251
  59.1 2.9 %solve.1 = (bf16[64,16,256]{2,1,0:T(8,128)(2,1)}, bf16[128,2,128]{2,1,0:T(2,128)(2,1)}) custom-call(s32[2]{0:T(128)} %pad_add_fusion.tracer_ref.where_ref, bf16[8,16,256]{2,1,0:T(8,128)(2,1)S(1)} %get-tuple-element.15.refs_0_, bf16[8,16,256]{2,1,0:T(8,128)(2,1)S(1)} %collective-permute-done.refs_1_, bf16[8,16,256]{2,1,0:T(8,128)(2,1)S(1)} %collective-permute-done.1.refs_2_, ...), custom_call_target="tpu_custom_call" | custom-call | tf_op jit(solution)/shard_map/solve/pallas_call | solution.py:256
  62.0 4.3 %all-to-all-start.1 = ((bf16[128,2,128]{2,1,0:T(2,128)(2,1)}), bf16[128,2,128]{2,1,0:T(2,128)(2,1)S(1)}, u32[]{:S(2)}, u32[]{:S(2)}) async-start(bf16[128,2,128]{2,1,0:T(2,128)(2,1)} %get-tuple-element.27), calls=%async_computation.1 | async-start | bytes 131072 | tf_op jit(solution)/shard_map/all_to_all | solution.py:264
  66.3 0.0 copy-done
  66.3 0.1 iota_compare_fusion
  66.4 0.1 lt.20
  66.5 9.3 %all-to-all-done.1 = bf16[128,2,128]{2,1,0:T(2,128)(2,1)S(1)} async-done(((bf16[128,2,128]{2,1,0:T(2,128)(2,1)}), bf16[128,2,128]{2,1,0:T(2,128)(2,1)S(1)}, u32[]{:S(2)}, u32[]{:S(2)}) %all-to-all-start.1) | async-done | bytes 65568 | tf_op jit(solution)/shard_map/all_to_all | solution.py:264
  75.8 0.1 reshape.26
  75.9 0.1 select_bitcast_fusion
  76.1 0.7 copy.10
Async XLA Ops:
  3.1 33.0 %all-to-all-start = ((bf16[128,40,128]{2,1,0:T(8,128)(2,1)}), bf16[128,40,128]{2,1,0:T(8,128)(2,1)S(1)}, u32[]{:S(2)}, u32[]{:S(2)}) async-start(bf16[128,40,128]{2,1,0:T(8,128)(2,1)} %send.1), calls=%async_computation | async-start | bytes 2621440 | tf_op jit(solution)/shard_map/all_to_all | solution.py:246
  46.2 6.5 %collective-permute-start = (bf16[8,16,256]{2,1,0:T(8,128)(2,1)S(1)}, bf16[8,16,256]{2,1,0:T(8,128)(2,1)S(1)}, u32[]{:S(2)}, u32[]{:S(2)}) collective-permute-start(bf16[8,16,256]{2,1,0:T(8,128)(2,1)S(1)} %get-tuple-element.16), channel_id=1, source_target_pairs={{0,1},{1,0},{2,3},{3,2},{4,5},{5,4},{6,7},{7,6},{8,9},{9,8},{10,11... | collective-permute-start | bytes 196616 | tf_op jit(solution)/shard_map/ppermute | solution.py:251
  47.7 5.0 %collective-permute-start.1 = (bf16[8,16,256]{2,1,0:T(8,128)(2,1)S(1)}, bf16[8,16,256]{2,1,0:T(8,128)(2,1)S(1)}, u32[]{:S(2)}, u32[]{:S(2)}) collective-permute-start(bf16[8,16,256]{2,1,0:T(8,128)(2,1)S(1)} %get-tuple-element.17), channel_id=1, source_target_pairs={{0,2},{1,3},{2,0},{3,1},{4,6},{5,7},{6,4},{7,5},{8,10},{9,11},{10,... | collective-permute-start | bytes 196616 | tf_op jit(solution)/shard_map/ppermute | solution.py:251
  47.8 9.2 %collective-permute-start.2 = (bf16[8,16,256]{2,1,0:T(8,128)(2,1)S(1)}, bf16[8,16,256]{2,1,0:T(8,128)(2,1)S(1)}, u32[]{:S(2)}, u32[]{:S(2)}) collective-permute-start(bf16[8,16,256]{2,1,0:T(8,128)(2,1)S(1)} %get-tuple-element.18), channel_id=1, source_target_pairs={{0,3},{1,2},{2,1},{3,0},{4,7},{5,6},{6,5},{7,4},{8,11},{9,10},{10,... | collective-permute-start | bytes 196616 | tf_op jit(solution)/shard_map/ppermute | solution.py:251
  49.4 7.6 %collective-permute-start.3 = (bf16[8,16,256]{2,1,0:T(8,128)(2,1)S(1)}, bf16[8,16,256]{2,1,0:T(8,128)(2,1)S(1)}, u32[]{:S(2)}, u32[]{:S(2)}) collective-permute-start(bf16[8,16,256]{2,1,0:T(8,128)(2,1)S(1)} %get-tuple-element.19), channel_id=1, source_target_pairs={{0,4},{1,5},{2,6},{3,7},{4,0},{5,1},{6,2},{7,3},{8,12},{9,13},{10,... | collective-permute-start | bytes 196616 | tf_op jit(solution)/shard_map/ppermute | solution.py:251
  49.5 7.5 %collective-permute-start.4 = (bf16[8,16,256]{2,1,0:T(8,128)(2,1)S(1)}, bf16[8,16,256]{2,1,0:T(8,128)(2,1)S(1)}, u32[]{:S(2)}, u32[]{:S(2)}) collective-permute-start(bf16[8,16,256]{2,1,0:T(8,128)(2,1)S(1)} %get-tuple-element.20), channel_id=1, source_target_pairs={{0,5},{1,4},{2,7},{3,6},{4,1},{5,0},{6,3},{7,2},{8,13},{9,12},{10,... | collective-permute-start | bytes 196616 | tf_op jit(solution)/shard_map/ppermute | solution.py:251
  52.7 4.8 %collective-permute-start.5 = (bf16[8,16,256]{2,1,0:T(8,128)(2,1)S(1)}, bf16[8,16,256]{2,1,0:T(8,128)(2,1)S(1)}, u32[]{:S(2)}, u32[]{:S(2)}) collective-permute-start(bf16[8,16,256]{2,1,0:T(8,128)(2,1)S(1)} %get-tuple-element.21), channel_id=1, source_target_pairs={{0,6},{1,7},{2,4},{3,5},{4,2},{5,3},{6,0},{7,1},{8,14},{9,15},{10,... | collective-permute-start | bytes 196616 | tf_op jit(solution)/shard_map/ppermute | solution.py:251
  52.7 13.6 %copy-start = (s32[1,128]{1,0:T(1,128)S(1)}, s32[1,128]{1,0:T(1,128)}, u32[]{:S(2)}) copy-start(s32[1,128]{1,0:T(1,128)} %cnt_ref.1) | copy-start | bytes 1540
  52.7 6.4 %collective-permute-start.6 = (bf16[8,16,256]{2,1,0:T(8,128)(2,1)S(1)}, bf16[8,16,256]{2,1,0:T(8,128)(2,1)S(1)}, u32[]{:S(2)}, u32[]{:S(2)}) collective-permute-start(bf16[8,16,256]{2,1,0:T(8,128)(2,1)S(1)} %get-tuple-element.22), channel_id=1, source_target_pairs={{0,7},{1,6},{2,5},{3,4},{4,3},{5,2},{6,1},{7,0},{8,15},{9,14},{10,... | collective-permute-start | bytes 196616 | tf_op jit(solution)/shard_map/ppermute | solution.py:251
  62.0 13.8 %all-to-all-start.1 = ((bf16[128,2,128]{2,1,0:T(2,128)(2,1)}), bf16[128,2,128]{2,1,0:T(2,128)(2,1)S(1)}, u32[]{:S(2)}, u32[]{:S(2)}) async-start(bf16[128,2,128]{2,1,0:T(2,128)(2,1)} %get-tuple-element.27), calls=%async_computation.1 | async-start | bytes 131072 | tf_op jit(solution)/shard_map/all_to_all | solution.py:264

commit v4 on v3

--- a/solution.py
+++ b/solution.py
@@ -18,6 +18,7 @@
 SLOTS = DEV * CAP
 SHARE = LAYERS // N_GY
 ROWS = 40
+ORDER = (4, 5, 6, 7, 2, 3, 1, 0)
 BF = jnp.bfloat16
 F32 = jnp.float32
 I32 = jnp.int32
@@ -35,7 +36,7 @@
     return lax.dot_general(a, b, (dims, ((), ())), preferred_element_type=F32)
 
 
-def send_kernel(inn_ref, col_ref, cnt_ref, mask_ref, out_ref):
+def send_kernel(inn_ref, col_ref, cnt_ref, mask_ref, out_ref, code_ref, message_ref, sems):
     counts = jnp.broadcast_to(cnt_ref[...], (8, DEV)).astype(F32).astype(BF)
     spread = one_hot(iota((DEV, SLOTS), 1) // CAP == iota((DEV, SLOTS), 0))
     count_lane = dot(counts, spread)[0:1, :]
@@ -63,13 +64,20 @@
         + [moved[1:2, c * DEV : (c + 1) * DEV] for c in range(CAP)],
         axis=0,
     ).astype(BF)
+    code_ref[...] = tile.astype(F32)
     for b in range(N_GY):
         block = values[b * SHARE : (b + 1) * SHARE, :]
-        message = jnp.concatenate(
+        message_ref[b] = jnp.concatenate(
             [block[:, q * DEV : (q + 1) * DEV] for q in range(CAP)] + [tile], axis=0
         )
-        for a in range(N_GX):
-            out_ref[a * N_GY + b] = message
+    copies = [
+        pltpu.make_async_copy(message_ref, out_ref.at[pl.ds(a * N_GY, N_GY)], sems.at[a])
+        for a in range(N_GX)
+    ]
+    for copy in copies:
+        copy.start()
+    for copy in copies:
+        copy.wait()
 
 
 def smooth_kernel(
@@ -119,9 +127,11 @@
             rhs = jnp.concatenate(right, axis=0)
             dense = dot(lhs, rhs)
             dense_ref[b * 128 : (b + 1) * 128, :] = dense.astype(BF)
-        gain = dot(dense_ref[...], kx_vmem[pl.ds(pl.multiple_of(step * CX, CX), CX), :])
-        for h in range(2):
-            acc_ref[h * 1024 : (h + 1) * 1024, :] += gain[:, h * 128 : (h + 1) * 128]
+        kernel_rows = kx_vmem[pl.ds(pl.multiple_of(step * CX, CX), CX), :]
+        for m in range(2):
+            gain = dot(dense_ref[m * 512 : (m + 1) * 512, :], kernel_rows)
+            for h in range(2):
+                acc_ref[h * 1024 + m * 512 : h * 1024 + (m + 1) * 512, :] += gain[:, h * 128 : (h + 1) * 128]
         return carry
 
     lax.fori_loop(0, N_GX, column_block, 0, unroll=16)
@@ -132,9 +142,9 @@
         along_y = dot(ky_ref[tracer_ref[0]], along_x, ((0,), (0,))).astype(BF)
         along_ref[l] = along_y
     mine = tracer_ref[1]
-    for k in range(N_GY):
+    for out_ref, k in zip(out_refs, ORDER):
         row = pl.multiple_of((mine ^ k) * CY, CY)
-        out_refs[k][...] = along_ref[:, pl.ds(row, CY), :]
+        out_ref[...] = along_ref[:, pl.ds(row, CY), :]
 
 
 def smooth_call(tracer, got, inverse_x, inverse_y):
@@ -180,10 +190,10 @@
 
 def solve_kernel(where_ref, *refs):
     parts = refs[:N_GY]
-    inv_ref, gain_ref, ratio_ref, mask_ref, col_ref, inc_ref, pick_ref, field_ref, part_ref = refs[N_GY:]
+    inv_ref, gain_ref, ratio_ref, mask_ref, code_ref, inc_ref, pick_ref, field_ref, part_ref = refs[N_GY:]
     mine = where_ref[1]
-    for k in range(N_GY):
-        field_ref[pl.ds((mine ^ k) * SHARE, SHARE)] = parts[k][...]
+    for part, k in zip(parts, ORDER):
+        field_ref[pl.ds((mine ^ k) * SHARE, SHARE)] = part[...]
     mask = mask_ref[...].astype(F32)
     prev0 = prev1 = None
     for k in range(LEV):
@@ -203,24 +213,17 @@
             x1 = part_ref[LEV + k] - ratio_ref[k] * x1
         inc_ref[k] = (x0 * mask).astype(BF)
         inc_ref[LEV + k] = (x1 * mask).astype(BF)
-    cells = col_ref[...]
-    row = cells // CX
-    col = cells % CX
-    packed = jnp.concatenate([row.astype(F32), col.astype(F32)] + [jnp.zeros((6, SLOTS), F32)], axis=0).astype(BF)
-    source = iota((SLOTS, SLOTS), 0)
-    target = iota((SLOTS, SLOTS), 1)
-    moved = dot(packed, one_hot((source % CAP) * DEV + source // CAP == target))
-    row = moved[0:1, :].astype(I32)
-    col = moved[1:2, :].astype(I32)
+    codes = code_ref[...]
+    row = jnp.concatenate([codes[c : c + 1, :] for c in range(CAP)], axis=1).astype(I32)
+    col = jnp.concatenate([codes[CAP + c : CAP + c + 1, :] for c in range(CAP)], axis=1).astype(I32)
     pick_col = one_hot(iota((CX, SLOTS), 0) == col)
-    row_iota = iota((LAYERS * CY, SLOTS), 0) % CY
     found = dot(inc_ref[...].reshape(LAYERS * CY, CX), pick_col)
-    chosen = jnp.where(row_iota == row, found, 0.0).astype(BF)
+    chosen = jnp.where(iota((LAYERS * CY, SLOTS), 0) % CY == row, found, 0.0).astype(BF)
     total = one_hot(iota((LAYERS, LAYERS * CY), 1) // CY == iota((LAYERS, LAYERS * CY), 0))
-    picked = dot(chosen, total, ((0,), (1,))).astype(BF)
+    picked = dot(total, chosen)
+    turned = [picked[:, c * DEV : (c + 1) * DEV].T for c in range(CAP)]
     for r in range(2):
-        pair = [picked[(2 * r + h) * DEV : (2 * r + h + 1) * DEV, :] for h in range(2)]
-        pick_ref[:, r, :] = jnp.concatenate(pair, axis=1)
+        pick_ref[:, r, :] = jnp.concatenate(turned[2 * r : 2 * r + 2], axis=1).astype(BF)
 
 
 def in_vmem(x):
@@ -240,27 +243,33 @@
 
 def body(innovations, station_columns, profile_counts, land_mask, vertical_coef, inverse_x, inverse_y):
     everyone = ("gx", "gy")
-    message = call(send_kernel, pltpu.VMEM((DEV, ROWS, DEV), BF), 4, "send")(
-        innovations, station_columns, profile_counts, land_mask
-    )
+    vmem = pl.BlockSpec(memory_space=pltpu.VMEM)
+    message, codes = pl.pallas_call(
+        send_kernel,
+        out_shape=(jax.ShapeDtypeStruct((DEV, ROWS, DEV), BF), pltpu.VMEM((2 * CAP, DEV), F32)),
+        in_specs=[vmem] * 4,
+        out_specs=(pl.BlockSpec(memory_space=pl.ANY), vmem),
+        scratch_shapes=[pltpu.VMEM((N_GY, ROWS, DEV), BF), pltpu.SemaphoreType.DMA((N_GX,))],
+        name="send",
+    )(innovations, station_columns, profile_counts, land_mask)
     got = lax.all_to_all(message, everyone, split_axis=0, concat_axis=0, tiled=True)
     mine = lax.axis_index("gy").astype(I32)
     where = jnp.stack([mine * SHARE // LEV, mine])
     products = smooth_call(where, in_vmem(got), inverse_x, inverse_y)
-    parts = [products[0]] + [
-        lax.ppermute(products[k], "gy", [(i, i ^ k) for i in range(N_GY)]) for k in range(1, N_GY)
+    parts = [
+        lax.ppermute(product, "gy", [(i, i ^ k) for i in range(N_GY)]) if k else product
+        for product, k in zip(products, ORDER)
     ]
     plane = pltpu.VMEM((LEV, CY, CX), F32)
     inv, gain, ratio = call(coef_kernel, (plane, plane, plane), 1, "coef")(vertical_coef)
-    vmem = pl.BlockSpec(memory_space=pltpu.VMEM)
     increment, picked = pl.pallas_call(
         solve_kernel,
-        out_shape=(jax.ShapeDtypeStruct((LAYERS, CY, CX), BF), pltpu.VMEM((DEV, 2, DEV), BF)),
+        out_shape=(pltpu.VMEM((LAYERS, CY, CX), BF), pltpu.VMEM((DEV, 2, DEV), BF)),
         in_specs=[pl.BlockSpec(memory_space=pltpu.SMEM)] + [vmem] * (N_GY + 5),
         out_specs=(vmem, vmem),
         scratch_shapes=[pltpu.VMEM((LAYERS, CY, CX), BF), pltpu.VMEM((LAYERS, CY, CX), F32)],
         name="solve",
-    )(where, *[in_vmem(p) for p in parts], in_vmem(inv), in_vmem(gain), in_vmem(ratio), land_mask, station_columns)
+    )(where, *[in_vmem(p) for p in parts], in_vmem(inv), in_vmem(gain), in_vmem(ratio), land_mask, in_vmem(codes))
     returned = lax.all_to_all(picked, everyone, split_axis=0, concat_axis=0, tiled=True)
     returned = returned.reshape(SLOTS, LAYERS).T.reshape(1, LAYERS, SLOTS)
     slot_index = lax.broadcasted_iota(I32, (DEV, CAP), 1)

time: 77.2 us -> 75.6 us (0.979)
  waiting for transfers between devices: 32.4 us -> 31 us
  local copies, waits for them, and re-layouts: 0.95 us -> 1.74 us
    all_to_all x1, waiting for transfers between devices: 9.34 us -> 8.54 us  [body(): lax.all_to_all(picked, everyone, split_axis=0, concat_axis=0, tiled=True)]
    unnamed x3 -> x4, local copies, waits for them, and re-layouts: 0.73 us -> 1.53 us
  transfers between devices with their start and end apart: 9 -> 9, of which waited for: 4 -> 3; matrix products, arithmetic and copies ran while one was open for 1% -> 2% of each run, Pallas kernels for 2% -> 2%
where the time goes in v4:
time: 75.6 us; the launch traced here: 75.2 us
  waiting for transfers between devices  31 us (41%)
  starting transfers between devices  24.8 us (33%)
  Pallas kernels  16.1 us (21%)
  local copies, waits for them, and re-layouts  1.74 us (2%)
  other arithmetic  0.84 us (1%)
    all_to_all x1, waiting for transfers between devices, body(): lax.all_to_all(message, everyone, split_axis=0, concat_axis=0, tiled=True)  20.9 us
    all_to_all x1, starting transfers between devices, body(): lax.all_to_all(message, everyone, split_axis=0, concat_axis=0, tiled=True)  11.5 us
    pallas_call x1, Pallas kernels, smooth_call(): pl.pallas_call(smooth_kernel, out_shape=[pltpu.VMEM((SHARE, CY, CX), BF)]...  9.85 us
    ppermute x7, starting transfers between devices, body(): lax.ppermute(product, 'gy', [(i, i ^ k) for i in range(N_GY)])  9.33 us
    all_to_all x1, waiting for transfers between devices, body(): lax.all_to_all(picked, everyone, split_axis=0, concat_axis=0, tiled=True)  8.54 us
    all_to_all x1, starting transfers between devices, body(): lax.all_to_all(picked, everyone, split_axis=0, concat_axis=0, tiled=True)  3.95 us
    pallas_call x1, Pallas kernels, body(): pl.pallas_call(solve_kernel, out_shape=(pltpu.VMEM((LAYERS, CY, CX), BF),...  2.48 us
    pallas_call x1, Pallas kernels, body(): pl.pallas_call(send_kernel, out_shape=(jax.ShapeDtypeStruct((DEV, ROWS, D...  2.44 us
  transfers between devices with their start and end apart: 9, of which 3 were waited for; matrix products, arithmetic and copies ran while one was open for 2% of the time, Pallas kernels for 2%

profile of v4, /device:TPU:1, one launch (start us, length us, event | category | flops | bytes accessed | tf_op | source)
XLA Modules:
  0.0 75.2 jit_solution(3859228642871129592)
XLA Ops:
  0.6 2.4 %send.1 = (bf16[128,40,128]{2,1,0:T(8,128)(2,1)}, f32[8,128]{1,0:T(8,128)S(1)}) custom-call(bf16[1,64,512]{2,1,0:T(8,128)(2,1)} %inn_ref.1, s32[1,512]{1,0:T(1,128)} %col_ref.1, s32[1,128]{1,0:T(1,128)} %cnt_ref.1, s32[16,256]{1,0:T(8,128)} %refs_11_.1), custom_call_target="tpu_custom_call" | custom-call | tf_op jit(solution)/shard_map/send/pallas_call | solution.py:247
  3.1 11.5 %all-to-all-start = ((bf16[128,40,128]{2,1,0:T(8,128)(2,1)}), bf16[128,40,128]{2,1,0:T(8,128)(2,1)S(1)}, u32[]{:S(2)}, u32[]{:S(2)}) async-start(bf16[128,40,128]{2,1,0:T(8,128)(2,1)} %get-tuple-element.17), calls=%async_computation | async-start | bytes 2621440 | tf_op jit(solution)/shard_map/all_to_all | solution.py:255
  14.6 0.6 pad_add_fusion.tracer_ref.where_ref
  15.2 20.9 %all-to-all-done.got_ref = bf16[128,40,128]{2,1,0:T(8,128)(2,1)S(1)} async-done(((bf16[128,40,128]{2,1,0:T(8,128)(2,1)}), bf16[128,40,128]{2,1,0:T(8,128)(2,1)S(1)}, u32[]{:S(2)}, u32[]{:S(2)}) %all-to-all-start) | async-done | bytes 1310752 | tf_op jit(solution)/shard_map/all_to_all | solution.py:255
  36.1 9.9 %smooth.1 = (bf16[8,16,256]{2,1,0:T(8,128)(2,1)S(1)}, bf16[8,16,256]{2,1,0:T(8,128)(2,1)S(1)}, bf16[8,16,256]{2,1,0:T(8,128)(2,1)S(1)}, bf16[8,16,256]{2,1,0:T(8...) custom-call(s32[2]{0:T(128)} %pad_add_fusion.tracer_ref.where_ref, ...), custom_call_target="tpu_custom_call" | custom-call | tf_op jit(solution)/shard_map/smooth/pallas_call | solution.py:152
  46.0 0.8 %collective-permute-start = (bf16[8,16,256]{2,1,0:T(8,128)(2,1)S(1)}, bf16[8,16,256]{2,1,0:T(8,128)(2,1)S(1)}, u32[]{:S(2)}, u32[]{:S(2)}) collective-permute-start(bf16[8,16,256]{2,1,0:T(8,128)(2,1)S(1)} %get-tuple-element.18), channel_id=1, source_target_pairs={{0,4},{1,5},{2,6},{3,7},{4,0},{5,1},{6,2},{7,3},{8,12},{9,13},{10,... | collective-permute-start | bytes 196616 | tf_op jit(solution)/shard_map/ppermute | solution.py:260
  46.7 3.9 %collective-permute-start.1 = (bf16[8,16,256]{2,1,0:T(8,128)(2,1)S(1)}, bf16[8,16,256]{2,1,0:T(8,128)(2,1)S(1)}, u32[]{:S(2)}, u32[]{:S(2)}) collective-permute-start(bf16[8,16,256]{2,1,0:T(8,128)(2,1)S(1)} %get-tuple-element.19), channel_id=1, source_target_pairs={{0,5},{1,4},{2,7},{3,6},{4,1},{5,0},{6,3},{7,2},{8,13},{9,12},{10,... | collective-permute-start | bytes 196616 | tf_op jit(solution)/shard_map/ppermute | solution.py:260
  50.6 0.0 collective-permute-start.2
  50.6 1.7 %collective-permute-start.3 = (bf16[8,16,256]{2,1,0:T(8,128)(2,1)S(1)}, bf16[8,16,256]{2,1,0:T(8,128)(2,1)S(1)}, u32[]{:S(2)}, u32[]{:S(2)}) collective-permute-start(bf16[8,16,256]{2,1,0:T(8,128)(2,1)S(1)} %get-tuple-element.21), channel_id=1, source_target_pairs={{0,7},{1,6},{2,5},{3,4},{4,3},{5,2},{6,1},{7,0},{8,15},{9,14},{10,... | collective-permute-start | bytes 196616 | tf_op jit(solution)/shard_map/ppermute | solution.py:260
  52.3 0.0 collective-permute-start.4
  52.3 0.0 collective-permute-done.refs_0_
  52.3 3.0 %collective-permute-start.5 = (bf16[8,16,256]{2,1,0:T(8,128)(2,1)S(1)}, bf16[8,16,256]{2,1,0:T(8,128)(2,1)S(1)}, u32[]{:S(2)}, u32[]{:S(2)}) collective-permute-start(bf16[8,16,256]{2,1,0:T(8,128)(2,1)S(1)} %get-tuple-element.23), channel_id=1, source_target_pairs={{0,3},{1,2},{2,1},{3,0},{4,7},{5,6},{6,5},{7,4},{8,11},{9,10},{10,... | collective-permute-start | bytes 196616 | tf_op jit(solution)/shard_map/ppermute | solution.py:260
  55.3 0.0 collective-permute-done.1.refs_1_
  55.3 0.0 copy-start
  55.3 0.0 collective-permute-start.6
  55.3 1.3 %coef.1 = (f32[32,16,256]{2,1,0:T(8,128)S(1)}, f32[32,16,256]{2,1,0:T(8,128)S(1)}, f32[32,16,256]{2,1,0:T(8,128)S(1)}) custom-call(f32[32,16,256]{2,1,0:T(8,128)} %coef_ref.1), custom_call_target="tpu_custom_call" | custom-call | tf_op jit(solution)/shard_map/coef/pallas_call | solution.py:264
  56.7 0.0 collective-permute-done.2.refs_2_
  56.7 0.0 collective-permute-done.3.refs_3_
  56.7 0.0 collective-permute-done.4.refs_4_
  56.7 1.5 %collective-permute-done.5.refs_5_ = bf16[8,16,256]{2,1,0:T(8,128)(2,1)S(1)} collective-permute-done((bf16[8,16,256]{2,1,0:T(8,128)(2,1)S(1)}, bf16[8,16,256]{2,1,0:T(8,128)(2,1)S(1)}, u32[]{:S(2)}, u32[]{:S(2)}) %collective-permute-start.5) | collective-permute-done | bytes 65568 | tf_op jit(solution)/shard_map/ppermute | solution.py:260
  58.2 0.0 collective-permute-done.6.refs_6_
  58.2 2.5 %solve.1 = (bf16[64,16,256]{2,1,0:T(8,128)(2,1)S(1)}, bf16[128,2,128]{2,1,0:T(2,128)(2,1)}) custom-call(s32[2]{0:T(128)} %pad_add_fusion.tracer_ref.where_ref, bf16[8,16,256]{2,1,0:T(8,128)(2,1)S(1)} %collective-permute-done.refs_0_, bf16[8,16,256]{2,1,0:T(8,128)(2,1)S(1)} %collective-permute-done.1.refs_1_, ...), custom_call_target="tpu_custom_call" | custom-call | tf_op jit(solution)/shard_map/solve/pallas_call | solution.py:265
  60.7 3.9 %all-to-all-start.1 = ((bf16[128,2,128]{2,1,0:T(2,128)(2,1)}), bf16[128,2,128]{2,1,0:T(2,128)(2,1)S(1)}, u32[]{:S(2)}, u32[]{:S(2)}) async-start(bf16[128,2,128]{2,1,0:T(2,128)(2,1)} %get-tuple-element.31), calls=%async_computation.1 | async-start | bytes 131072 | tf_op jit(solution)/shard_map/all_to_all | solution.py:273
  64.6 0.0 copy-done
  64.6 0.1 iota_compare_fusion
  64.7 0.1 lt.20
  64.8 0.8 %copy.11 = bf16[64,16,256]{2,1,0:T(8,128)(2,1)} copy(bf16[64,16,256]{2,1,0:T(8,128)(2,1)S(1)} %get-tuple-element.34) | data formatting | bytes 1048576
  65.6 8.5 %all-to-all-done.1 = bf16[128,2,128]{2,1,0:T(2,128)(2,1)S(1)} async-done(((bf16[128,2,128]{2,1,0:T(2,128)(2,1)}), bf16[128,2,128]{2,1,0:T(2,128)(2,1)S(1)}, u32[]{:S(2)}, u32[]{:S(2)}) %all-to-all-start.1) | async-done | bytes 65568 | tf_op jit(solution)/shard_map/all_to_all | solution.py:273
  74.2 0.1 reshape.26
  74.3 0.1 select_bitcast_fusion
  74.4 0.7 copy.10
Async XLA Ops:
  3.1 33.0 %all-to-all-start = ((bf16[128,40,128]{2,1,0:T(8,128)(2,1)}), bf16[128,40,128]{2,1,0:T(8,128)(2,1)S(1)}, u32[]{:S(2)}, u32[]{:S(2)}) async-start(bf16[128,40,128]{2,1,0:T(8,128)(2,1)} %get-tuple-element.17), calls=%async_computation | async-start | bytes 2621440 | tf_op jit(solution)/shard_map/all_to_all | solution.py:255
  46.0 6.3 %collective-permute-start = (bf16[8,16,256]{2,1,0:T(8,128)(2,1)S(1)}, bf16[8,16,256]{2,1,0:T(8,128)(2,1)S(1)}, u32[]{:S(2)}, u32[]{:S(2)}) collective-permute-start(bf16[8,16,256]{2,1,0:T(8,128)(2,1)S(1)} %get-tuple-element.18), channel_id=1, source_target_pairs={{0,4},{1,5},{2,6},{3,7},{4,0},{5,1},{6,2},{7,3},{8,12},{9,13},{10,... | collective-permute-start | bytes 196616 | tf_op jit(solution)/shard_map/ppermute | solution.py:260
  46.7 8.6 %collective-permute-start.1 = (bf16[8,16,256]{2,1,0:T(8,128)(2,1)S(1)}, bf16[8,16,256]{2,1,0:T(8,128)(2,1)S(1)}, u32[]{:S(2)}, u32[]{:S(2)}) collective-permute-start(bf16[8,16,256]{2,1,0:T(8,128)(2,1)S(1)} %get-tuple-element.19), channel_id=1, source_target_pairs={{0,5},{1,4},{2,7},{3,6},{4,1},{5,0},{6,3},{7,2},{8,13},{9,12},{10,... | collective-permute-start | bytes 196616 | tf_op jit(solution)/shard_map/ppermute | solution.py:260
  50.6 6.1 %collective-permute-start.2 = (bf16[8,16,256]{2,1,0:T(8,128)(2,1)S(1)}, bf16[8,16,256]{2,1,0:T(8,128)(2,1)S(1)}, u32[]{:S(2)}, u32[]{:S(2)}) collective-permute-start(bf16[8,16,256]{2,1,0:T(8,128)(2,1)S(1)} %get-tuple-element.20), channel_id=1, source_target_pairs={{0,6},{1,7},{2,4},{3,5},{4,2},{5,3},{6,0},{7,1},{8,14},{9,15},{10,... | collective-permute-start | bytes 196616 | tf_op jit(solution)/shard_map/ppermute | solution.py:260
  50.6 6.1 %collective-permute-start.3 = (bf16[8,16,256]{2,1,0:T(8,128)(2,1)S(1)}, bf16[8,16,256]{2,1,0:T(8,128)(2,1)S(1)}, u32[]{:S(2)}, u32[]{:S(2)}) collective-permute-start(bf16[8,16,256]{2,1,0:T(8,128)(2,1)S(1)} %get-tuple-element.21), channel_id=1, source_target_pairs={{0,7},{1,6},{2,5},{3,4},{4,3},{5,2},{6,1},{7,0},{8,15},{9,14},{10,... | collective-permute-start | bytes 196616 | tf_op jit(solution)/shard_map/ppermute | solution.py:260
  52.3 4.4 %collective-permute-start.4 = (bf16[8,16,256]{2,1,0:T(8,128)(2,1)S(1)}, bf16[8,16,256]{2,1,0:T(8,128)(2,1)S(1)}, u32[]{:S(2)}, u32[]{:S(2)}) collective-permute-start(bf16[8,16,256]{2,1,0:T(8,128)(2,1)S(1)} %get-tuple-element.22), channel_id=1, source_target_pairs={{0,2},{1,3},{2,0},{3,1},{4,6},{5,7},{6,4},{7,5},{8,10},{9,11},{10,... | collective-permute-start | bytes 196616 | tf_op jit(solution)/shard_map/ppermute | solution.py:260
  52.3 5.9 %collective-permute-start.5 = (bf16[8,16,256]{2,1,0:T(8,128)(2,1)S(1)}, bf16[8,16,256]{2,1,0:T(8,128)(2,1)S(1)}, u32[]{:S(2)}, u32[]{:S(2)}) collective-permute-start(bf16[8,16,256]{2,1,0:T(8,128)(2,1)S(1)} %get-tuple-element.23), channel_id=1, source_target_pairs={{0,3},{1,2},{2,1},{3,0},{4,7},{5,6},{6,5},{7,4},{8,11},{9,10},{10,... | collective-permute-start | bytes 196616 | tf_op jit(solution)/shard_map/ppermute | solution.py:260
  55.3 9.3 %copy-start = (s32[1,128]{1,0:T(1,128)S(1)}, s32[1,128]{1,0:T(1,128)}, u32[]{:S(2)}) copy-start(s32[1,128]{1,0:T(1,128)} %cnt_ref.1) | copy-start | bytes 1540
  55.3 2.9 %collective-permute-start.6 = (bf16[8,16,256]{2,1,0:T(8,128)(2,1)S(1)}, bf16[8,16,256]{2,1,0:T(8,128)(2,1)S(1)}, u32[]{:S(2)}, u32[]{:S(2)}) collective-permute-start(bf16[8,16,256]{2,1,0:T(8,128)(2,1)S(1)} %get-tuple-element.24), channel_id=1, source_target_pairs={{0,1},{1,0},{2,3},{3,2},{4,5},{5,4},{6,7},{7,6},{8,9},{9,8},{10,11... | collective-permute-start | bytes 196616 | tf_op jit(solution)/shard_map/ppermute | solution.py:260
  60.7 13.5 %all-to-all-start.1 = ((bf16[128,2,128]{2,1,0:T(2,128)(2,1)}), bf16[128,2,128]{2,1,0:T(2,128)(2,1)S(1)}, u32[]{:S(2)}, u32[]{:S(2)}) async-start(bf16[128,2,128]{2,1,0:T(2,128)(2,1)} %get-tuple-element.31), calls=%async_computation.1 | async-start | bytes 131072 | tf_op jit(solution)/shard_map/all_to_all | solution.py:273

commit v5 on v4

--- a/solution.py
+++ b/solution.py
@@ -1,4 +1,3 @@
-import functools
 import jax
 import jax.numpy as jnp
 from jax import lax
@@ -34,6 +33,13 @@
 
 def dot(a, b, dims=((1,), (0,))):
     return lax.dot_general(a, b, (dims, ((), ())), preferred_element_type=F32)
+
+
+def by_source():
+    source = iota((SLOTS, SLOTS), 0)
+    owner = source % DEV
+    lane = (owner % N_GY) * 64 + (source // DEV) * N_GX + owner // N_GY
+    return one_hot(lane == iota((SLOTS, SLOTS), 1))
 
 
 def send_kernel(inn_ref, col_ref, cnt_ref, mask_ref, out_ref, code_ref, message_ref, sems):
@@ -84,7 +90,7 @@
     tracer_ref, got_ref, kx_ref, ky_ref, *refs
 ):
     out_refs = refs[:N_GY]
-    wide_ref, turned_ref, column_ref, dense_ref, acc_ref, along_ref, kx_vmem, sem = refs[N_GY:]
+    wide_ref, turned_ref, column_ref, dense_ref, acc_ref, along_ref, station_ref, kx_vmem, sem = refs[N_GY:]
     fetch = pltpu.make_async_copy(kx_ref.at[tracer_ref[0]], kx_vmem, sem)
     fetch.start()
     acc_ref[...] = jnp.zeros_like(acc_ref)
@@ -141,17 +147,41 @@
         ).astype(BF)
         along_y = dot(ky_ref[tracer_ref[0]], along_x, ((0,), (0,))).astype(BF)
         along_ref[l] = along_y
+        for h in range(2):
+            acc_ref[pl.ds(h * 1024 + l, NY, stride=SHARE), :] = along_y[:, h * 128 : (h + 1) * 128].astype(F32)
+    own = [got_ref[tracer_ref[2] * N_GY + b, 32:40, :].astype(F32) for b in range(N_GY)]
+    lines = [jnp.concatenate([x[c : c + 1, :] for c in range(CAP)], axis=1) for x in own]
+    lines += [jnp.concatenate([x[CAP + c : CAP + c + 1, :] for c in range(CAP)], axis=1) for x in own]
+    moved = dot(jnp.concatenate(lines, axis=0).astype(BF), by_source())
+    tall_iota = iota((CX, SLOTS), 0).astype(F32).astype(BF)
+    found = []
+    for b in range(N_GY):
+        field = jnp.concatenate(
+            [acc_ref[h * 1024 + b * 128 : h * 1024 + (b + 1) * 128, :] for h in range(2)], axis=1
+        ).astype(BF)
+        col = jnp.broadcast_to(moved[N_GY + b : N_GY + b + 1, :], (16, SLOTS)).astype(BF)
+        hit = jnp.where(jnp.concatenate([col] * (CX // 16), axis=0) == tall_iota, one, zero)
+        values = dot(field, hit)
+        row = jnp.broadcast_to(moved[b : b + 1, :], (SHARE, SLOTS))
+        total = jnp.zeros((SHARE, SLOTS), F32)
+        for j in range(CY):
+            total = total + jnp.where(row == j, values[j * SHARE : (j + 1) * SHARE, :], 0.0)
+        found.append(total)
+    for g in range(N_GY):
+        line = jnp.concatenate([x[:, g * 64 : (g + 1) * 64] for x in found], axis=1)
+        station_ref[g] = jnp.concatenate([line[:, :CX], line[:, CX:]], axis=0).astype(BF)
     mine = tracer_ref[1]
     for out_ref, k in zip(out_refs, ORDER):
         row = pl.multiple_of((mine ^ k) * CY, CY)
-        out_ref[...] = along_ref[:, pl.ds(row, CY), :]
+        out_ref[0:SHARE] = along_ref[:, pl.ds(row, CY), :]
+        out_ref[SHARE] = station_ref[mine ^ k]
 
 
 def smooth_call(tracer, got, inverse_x, inverse_y):
     vmem = pl.BlockSpec(memory_space=pltpu.VMEM)
     return pl.pallas_call(
         smooth_kernel,
-        out_shape=[pltpu.VMEM((SHARE, CY, CX), BF)] * N_GY,
+        out_shape=[pltpu.VMEM((SHARE + 1, CY, CX), BF)] * N_GY,
         in_specs=[
             pl.BlockSpec(memory_space=pltpu.SMEM),
             vmem,
@@ -166,6 +196,7 @@
             pltpu.VMEM((NY * SHARE, CX), BF),
             pltpu.VMEM((2 * NY * SHARE, 128), F32),
             pltpu.VMEM((SHARE, NY, CX), BF),
+            pltpu.VMEM((N_GY, CY, CX), BF),
             pltpu.VMEM((N_GX * CX, CX), BF),
             pltpu.SemaphoreType.DMA(()),
         ],
@@ -190,10 +221,10 @@
 
 def solve_kernel(where_ref, *refs):
     parts = refs[:N_GY]
-    inv_ref, gain_ref, ratio_ref, mask_ref, code_ref, inc_ref, pick_ref, field_ref, part_ref = refs[N_GY:]
+    inv_ref, gain_ref, ratio_ref, mask_ref, _, inc_ref, field_ref, part_ref = refs[N_GY:]
     mine = where_ref[1]
     for part, k in zip(parts, ORDER):
-        field_ref[pl.ds((mine ^ k) * SHARE, SHARE)] = part[...]
+        field_ref[pl.ds((mine ^ k) * SHARE, SHARE)] = part[0:SHARE]
     mask = mask_ref[...].astype(F32)
     prev0 = prev1 = None
     for k in range(LEV):
@@ -213,35 +244,109 @@
             x1 = part_ref[LEV + k] - ratio_ref[k] * x1
         inc_ref[k] = (x0 * mask).astype(BF)
         inc_ref[LEV + k] = (x1 * mask).astype(BF)
+
+
+def gather_kernel(where_ref, coef_ref, code_ref, *refs):
+    out_refs = refs[:N_GY]
+    found_ref = refs[N_GY]
     codes = code_ref[...]
-    row = jnp.concatenate([codes[c : c + 1, :] for c in range(CAP)], axis=1).astype(I32)
-    col = jnp.concatenate([codes[CAP + c : CAP + c + 1, :] for c in range(CAP)], axis=1).astype(I32)
-    pick_col = one_hot(iota((CX, SLOTS), 0) == col)
-    found = dot(inc_ref[...].reshape(LAYERS * CY, CX), pick_col)
-    chosen = jnp.where(iota((LAYERS * CY, SLOTS), 0) % CY == row, found, 0.0).astype(BF)
-    total = one_hot(iota((LAYERS, LAYERS * CY), 1) // CY == iota((LAYERS, LAYERS * CY), 0))
-    picked = dot(total, chosen)
-    turned = [picked[:, c * DEV : (c + 1) * DEV].T for c in range(CAP)]
-    for r in range(2):
-        pick_ref[:, r, :] = jnp.concatenate(turned[2 * r : 2 * r + 2], axis=1).astype(BF)
+    lines = [jnp.concatenate([codes[h * CAP + c : h * CAP + c + 1, :] for c in range(CAP)], axis=1) for h in range(2)]
+    moved = dot(jnp.concatenate(lines + [jnp.zeros((6, SLOTS), F32)], axis=0).astype(BF), by_source())
+    row = moved[0:1, :].astype(I32)
+    hit = one_hot(iota((CX, SLOTS), 0) == moved[1:2, :].astype(I32))
+    whole = coef_ref[...].reshape(LEV * CY, CX)
+    high = whole.astype(BF)
+    rest = whole - high.astype(F32)
+    middle = rest.astype(BF)
+    low = (rest - middle.astype(F32)).astype(BF)
+    values = dot(high, hit) + dot(middle, hit) + dot(low, hit)
+    chosen = jnp.where(iota((LEV * CY, SLOTS), 0) % CY == row, values, 0.0)
+    lines = jnp.sum(chosen.reshape(LEV, CY, SLOTS), axis=1)
+    for g in range(N_GY):
+        tile = lines[:, (g // 2) * DEV : (g // 2 + 1) * DEV]
+        found_ref[g] = pltpu.roll(tile, 64, 1) if g % 2 else tile
+    for out_ref, k in zip(out_refs, ORDER):
+        out_ref[...] = found_ref[where_ref[1] ^ k]
+
+
+def station_coef_kernel(where_ref, *refs):
+    parts = refs[:N_GY]
+    inv_ref, gain_ref, ratio_ref, stage_ref, coef_ref = refs[N_GY:]
+    for part, k in zip(parts, ORDER):
+        stage_ref[where_ref[1] ^ k] = part[...]
+    low = iota((LEV, DEV), 1) < 64
+    for t in range(CAP):
+        coef_ref[:, t * DEV : (t + 1) * DEV] = jnp.where(
+            low, stage_ref[2 * t], pltpu.roll(stage_ref[2 * t + 1], 64, 1)
+        )
+    ratio = None
+    for k in range(LEV):
+        here = coef_ref[k : k + 1, :]
+        below = coef_ref[k + 1 : k + 2, :] if k + 1 < LEV else jnp.zeros_like(here)
+        diagonal = 1.0 + here + below
+        if k > 0:
+            diagonal = diagonal + here * ratio
+        inv = 1.0 / diagonal
+        ratio = -below * inv
+        inv_ref[k : k + 1, :] = inv
+        gain_ref[k : k + 1, :] = here * inv
+        ratio_ref[k : k + 1, :] = ratio
+
+
+def station_kernel(where_ref, *refs):
+    parts = refs[:N_GY]
+    inv_ref, gain_ref, ratio_ref, out_ref, field_ref, part_ref, turned_ref = refs[N_GY:]
+    for part, k in zip(parts, ORDER):
+        start = pl.multiple_of((where_ref[1] ^ k) * SHARE, SHARE)
+        both = part[SHARE].astype(F32)
+        field_ref[pl.ds(start, SHARE), 0:CX] = both[0:SHARE]
+        field_ref[pl.ds(start, SHARE), CX:SLOTS] = both[SHARE:CY]
+    prev0 = prev1 = None
+    for k in range(LEV):
+        inv = inv_ref[k : k + 1, :]
+        f0 = field_ref[k : k + 1, :] * inv
+        f1 = field_ref[LEV + k : LEV + k + 1, :] * inv
+        if k == 0:
+            prev0, prev1 = f0, f1
+        else:
+            gain = gain_ref[k : k + 1, :]
+            prev0 = f0 + gain * prev0
+            prev1 = f1 + gain * prev1
+        part_ref[k : k + 1, :] = prev0
+        part_ref[LEV + k : LEV + k + 1, :] = prev1
+    x0, x1 = prev0, prev1
+    for k in range(LEV - 2, -1, -1):
+        ratio = ratio_ref[k : k + 1, :]
+        x0 = part_ref[k : k + 1, :] - ratio * x0
+        x1 = part_ref[LEV + k : LEV + k + 1, :] - ratio * x1
+        part_ref[k : k + 1, :] = x0
+        part_ref[LEV + k : LEV + k + 1, :] = x1
+    empty = jnp.zeros((DEV - LAYERS, DEV), F32)
+    for t in range(CAP):
+        tile = jnp.concatenate([part_ref[:, t * DEV : (t + 1) * DEV], empty], axis=0)
+        turned_ref[t * DEV : (t + 1) * DEV, :] = tile.T
+    left = iota((N_GX, DEV), 1) < LAYERS
+    for g in range(N_GX):
+        even = turned_ref[pl.ds(g, N_GX, stride=32), :]
+        odd = turned_ref[pl.ds(N_GX + g, N_GX, stride=32), :]
+        out_ref[g] = jnp.where(left, even, pltpu.roll(odd, 64, 1)).astype(BF)
 
 
 def in_vmem(x):
     return pltpu.with_memory_space_constraint(x, pltpu.VMEM)
 
 
-def call(kernel, out_shape, n_in, name, scratch=()):
+def call(kernel, out_shape, n_in, scratch=()):
     return pl.pallas_call(
         kernel,
         out_shape=out_shape,
         in_specs=[pl.BlockSpec(memory_space=pltpu.VMEM)] * n_in,
         out_specs=jax.tree.map(lambda _: pl.BlockSpec(memory_space=pltpu.VMEM), out_shape),
         scratch_shapes=list(scratch),
-        name=name,
     )
 
 
-def body(innovations, station_columns, profile_counts, land_mask, vertical_coef, inverse_x, inverse_y):
+def inner(innovations, station_columns, profile_counts, land_mask, vertical_coef, inverse_x, inverse_y):
     everyone = ("gx", "gy")
     vmem = pl.BlockSpec(memory_space=pltpu.VMEM)
     message, codes = pl.pallas_call(
@@ -254,23 +359,61 @@
     )(innovations, station_columns, profile_counts, land_mask)
     got = lax.all_to_all(message, everyone, split_axis=0, concat_axis=0, tiled=True)
     mine = lax.axis_index("gy").astype(I32)
-    where = jnp.stack([mine * SHARE // LEV, mine])
-    products = smooth_call(where, in_vmem(got), inverse_x, inverse_y)
-    parts = [
-        lax.ppermute(product, "gy", [(i, i ^ k) for i in range(N_GY)]) if k else product
-        for product, k in zip(products, ORDER)
-    ]
+    where = jnp.stack([mine * SHARE // LEV, mine, lax.axis_index("gx").astype(I32)])
+    smem = pl.BlockSpec(memory_space=pltpu.SMEM)
+
+    def exchange(parts):
+        moved = []
+        for part, k in zip(parts, ORDER):
+            if k:
+                part = lax.ppermute(part, "gy", [(i, i ^ k) for i in range(N_GY)])
+            moved.append(in_vmem(part))
+        return moved
+
+    station_coefs = exchange(
+        pl.pallas_call(
+            gather_kernel,
+            out_shape=[pltpu.VMEM((LEV, DEV), F32)] * N_GY,
+            in_specs=[smem, vmem, vmem],
+            out_specs=[vmem] * N_GY,
+            scratch_shapes=[pltpu.VMEM((N_GY, LEV, DEV), F32)],
+            name="gather",
+        )(where, vertical_coef, in_vmem(codes)),
+    )
+    line = pltpu.VMEM((LEV, SLOTS), F32)
+    station_lines = pl.pallas_call(
+        station_coef_kernel,
+        out_shape=[line] * 3,
+        in_specs=[smem] + [vmem] * N_GY,
+        out_specs=[vmem] * 3,
+        scratch_shapes=[pltpu.VMEM((N_GY, LEV, DEV), F32), pltpu.VMEM((LEV, SLOTS), F32)],
+        name="station_coef",
+    )(where, *station_coefs)
+    product = smooth_call(where, in_vmem(got), inverse_x, inverse_y)
+    parts = exchange(product)
     plane = pltpu.VMEM((LEV, CY, CX), F32)
-    inv, gain, ratio = call(coef_kernel, (plane, plane, plane), 1, "coef")(vertical_coef)
-    increment, picked = pl.pallas_call(
+    planes = call(coef_kernel, (plane, plane, plane), 1)(vertical_coef)
+    picked = pl.pallas_call(
+        station_kernel,
+        out_shape=pltpu.VMEM((N_GX, N_GX, DEV), BF),
+        in_specs=[smem] + [vmem] * (N_GY + 3),
+        out_specs=vmem,
+        scratch_shapes=[
+            pltpu.VMEM((LAYERS, SLOTS), F32),
+            pltpu.VMEM((LAYERS, SLOTS), F32),
+            pltpu.VMEM((SLOTS, DEV), F32),
+        ],
+        name="station",
+    )(where, *parts, *[in_vmem(x) for x in station_lines])
+    returned = lax.all_to_all(picked, "gx", split_axis=0, concat_axis=0, tiled=True)
+    increment = pl.pallas_call(
         solve_kernel,
-        out_shape=(pltpu.VMEM((LAYERS, CY, CX), BF), pltpu.VMEM((DEV, 2, DEV), BF)),
-        in_specs=[pl.BlockSpec(memory_space=pltpu.SMEM)] + [vmem] * (N_GY + 5),
-        out_specs=(vmem, vmem),
+        out_shape=pltpu.VMEM((LAYERS, CY, CX), BF),
+        in_specs=[smem] + [vmem] * (N_GY + 4) + [pl.BlockSpec(memory_space=pl.ANY)],
+        out_specs=vmem,
         scratch_shapes=[pltpu.VMEM((LAYERS, CY, CX), BF), pltpu.VMEM((LAYERS, CY, CX), F32)],
         name="solve",
-    )(where, *[in_vmem(p) for p in parts], in_vmem(inv), in_vmem(gain), in_vmem(ratio), land_mask, in_vmem(codes))
-    returned = lax.all_to_all(picked, everyone, split_axis=0, concat_axis=0, tiled=True)
+    )(where, *parts, *[in_vmem(x) for x in planes], land_mask, picked)
     returned = returned.reshape(SLOTS, LAYERS).T.reshape(1, LAYERS, SLOTS)
     slot_index = lax.broadcasted_iota(I32, (DEV, CAP), 1)
     live = (slot_index < profile_counts[0][:, None]).reshape(SLOTS)
@@ -289,4 +432,4 @@
         P(),
     )
     out_specs = (P(None, "gy", "gx"), P(("gx", "gy"), None, None))
-    return jax.shard_map(body, mesh=mesh, in_specs=in_specs, out_specs=out_specs, check_vma=False)
+    return jax.shard_map(inner, mesh=mesh, in_specs=in_specs, out_specs=out_specs, check_vma=False)

time: 75.6 us -> 84.5 us (1.12)
  starting transfers between devices: 24.8 us -> 30.5 us
  Pallas kernels: 16.1 us -> 20.2 us
  waiting for transfers between devices: 31 us -> 29.5 us
    ppermute x7 -> x14, starting transfers between devices: 9.33 us -> 15.5 us  [exchange(): part = lax.ppermute(part, 'gy', [(i, i ^ k) for i in range(N_GY)])]
    all_to_all x2, waiting for transfers between devices: 29.5 us -> 24 us  [the longest x1 20.9 us: inner(): lax.all_to_all(message, everyone, split_axis=0, concat_axis=0, tiled=True)]
    pallas_call x4 -> x7, Pallas kernels: 16.1 us -> 20.2 us  [the longest x1 10.7 us: smooth_call(): pl.pallas_call(smooth_kernel, out_shape=[pltpu.VMEM((SHARE + 1, CY, CX),...]
    ppermute x7 -> x14, waiting for transfers between devices: 1.5 us -> 5.56 us  [exchange(): part = lax.ppermute(part, 'gy', [(i, i ^ k) for i in range(N_GY)])]
  transfers between devices with their start and end apart: 9 -> 16, of which waited for: 3 -> 7; matrix products, arithmetic and copies ran while one was open for 2% -> 2% of each run, Pallas kernels for 2% -> 6%
where the time goes in v5:
time: 84.5 us; the launch traced here: 83.6 us
  starting transfers between devices  30.5 us (36%)
  waiting for transfers between devices  29.5 us (35%)
  Pallas kernels  20.2 us (24%)
  local copies, waits for them, and re-layouts  1.74 us (2%)
    all_to_all x1, waiting for transfers between devices, inner(): lax.all_to_all(message, everyone, split_axis=0, concat_axis=0, tiled=True)  20.9 us
    ppermute x14, starting transfers between devices, exchange(): part = lax.ppermute(part, 'gy', [(i, i ^ k) for i in range(N_GY)])  15.5 us
    all_to_all x1, starting transfers between devices, inner(): lax.all_to_all(message, everyone, split_axis=0, concat_axis=0, tiled=True)  11.5 us
    pallas_call x1, Pallas kernels, smooth_call(): pl.pallas_call(smooth_kernel, out_shape=[pltpu.VMEM((SHARE + 1, CY, CX),...  10.7 us
    ppermute x14, waiting for transfers between devices, exchange(): part = lax.ppermute(part, 'gy', [(i, i ^ k) for i in range(N_GY)])  5.56 us
    all_to_all x1, starting transfers between devices, inner(): lax.all_to_all(picked, 'gx', split_axis=0, concat_axis=0, tiled=True)  3.5 us
    all_to_all x1, waiting for transfers between devices, inner(): lax.all_to_all(picked, 'gx', split_axis=0, concat_axis=0, tiled=True)  3.07 us
    pallas_call x1, Pallas kernels, inner(): pl.pallas_call(send_kernel, out_shape=(jax.ShapeDtypeStruct((DEV, ROWS, D...  2.44 us
  transfers between devices with their start and end apart: 16, of which 7 were waited for; matrix products, arithmetic and copies ran while one was open for 2% of the time, Pallas kernels for 6%

profile of v5, /device:TPU:1, one launch (start us, length us, event | category | flops | bytes accessed | tf_op | source)
XLA Modules:
  0.0 83.6 jit_solution(15138014078339824636)
XLA Ops:
  0.6 2.4 %send.1 = (bf16[128,40,128]{2,1,0:T(8,128)(2,1)}, f32[8,128]{1,0:T(8,128)S(1)}) custom-call(bf16[1,64,512]{2,1,0:T(8,128)(2,1)} %inn_ref.1, s32[1,512]{1,0:T(1,128)} %col_ref.1, s32[1,128]{1,0:T(1,128)} %cnt_ref.1, s32[16,256]{1,0:T(8,128)} %refs_11_.1), custom_call_target="tpu_custom_call" | custom-call | tf_op jit(solution)/shard_map/send/pallas_call | solution.py:352
  3.1 11.5 %all-to-all-start = ((bf16[128,40,128]{2,1,0:T(8,128)(2,1)}), bf16[128,40,128]{2,1,0:T(8,128)(2,1)S(1)}, u32[]{:S(2)}, u32[]{:S(2)}) async-start(bf16[128,40,128]{2,1,0:T(8,128)(2,1)} %get-tuple-element.26), calls=%async_computation | async-start | bytes 2621440 | tf_op jit(solution)/shard_map/all_to_all | solution.py:360
  14.6 0.6 pad_add_fusion.tracer_ref.where_ref
  15.2 20.9 %all-to-all-done.got_ref = bf16[128,40,128]{2,1,0:T(8,128)(2,1)S(1)} async-done(((bf16[128,40,128]{2,1,0:T(8,128)(2,1)}), bf16[128,40,128]{2,1,0:T(8,128)(2,1)S(1)}, u32[]{:S(2)}, u32[]{:S(2)}) %all-to-all-start) | async-done | bytes 1310752 | tf_op jit(solution)/shard_map/all_to_all | solution.py:360
  36.1 10.7 %smooth.1 = (bf16[9,16,256]{2,1,0:T(8,128)(2,1)S(1)}, bf16[9,16,256]{2,1,0:T(8,128)(2,1)S(1)}, bf16[9,16,256]{2,1,0:T(8,128)(2,1)S(1)}, bf16[9,16,256]{2,1,0:T(8...) custom-call(s32[3]{0:T(128)} %pad_add_fusion.tracer_ref.where_ref, ...), custom_call_target="tpu_custom_call" | custom-call | tf_op jit(solution)/shard_map/smooth/pallas_call | solution.py:182
  46.8 0.0 copy-start
  46.8 0.8 collective-permute-start
  47.6 3.9 %collective-permute-start.1 = (bf16[9,16,256]{2,1,0:T(8,128)(2,1)S(1)}, bf16[9,16,256]{2,1,0:T(8,128)(2,1)S(1)}, u32[]{:S(2)}, u32[]{:S(2)}) collective-permute-start(bf16[9,16,256]{2,1,0:T(8,128)(2,1)S(1)} %get-tuple-element.28), channel_id=1, source_target_pairs={{0,5},{1,4},{2,7},{3,6},{4,1},{5,0},{6,3},{7,2},{8,13},{9,12},{10,... | collective-permute-start | bytes 221192 | tf_op jit(solution)/shard_map/ppermute | solution.py:369
  51.5 2.0 %gather.1 = (f32[32,128]{1,0:T(8,128)S(1)}, f32[32,128]{1,0:T(8,128)S(1)}, f32[32,128]{1,0:T(8,128)S(1)}, f32[32,128]{1,0:T(8,128)S(1)}, f32[32,128]{1,0:T(8,128...) custom-call(s32[3]{0:T(128)} %pad_add_fusion.tracer_ref.where_ref, ...), custom_call_target="tpu_custom_call" | custom-call | tf_op jit(solution)/shard_map/gather/pallas_call | solution.py:374
  53.5 0.2 collective-permute-start.7
  53.7 1.8 %collective-permute-start.8 = (f32[32,128]{1,0:T(8,128)S(1)}, f32[32,128]{1,0:T(8,128)S(1)}, u32[]{:S(2)}, u32[]{:S(2)}) collective-permute-start(f32[32,128]{1,0:T(8,128)S(1)} %get-tuple-element.40), channel_id=1, source_target_pairs={{0,5},{1,4},{2,7},{3,6},{4,1},{5,0},{6,3},{7,2},{8,13},{9,12},{10,... | collective-permute-start | bytes 49160 | tf_op jit(solution)/shard_map/ppermute | solution.py:369
  55.5 0.8 %collective-permute-start.9 = (f32[32,128]{1,0:T(8,128)S(1)}, f32[32,128]{1,0:T(8,128)S(1)}, u32[]{:S(2)}, u32[]{:S(2)}) collective-permute-start(f32[32,128]{1,0:T(8,128)S(1)} %get-tuple-element.41), channel_id=1, source_target_pairs={{0,6},{1,7},{2,4},{3,5},{4,2},{5,3},{6,0},{7,1},{8,14},{9,15},{10,... | collective-permute-start | bytes 49160 | tf_op jit(solution)/shard_map/ppermute | solution.py:369
  56.4 1.3 %collective-permute-done.7.refs_0_ = f32[32,128]{1,0:T(8,128)S(1)} collective-permute-done((f32[32,128]{1,0:T(8,128)S(1)}, f32[32,128]{1,0:T(8,128)S(1)}, u32[]{:S(2)}, u32[]{:S(2)}) %collective-permute-start.7) | collective-permute-done | bytes 16416 | tf_op jit(solution)/shard_map/ppermute | solution.py:369
  57.7 2.1 %collective-permute-start.10 = (f32[32,128]{1,0:T(8,128)S(1)}, f32[32,128]{1,0:T(8,128)S(1)}, u32[]{:S(2)}, u32[]{:S(2)}) collective-permute-start(f32[32,128]{1,0:T(8,128)S(1)} %get-tuple-element.42), channel_id=1, source_target_pairs={{0,7},{1,6},{2,5},{3,4},{4,3},{5,2},{6,1},{7,0},{8,15},{9,14},{10,... | collective-permute-start | bytes 49160 | tf_op jit(solution)/shard_map/ppermute | solution.py:369
  59.8 0.0 collective-permute-done.8.refs_1_
  59.8 0.0 collective-permute-start.11
  59.8 0.0 collective-permute-done.9.refs_2_
  59.8 1.0 %collective-permute-start.12 = (f32[32,128]{1,0:T(8,128)S(1)}, f32[32,128]{1,0:T(8,128)S(1)}, u32[]{:S(2)}, u32[]{:S(2)}) collective-permute-start(f32[32,128]{1,0:T(8,128)S(1)} %get-tuple-element.44), channel_id=1, source_target_pairs={{0,3},{1,2},{2,1},{3,0},{4,7},{5,6},{6,5},{7,4},{8,11},{9,10},{10,... | collective-permute-start | bytes 49160 | tf_op jit(solution)/shard_map/ppermute | solution.py:369
  60.8 1.3 %collective-permute-done.10.refs_3_ = f32[32,128]{1,0:T(8,128)S(1)} collective-permute-done((f32[32,128]{1,0:T(8,128)S(1)}, f32[32,128]{1,0:T(8,128)S(1)}, u32[]{:S(2)}, u32[]{:S(2)}) %collective-permute-start.10) | collective-permute-done | bytes 16416 | tf_op jit(solution)/shard_map/ppermute | solution.py:369
  62.0 0.0 collective-permute-start.13
  62.1 0.3 collective-permute-done.11.refs_4_
  62.4 1.9 %collective-permute-start.2 = (bf16[9,16,256]{2,1,0:T(8,128)(2,1)S(1)}, bf16[9,16,256]{2,1,0:T(8,128)(2,1)S(1)}, u32[]{:S(2)}, u32[]{:S(2)}) collective-permute-start(bf16[9,16,256]{2,1,0:T(8,128)(2,1)S(1)} %get-tuple-element.29), channel_id=1, source_target_pairs={{0,6},{1,7},{2,4},{3,5},{4,2},{5,3},{6,0},{7,1},{8,14},{9,15},{10,... | collective-permute-start | bytes 221192 | tf_op jit(solution)/shard_map/ppermute | solution.py:369
  64.3 0.0 collective-permute-done.12.refs_5_
  64.3 1.1 %collective-permute-start.3 = (bf16[9,16,256]{2,1,0:T(8,128)(2,1)S(1)}, bf16[9,16,256]{2,1,0:T(8,128)(2,1)S(1)}, u32[]{:S(2)}, u32[]{:S(2)}) collective-permute-start(bf16[9,16,256]{2,1,0:T(8,128)(2,1)S(1)} %get-tuple-element.30), channel_id=1, source_target_pairs={{0,7},{1,6},{2,5},{3,4},{4,3},{5,2},{6,1},{7,0},{8,15},{9,14},{10,... | collective-permute-start | bytes 221192 | tf_op jit(solution)/shard_map/ppermute | solution.py:369
  65.4 0.0 collective-permute-done.13.refs_6_
  65.4 0.0 collective-permute-start.4
  65.4 0.0 collective-permute-done.refs_0_
  65.4 1.6 %collective-permute-start.5 = (bf16[9,16,256]{2,1,0:T(8,128)(2,1)S(1)}, bf16[9,16,256]{2,1,0:T(8,128)(2,1)S(1)}, u32[]{:S(2)}, u32[]{:S(2)}) collective-permute-start(bf16[9,16,256]{2,1,0:T(8,128)(2,1)S(1)} %get-tuple-element.32), channel_id=1, source_target_pairs={{0,3},{1,2},{2,1},{3,0},{4,7},{5,6},{6,5},{7,4},{8,11},{9,10},{10,... | collective-permute-start | bytes 221192 | tf_op jit(solution)/shard_map/ppermute | solution.py:369
  67.1 0.0 collective-permute-done.1.refs_1_
  67.1 0.2 collective-permute-start.6
  67.3 1.0 %station_coef.1 = (f32[32,512]{1,0:T(8,128)S(1)}, f32[32,512]{1,0:T(8,128)S(1)}, f32[32,512]{1,0:T(8,128)S(1)}) custom-call(s32[3]{0:T(128)} %pad_add_fusion.tracer_ref.where_ref, f32[32,128]{1,0:T(8,128)S(1)} %collective-permute-done.7.refs_0_, f32[32,128]{1,0:T(8,128)S(1)} %collective-permute-done.8.refs_1_, f32[32,128]{1,0:T(8,128)S(1)} %collective-permute-done.9.refs_2_, ...), custom_call_target="tpu_custom_call" | custom-call | tf_op jit(solution)/shard_map/station_coef/pallas_call | solution.py:384
  68.3 0.0 collective-permute-done.2.refs_2_
  68.3 1.9 %collective-permute-done.3.refs_3_ = bf16[9,16,256]{2,1,0:T(8,128)(2,1)S(1)} collective-permute-done((bf16[9,16,256]{2,1,0:T(8,128)(2,1)S(1)}, bf16[9,16,256]{2,1,0:T(8,128)(2,1)S(1)}, u32[]{:S(2)}, u32[]{:S(2)}) %collective-permute-start.3) | collective-permute-done | bytes 73760 | tf_op jit(solution)/shard_map/ppermute | solution.py:369
  70.2 0.0 collective-permute-done.4.refs_4_
  70.2 0.8 collective-permute-done.5.refs_5_
  71.0 0.0 collective-permute-done.6.refs_6_
  71.0 1.7 %station.1.refs_12_ = bf16[16,16,128]{2,1,0:T(8,128)(2,1)} custom-call(s32[3]{0:T(128)} %pad_add_fusion.tracer_ref.where_ref, bf16[9,16,256]{2,1,0:T(8,128)(2,1)S(1)} %collective-permute-done.refs_0_, bf16[9,16,256]{2,1,0:T(8,128)(2,1)S(1)} %collective-permute-done.1.refs_1_, bf16[9,16,256]{2,1,0:T(8,128)(2,1)S(1)} %collective-permute-done.2.refs_2_, ...), custom_call_target="tpu_custom_call" | custom-call | tf_op jit(solution)/shard_map/station/pallas_call | solution.py:396
  72.7 3.5 %all-to-all-start.1 = ((bf16[16,16,128]{2,1,0:T(8,128)(2,1)}), bf16[16,16,128]{2,1,0:T(8,128)(2,1)S(1)}, u32[]{:S(2)}, u32[]{:S(2)}) async-start(bf16[16,16,128]{2,1,0:T(8,128)(2,1)} %station.1.refs_12_), calls=%async_computation.1 | async-start | bytes 131072 | tf_op jit(solution)/shard_map/all_to_all | solution.py:408
  76.2 0.0 copy-done
  76.2 0.1 iota_compare_fusion
  76.3 1.3 %shard_map.86 = (f32[32,16,256]{2,1,0:T(8,128)S(1)}, f32[32,16,256]{2,1,0:T(8,128)S(1)}, f32[32,16,256]{2,1,0:T(8,128)S(1)}) custom-call(f32[32,16,256]{2,1,0:T(8,128)} %coef_ref.3), custom_call_target="tpu_custom_call" | custom-call | tf_op jit(solution)/shard_map/pallas_call | solution.py:395
  77.6 0.1 lt.20
  77.8 1.0 %solve.1 = bf16[64,16,256]{2,1,0:T(8,128)(2,1)S(1)} custom-call(s32[3]{0:T(128)} %pad_add_fusion.tracer_ref.where_ref, bf16[9,16,256]{2,1,0:T(8,128)(2,1)S(1)} %collective-permute-done.refs_0_, bf16[9,16,256]{2,1,0:T(8,128)(2,1)S(1)} %collective-permute-done.1.refs_1_, bf16[9,16,256]{2,1,0:T(8,128)(2,1)S(1)} %collective-permute-done.2.refs_2_, ...), custom_call_target="tpu_custom_call" | custom-call | tf_op jit(solution)/shard_map/solve/pallas_call | solution.py:409
  78.8 0.8 copy.11
  79.6 3.1 %all-to-all-done.1 = bf16[16,16,128]{2,1,0:T(8,128)(2,1)S(1)} async-done(((bf16[16,16,128]{2,1,0:T(8,128)(2,1)}), bf16[16,16,128]{2,1,0:T(8,128)(2,1)S(1)}, u32[]{:S(2)}, u32[]{:S(2)}) %all-to-all-start.1) | async-done | bytes 65568 | tf_op jit(solution)/shard_map/all_to_all | solution.py:408
  82.7 0.1 reshape.26
  82.8 0.1 select_bitcast_fusion
  82.9 0.7 copy.10
Async XLA Ops:
  3.1 33.0 %all-to-all-start = ((bf16[128,40,128]{2,1,0:T(8,128)(2,1)}), bf16[128,40,128]{2,1,0:T(8,128)(2,1)S(1)}, u32[]{:S(2)}, u32[]{:S(2)}) async-start(bf16[128,40,128]{2,1,0:T(8,128)(2,1)} %get-tuple-element.26), calls=%async_computation | async-start | bytes 2621440 | tf_op jit(solution)/shard_map/all_to_all | solution.py:360
  46.8 29.4 %copy-start = (s32[1,128]{1,0:T(1,128)S(1)}, s32[1,128]{1,0:T(1,128)}, u32[]{:S(2)}) copy-start(s32[1,128]{1,0:T(1,128)} %cnt_ref.1) | copy-start | bytes 1540
  46.8 18.6 %collective-permute-start = (bf16[9,16,256]{2,1,0:T(8,128)(2,1)S(1)}, bf16[9,16,256]{2,1,0:T(8,128)(2,1)S(1)}, u32[]{:S(2)}, u32[]{:S(2)}) collective-permute-start(bf16[9,16,256]{2,1,0:T(8,128)(2,1)S(1)} %get-tuple-element.27), channel_id=1, source_target_pairs={{0,4},{1,5},{2,6},{3,7},{4,0},{5,1},{6,2},{7,3},{8,12},{9,13},{10,... | collective-permute-start | bytes 221192 | tf_op jit(solution)/shard_map/ppermute | solution.py:369
  47.6 19.5 %collective-permute-start.1 = (bf16[9,16,256]{2,1,0:T(8,128)(2,1)S(1)}, bf16[9,16,256]{2,1,0:T(8,128)(2,1)S(1)}, u32[]{:S(2)}, u32[]{:S(2)}) collective-permute-start(bf16[9,16,256]{2,1,0:T(8,128)(2,1)S(1)} %get-tuple-element.28), channel_id=1, source_target_pairs={{0,5},{1,4},{2,7},{3,6},{4,1},{5,0},{6,3},{7,2},{8,13},{9,12},{10,... | collective-permute-start | bytes 221192 | tf_op jit(solution)/shard_map/ppermute | solution.py:369
  53.5 4.2 %collective-permute-start.7 = (f32[32,128]{1,0:T(8,128)S(1)}, f32[32,128]{1,0:T(8,128)S(1)}, u32[]{:S(2)}, u32[]{:S(2)}) collective-permute-start(f32[32,128]{1,0:T(8,128)S(1)} %get-tuple-element.39), channel_id=1, source_target_pairs={{0,4},{1,5},{2,6},{3,7},{4,0},{5,1},{6,2},{7,3},{8,12},{9,13},{10,... | collective-permute-start | bytes 49160 | tf_op jit(solution)/shard_map/ppermute | solution.py:369
  53.7 6.1 %collective-permute-start.8 = (f32[32,128]{1,0:T(8,128)S(1)}, f32[32,128]{1,0:T(8,128)S(1)}, u32[]{:S(2)}, u32[]{:S(2)}) collective-permute-start(f32[32,128]{1,0:T(8,128)S(1)} %get-tuple-element.40), channel_id=1, source_target_pairs={{0,5},{1,4},{2,7},{3,6},{4,1},{5,0},{6,3},{7,2},{8,13},{9,12},{10,... | collective-permute-start | bytes 49160 | tf_op jit(solution)/shard_map/ppermute | solution.py:369
  55.5 4.3 %collective-permute-start.9 = (f32[32,128]{1,0:T(8,128)S(1)}, f32[32,128]{1,0:T(8,128)S(1)}, u32[]{:S(2)}, u32[]{:S(2)}) collective-permute-start(f32[32,128]{1,0:T(8,128)S(1)} %get-tuple-element.41), channel_id=1, source_target_pairs={{0,6},{1,7},{2,4},{3,5},{4,2},{5,3},{6,0},{7,1},{8,14},{9,15},{10,... | collective-permute-start | bytes 49160 | tf_op jit(solution)/shard_map/ppermute | solution.py:369
  57.7 4.4 %collective-permute-start.10 = (f32[32,128]{1,0:T(8,128)S(1)}, f32[32,128]{1,0:T(8,128)S(1)}, u32[]{:S(2)}, u32[]{:S(2)}) collective-permute-start(f32[32,128]{1,0:T(8,128)S(1)} %get-tuple-element.42), channel_id=1, source_target_pairs={{0,7},{1,6},{2,5},{3,4},{4,3},{5,2},{6,1},{7,0},{8,15},{9,14},{10,... | collective-permute-start | bytes 49160 | tf_op jit(solution)/shard_map/ppermute | solution.py:369
  59.8 2.6 %collective-permute-start.11 = (f32[32,128]{1,0:T(8,128)S(1)}, f32[32,128]{1,0:T(8,128)S(1)}, u32[]{:S(2)}, u32[]{:S(2)}) collective-permute-start(f32[32,128]{1,0:T(8,128)S(1)} %get-tuple-element.43), channel_id=1, source_target_pairs={{0,2},{1,3},{2,0},{3,1},{4,6},{5,7},{6,4},{7,5},{8,10},{9,11},{10,... | collective-permute-start | bytes 49160 | tf_op jit(solution)/shard_map/ppermute | solution.py:369
  59.8 4.5 %collective-permute-start.12 = (f32[32,128]{1,0:T(8,128)S(1)}, f32[32,128]{1,0:T(8,128)S(1)}, u32[]{:S(2)}, u32[]{:S(2)}) collective-permute-start(f32[32,128]{1,0:T(8,128)S(1)} %get-tuple-element.44), channel_id=1, source_target_pairs={{0,3},{1,2},{2,1},{3,0},{4,7},{5,6},{6,5},{7,4},{8,11},{9,10},{10,... | collective-permute-start | bytes 49160 | tf_op jit(solution)/shard_map/ppermute | solution.py:369
  62.0 3.4 %collective-permute-start.13 = (f32[32,128]{1,0:T(8,128)S(1)}, f32[32,128]{1,0:T(8,128)S(1)}, u32[]{:S(2)}, u32[]{:S(2)}) collective-permute-start(f32[32,128]{1,0:T(8,128)S(1)} %get-tuple-element.45), channel_id=1, source_target_pairs={{0,1},{1,0},{2,3},{3,2},{4,5},{5,4},{6,7},{7,6},{8,9},{9,8},{10,11... | collective-permute-start | bytes 49160 | tf_op jit(solution)/shard_map/ppermute | solution.py:369
  62.4 5.9 %collective-permute-start.2 = (bf16[9,16,256]{2,1,0:T(8,128)(2,1)S(1)}, bf16[9,16,256]{2,1,0:T(8,128)(2,1)S(1)}, u32[]{:S(2)}, u32[]{:S(2)}) collective-permute-start(bf16[9,16,256]{2,1,0:T(8,128)(2,1)S(1)} %get-tuple-element.29), channel_id=1, source_target_pairs={{0,6},{1,7},{2,4},{3,5},{4,2},{5,3},{6,0},{7,1},{8,14},{9,15},{10,... | collective-permute-start | bytes 221192 | tf_op jit(solution)/shard_map/ppermute | solution.py:369
  64.3 5.9 %collective-permute-start.3 = (bf16[9,16,256]{2,1,0:T(8,128)(2,1)S(1)}, bf16[9,16,256]{2,1,0:T(8,128)(2,1)S(1)}, u32[]{:S(2)}, u32[]{:S(2)}) collective-permute-start(bf16[9,16,256]{2,1,0:T(8,128)(2,1)S(1)} %get-tuple-element.30), channel_id=1, source_target_pairs={{0,7},{1,6},{2,5},{3,4},{4,3},{5,2},{6,1},{7,0},{8,15},{9,14},{10,... | collective-permute-start | bytes 221192 | tf_op jit(solution)/shard_map/ppermute | solution.py:369
  65.4 4.8 %collective-permute-start.4 = (bf16[9,16,256]{2,1,0:T(8,128)(2,1)S(1)}, bf16[9,16,256]{2,1,0:T(8,128)(2,1)S(1)}, u32[]{:S(2)}, u32[]{:S(2)}) collective-permute-start(bf16[9,16,256]{2,1,0:T(8,128)(2,1)S(1)} %get-tuple-element.31), channel_id=1, source_target_pairs={{0,2},{1,3},{2,0},{3,1},{4,6},{5,7},{6,4},{7,5},{8,10},{9,11},{10,... | collective-permute-start | bytes 221192 | tf_op jit(solution)/shard_map/ppermute | solution.py:369
  65.4 5.5 %collective-permute-start.5 = (bf16[9,16,256]{2,1,0:T(8,128)(2,1)S(1)}, bf16[9,16,256]{2,1,0:T(8,128)(2,1)S(1)}, u32[]{:S(2)}, u32[]{:S(2)}) collective-permute-start(bf16[9,16,256]{2,1,0:T(8,128)(2,1)S(1)} %get-tuple-element.32), channel_id=1, source_target_pairs={{0,3},{1,2},{2,1},{3,0},{4,7},{5,6},{6,5},{7,4},{8,11},{9,10},{10,... | collective-permute-start | bytes 221192 | tf_op jit(solution)/shard_map/ppermute | solution.py:369
  67.1 3.9 %collective-permute-start.6 = (bf16[9,16,256]{2,1,0:T(8,128)(2,1)S(1)}, bf16[9,16,256]{2,1,0:T(8,128)(2,1)S(1)}, u32[]{:S(2)}, u32[]{:S(2)}) collective-permute-start(bf16[9,16,256]{2,1,0:T(8,128)(2,1)S(1)} %get-tuple-element.33), channel_id=1, source_target_pairs={{0,1},{1,0},{2,3},{3,2},{4,5},{5,4},{6,7},{7,6},{8,9},{9,8},{10,11... | collective-permute-start | bytes 221192 | tf_op jit(solution)/shard_map/ppermute | solution.py:369
  72.7 10.0 %all-to-all-start.1 = ((bf16[16,16,128]{2,1,0:T(8,128)(2,1)}), bf16[16,16,128]{2,1,0:T(8,128)(2,1)S(1)}, u32[]{:S(2)}, u32[]{:S(2)}) async-start(bf16[16,16,128]{2,1,0:T(8,128)(2,1)} %station.1.refs_12_), calls=%async_computation.1 | async-start | bytes 131072 | tf_op jit(solution)/shard_map/all_to_all | solution.py:408

commit v6 on v5

--- a/solution.py
+++ b/solution.py
@@ -36,22 +36,22 @@
 
 
 def by_source():
-    source = iota((SLOTS, SLOTS), 0)
-    owner = source % DEV
-    lane = (owner % N_GY) * 64 + (source // DEV) * N_GX + owner // N_GY
-    return one_hot(lane == iota((SLOTS, SLOTS), 1))
+    source = iota((SLOTS, DEV), 0)
+    lane = (source & 7) * 64 + (source >> 7) * N_GX + ((source >> 3) & 15)
+    target = iota((SLOTS, DEV), 1)
+    return jnp.concatenate([one_hot(lane - t * DEV == target) for t in range(CAP)], axis=1)
 
 
 def send_kernel(inn_ref, col_ref, cnt_ref, mask_ref, out_ref, code_ref, message_ref, sems):
     counts = jnp.broadcast_to(cnt_ref[...], (8, DEV)).astype(F32).astype(BF)
-    spread = one_hot(iota((DEV, SLOTS), 1) // CAP == iota((DEV, SLOTS), 0))
+    spread = one_hot(iota((DEV, SLOTS), 1) >> 2 == iota((DEV, SLOTS), 0))
     count_lane = dot(counts, spread)[0:1, :]
-    slot_lane = (iota((1, SLOTS), 1) % CAP).astype(F32)
+    slot_lane = (iota((1, SLOTS), 1) & 3).astype(F32)
     live = slot_lane < count_lane
     values = jnp.where(live, inn_ref[0].astype(F32), 0.0).astype(BF)
     cells = col_ref[...]
-    row = cells // CX
-    col = cells % CX
+    row = cells >> 8
+    col = cells & 255
     pick_col = one_hot(iota((CX, SLOTS), 0) == col)
     sea_rows = dot(mask_ref[...].astype(F32).astype(BF), pick_col)
     sea = jnp.sum(jnp.where(iota((CY, SLOTS), 0) == row, sea_rows, 0.0), axis=0, keepdims=True)
@@ -61,9 +61,10 @@
         jnp.broadcast_to(row_code, (8, SLOTS)),
         jnp.broadcast_to(col.astype(F32), (8, SLOTS)),
     ).astype(BF)
-    source = iota((SLOTS, SLOTS), 0)
-    target = iota((SLOTS, SLOTS), 1)
-    permute = one_hot((source % CAP) * DEV + source // CAP == target)
+    source = iota((SLOTS, DEV), 0)
+    lane = (source & 3) * DEV + (source >> 2)
+    target = iota((SLOTS, DEV), 1)
+    permute = jnp.concatenate([one_hot(lane - t * DEV == target) for t in range(CAP)], axis=1)
     moved = dot(codes, permute)
     tile = jnp.concatenate(
         [moved[0:1, c * DEV : (c + 1) * DEV] for c in range(CAP)]
@@ -87,11 +88,12 @@
 
 
 def smooth_kernel(
-    tracer_ref, got_ref, kx_ref, ky_ref, *refs
+    got_ref, kx_ref, ky_ref, *refs
 ):
+    tracer = lax.axis_index("gy") * SHARE // LEV
     out_refs = refs[:N_GY]
     wide_ref, turned_ref, column_ref, dense_ref, acc_ref, along_ref, station_ref, kx_vmem, sem = refs[N_GY:]
-    fetch = pltpu.make_async_copy(kx_ref.at[tracer_ref[0]], kx_vmem, sem)
+    fetch = pltpu.make_async_copy(kx_ref.at[tracer], kx_vmem, sem)
     fetch.start()
     acc_ref[...] = jnp.zeros_like(acc_ref)
 
@@ -145,11 +147,11 @@
         along_x = jnp.concatenate(
             [acc_ref[pl.ds(h * 1024 + l, NY, stride=SHARE), :] for h in range(2)], axis=1
         ).astype(BF)
-        along_y = dot(ky_ref[tracer_ref[0]], along_x, ((0,), (0,))).astype(BF)
+        along_y = dot(ky_ref[tracer], along_x, ((0,), (0,))).astype(BF)
         along_ref[l] = along_y
         for h in range(2):
             acc_ref[pl.ds(h * 1024 + l, NY, stride=SHARE), :] = along_y[:, h * 128 : (h + 1) * 128].astype(F32)
-    own = [got_ref[tracer_ref[2] * N_GY + b, 32:40, :].astype(F32) for b in range(N_GY)]
+    own = [got_ref[lax.axis_index("gx") * N_GY + b, 32:40, :].astype(F32) for b in range(N_GY)]
     lines = [jnp.concatenate([x[c : c + 1, :] for c in range(CAP)], axis=1) for x in own]
     lines += [jnp.concatenate([x[CAP + c : CAP + c + 1, :] for c in range(CAP)], axis=1) for x in own]
     moved = dot(jnp.concatenate(lines, axis=0).astype(BF), by_source())
@@ -170,20 +172,19 @@
     for g in range(N_GY):
         line = jnp.concatenate([x[:, g * 64 : (g + 1) * 64] for x in found], axis=1)
         station_ref[g] = jnp.concatenate([line[:, :CX], line[:, CX:]], axis=0).astype(BF)
-    mine = tracer_ref[1]
+    mine = lax.axis_index("gy")
     for out_ref, k in zip(out_refs, ORDER):
         row = pl.multiple_of((mine ^ k) * CY, CY)
         out_ref[0:SHARE] = along_ref[:, pl.ds(row, CY), :]
         out_ref[SHARE] = station_ref[mine ^ k]
 
 
-def smooth_call(tracer, got, inverse_x, inverse_y):
+def smooth_call(got, inverse_x, inverse_y):
     vmem = pl.BlockSpec(memory_space=pltpu.VMEM)
     return pl.pallas_call(
         smooth_kernel,
         out_shape=[pltpu.VMEM((SHARE + 1, CY, CX), BF)] * N_GY,
         in_specs=[
-            pl.BlockSpec(memory_space=pltpu.SMEM),
             vmem,
             pl.BlockSpec(memory_space=pl.ANY),
             vmem,
@@ -201,7 +202,7 @@
             pltpu.SemaphoreType.DMA(()),
         ],
         name="smooth",
-    )(tracer, got, inverse_x, inverse_y)
+    )(got, inverse_x, inverse_y)
 
 
 def coef_kernel(coef_ref, inv_ref, gain_ref, ratio_ref):
@@ -219,10 +220,10 @@
         ratio_ref[k] = ratio
 
 
-def solve_kernel(where_ref, *refs):
+def solve_kernel(*refs):
     parts = refs[:N_GY]
     inv_ref, gain_ref, ratio_ref, mask_ref, _, inc_ref, field_ref, part_ref = refs[N_GY:]
-    mine = where_ref[1]
+    mine = lax.axis_index("gy")
     for part, k in zip(parts, ORDER):
         field_ref[pl.ds((mine ^ k) * SHARE, SHARE)] = part[0:SHARE]
     mask = mask_ref[...].astype(F32)
@@ -246,7 +247,7 @@
         inc_ref[LEV + k] = (x1 * mask).astype(BF)
 
 
-def gather_kernel(where_ref, coef_ref, code_ref, *refs):
+def gather_kernel(coef_ref, code_ref, *refs):
     out_refs = refs[:N_GY]
     found_ref = refs[N_GY]
     codes = code_ref[...]
@@ -266,14 +267,14 @@
         tile = lines[:, (g // 2) * DEV : (g // 2 + 1) * DEV]
         found_ref[g] = pltpu.roll(tile, 64, 1) if g % 2 else tile
     for out_ref, k in zip(out_refs, ORDER):
-        out_ref[...] = found_ref[where_ref[1] ^ k]
-
-
-def station_coef_kernel(where_ref, *refs):
+        out_ref[...] = found_ref[lax.axis_index("gy") ^ k]
+
+
+def station_coef_kernel(*refs):
     parts = refs[:N_GY]
     inv_ref, gain_ref, ratio_ref, stage_ref, coef_ref = refs[N_GY:]
     for part, k in zip(parts, ORDER):
-        stage_ref[where_ref[1] ^ k] = part[...]
+        stage_ref[lax.axis_index("gy") ^ k] = part[...]
     low = iota((LEV, DEV), 1) < 64
     for t in range(CAP):
         coef_ref[:, t * DEV : (t + 1) * DEV] = jnp.where(
@@ -293,11 +294,11 @@
         ratio_ref[k : k + 1, :] = ratio
 
 
-def station_kernel(where_ref, *refs):
+def station_kernel(*refs):
     parts = refs[:N_GY]
     inv_ref, gain_ref, ratio_ref, out_ref, field_ref, part_ref, turned_ref = refs[N_GY:]
     for part, k in zip(parts, ORDER):
-        start = pl.multiple_of((where_ref[1] ^ k) * SHARE, SHARE)
+        start = pl.multiple_of((lax.axis_index("gy") ^ k) * SHARE, SHARE)
         both = part[SHARE].astype(F32)
         field_ref[pl.ds(start, SHARE), 0:CX] = both[0:SHARE]
         field_ref[pl.ds(start, SHARE), CX:SLOTS] = both[SHARE:CY]
@@ -358,9 +359,6 @@
         name="send",
     )(innovations, station_columns, profile_counts, land_mask)
     got = lax.all_to_all(message, everyone, split_axis=0, concat_axis=0, tiled=True)
-    mine = lax.axis_index("gy").astype(I32)
-    where = jnp.stack([mine * SHARE // LEV, mine, lax.axis_index("gx").astype(I32)])
-    smem = pl.BlockSpec(memory_space=pltpu.SMEM)
 
     def exchange(parts):
         moved = []
@@ -374,29 +372,29 @@
         pl.pallas_call(
             gather_kernel,
             out_shape=[pltpu.VMEM((LEV, DEV), F32)] * N_GY,
-            in_specs=[smem, vmem, vmem],
+            in_specs=[vmem, vmem],
             out_specs=[vmem] * N_GY,
             scratch_shapes=[pltpu.VMEM((N_GY, LEV, DEV), F32)],
             name="gather",
-        )(where, vertical_coef, in_vmem(codes)),
+        )(vertical_coef, in_vmem(codes)),
     )
     line = pltpu.VMEM((LEV, SLOTS), F32)
     station_lines = pl.pallas_call(
         station_coef_kernel,
         out_shape=[line] * 3,
-        in_specs=[smem] + [vmem] * N_GY,
+        in_specs=[vmem] * N_GY,
         out_specs=[vmem] * 3,
         scratch_shapes=[pltpu.VMEM((N_GY, LEV, DEV), F32), pltpu.VMEM((LEV, SLOTS), F32)],
         name="station_coef",
-    )(where, *station_coefs)
-    product = smooth_call(where, in_vmem(got), inverse_x, inverse_y)
+    )(*station_coefs)
+    product = smooth_call(in_vmem(got), inverse_x, inverse_y)
     parts = exchange(product)
     plane = pltpu.VMEM((LEV, CY, CX), F32)
     planes = call(coef_kernel, (plane, plane, plane), 1)(vertical_coef)
     picked = pl.pallas_call(
         station_kernel,
         out_shape=pltpu.VMEM((N_GX, N_GX, DEV), BF),
-        in_specs=[smem] + [vmem] * (N_GY + 3),
+        in_specs=[vmem] * (N_GY + 3),
         out_specs=vmem,
         scratch_shapes=[
             pltpu.VMEM((LAYERS, SLOTS), F32),
@@ -404,16 +402,16 @@
             pltpu.VMEM((SLOTS, DEV), F32),
         ],
         name="station",
-    )(where, *parts, *[in_vmem(x) for x in station_lines])
+    )(*parts, *[in_vmem(x) for x in station_lines])
     returned = lax.all_to_all(picked, "gx", split_axis=0, concat_axis=0, tiled=True)
     increment = pl.pallas_call(
         solve_kernel,
         out_shape=pltpu.VMEM((LAYERS, CY, CX), BF),
-        in_specs=[smem] + [vmem] * (N_GY + 4) + [pl.BlockSpec(memory_space=pl.ANY)],
+        in_specs=[vmem] * (N_GY + 4) + [pl.BlockSpec(memory_space=pl.ANY)],
         out_specs=vmem,
         scratch_shapes=[pltpu.VMEM((LAYERS, CY, CX), BF), pltpu.VMEM((LAYERS, CY, CX), F32)],
         name="solve",
-    )(where, *parts, *[in_vmem(x) for x in planes], land_mask, picked)
+    )(*parts, *[in_vmem(x) for x in planes], land_mask, picked)
     returned = returned.reshape(SLOTS, LAYERS).T.reshape(1, LAYERS, SLOTS)
     slot_index = lax.broadcasted_iota(I32, (DEV, CAP), 1)
     live = (slot_index < profile_counts[0][:, None]).reshape(SLOTS)

time: 84.5 us -> 83.9 us (level)
  blocking collectives: 0 us -> 33.1 us
  waiting for transfers between devices: 29.5 us -> 9.29 us
  starting transfers between devices: 30.5 us -> 19 us
  Pallas kernels: 20.2 us -> 19 us
    all_to_all x0 -> x1, blocking collectives: none -> 33.1 us  [inner(): lax.all_to_all(message, everyone, split_axis=0, concat_axis=0, tiled=True)]
    all_to_all x1 -> x0, waiting for transfers between devices: 20.9 us -> none  [inner(): lax.all_to_all(message, everyone, split_axis=0, concat_axis=0, tiled=True)]
    all_to_all x1 -> x0, starting transfers between devices: 11.5 us -> none  [inner(): lax.all_to_all(message, everyone, split_axis=0, concat_axis=0, tiled=True)]
  transfers between devices with their start and end apart: 16 -> 15, of which waited for: 7 -> 6; matrix products, arithmetic and copies ran while one was open for 2% -> 1% of each run, Pallas kernels for 6% -> 6%
where the time goes in v6:
time: 83.9 us; the launch traced here: 83 us
  blocking collectives  33.1 us (39%)
  Pallas kernels  19 us (23%)
  starting transfers between devices  19 us (23%)
  waiting for transfers between devices  9.29 us (11%)
  local copies, waits for them, and re-layouts  1.74 us (2%)
    all_to_all x1, blocking collectives, inner(): lax.all_to_all(message, everyone, split_axis=0, concat_axis=0, tiled=True)  33.1 us
    ppermute x14, starting transfers between devices, exchange(): part = lax.ppermute(part, 'gy', [(i, i ^ k) for i in range(N_GY)])  15.5 us
    pallas_call x1, Pallas kernels, smooth_call(): pl.pallas_call(smooth_kernel, out_shape=[pltpu.VMEM((SHARE + 1, CY, CX),...  10.7 us
    ppermute x14, waiting for transfers between devices, exchange(): part = lax.ppermute(part, 'gy', [(i, i ^ k) for i in range(N_GY)])  6.25 us
    all_to_all x1, starting transfers between devices, inner(): lax.all_to_all(picked, 'gx', split_axis=0, concat_axis=0, tiled=True)  3.5 us
    all_to_all x1, waiting for transfers between devices, inner(): lax.all_to_all(picked, 'gx', split_axis=0, concat_axis=0, tiled=True)  3.04 us
    pallas_call x1, Pallas kernels, inner(): pl.pallas_call(send_kernel, out_shape=(jax.ShapeDtypeStruct((DEV, ROWS, D...  2.45 us
    pallas_call x1, Pallas kernels, inner(): pl.pallas_call(gather_kernel, out_shape=[pltpu.VMEM((LEV, DEV), F32)] * N...  2.03 us
  transfers between devices with their start and end apart: 15, of which 6 were waited for; matrix products, arithmetic and copies ran while one was open for 1% of the time, Pallas kernels for 6%

profile of v6, /device:TPU:1, one launch (start us, length us, event | category | flops | bytes accessed | tf_op | source)
XLA Modules:
  0.0 83.0 jit_solution(15335880352008216738)
XLA Ops:
  0.6 2.4 %send.1 = (bf16[128,40,128]{2,1,0:T(8,128)(2,1)}, f32[8,128]{1,0:T(8,128)S(1)}) custom-call(bf16[1,64,512]{2,1,0:T(8,128)(2,1)} %inn_ref.1, s32[1,512]{1,0:T(1,128)} %col_ref.1, s32[1,128]{1,0:T(1,128)} %cnt_ref.1, s32[16,256]{1,0:T(8,128)} %refs_11_.1), custom_call_target="tpu_custom_call" | custom-call | tf_op jit(solution)/shard_map/send/pallas_call | solution.py:353
  3.1 33.1 %all_to_all.10.got_ref = bf16[128,40,128]{2,1,0:T(8,128)(2,1)S(1)} all-to-all(bf16[128,40,128]{2,1,0:T(8,128)(2,1)} %get-tuple-element.26), channel_id=1, replica_groups=mesh['gx'=16,'gy'=8] {'gx','gy'}, dimensions={0} | all-to-all | bytes 2621440 | tf_op jit(solution)/shard_map/all_to_all | solution.py:361
  36.1 10.7 %smooth.1 = (bf16[9,16,256]{2,1,0:T(8,128)(2,1)S(1)}, bf16[9,16,256]{2,1,0:T(8,128)(2,1)S(1)}, bf16[9,16,256]{2,1,0:T(8,128)(2,1)S(1)}, bf16[9,16,256]{2,1,0:T(8...) custom-call(bf16[128,40,128]{2,1,0:T(8,128)(2,1)S(1)} %all_to_all.10, ...), custom_call_target="tpu_custom_call" | custom-call | tf_op jit(solution)/shard_map/smooth/pallas_call | solution.py:184
  46.8 0.0 copy-start
  46.8 0.8 collective-permute-start
  47.6 3.9 %collective-permute-start.1 = (bf16[9,16,256]{2,1,0:T(8,128)(2,1)S(1)}, bf16[9,16,256]{2,1,0:T(8,128)(2,1)S(1)}, u32[]{:S(2)}, u32[]{:S(2)}) collective-permute-start(bf16[9,16,256]{2,1,0:T(8,128)(2,1)S(1)} %get-tuple-element.28), channel_id=1, source_target_pairs={{0,5},{1,4},{2,7},{3,6},{4,1},{5,0},{6,3},{7,2},{8,13},{9,12},{10,... | collective-permute-start | bytes 221192 | tf_op jit(solution)/shard_map/ppermute | solution.py:367
  51.5 2.0 %gather.1 = (f32[32,128]{1,0:T(8,128)S(1)}, f32[32,128]{1,0:T(8,128)S(1)}, f32[32,128]{1,0:T(8,128)S(1)}, f32[32,128]{1,0:T(8,128)S(1)}, f32[32,128]{1,0:T(8,128...) custom-call(f32[32,16,256]{2,1,0:T(8,128)} %coef_ref.3, ...), custom_call_target="tpu_custom_call" | custom-call | tf_op jit(solution)/shard_map/gather/pallas_call | solution.py:372
  53.5 0.2 collective-permute-start.7
  53.7 1.8 %collective-permute-start.8 = (f32[32,128]{1,0:T(8,128)S(1)}, f32[32,128]{1,0:T(8,128)S(1)}, u32[]{:S(2)}, u32[]{:S(2)}) collective-permute-start(f32[32,128]{1,0:T(8,128)S(1)} %get-tuple-element.40), channel_id=1, source_target_pairs={{0,5},{1,4},{2,7},{3,6},{4,1},{5,0},{6,3},{7,2},{8,13},{9,12},{10,... | collective-permute-start | bytes 49160 | tf_op jit(solution)/shard_map/ppermute | solution.py:367
  55.5 0.8 %collective-permute-start.9 = (f32[32,128]{1,0:T(8,128)S(1)}, f32[32,128]{1,0:T(8,128)S(1)}, u32[]{:S(2)}, u32[]{:S(2)}) collective-permute-start(f32[32,128]{1,0:T(8,128)S(1)} %get-tuple-element.41), channel_id=1, source_target_pairs={{0,6},{1,7},{2,4},{3,5},{4,2},{5,3},{6,0},{7,1},{8,14},{9,15},{10,... | collective-permute-start | bytes 49160 | tf_op jit(solution)/shard_map/ppermute | solution.py:367
  56.4 1.3 %collective-permute-done.7.refs_0_ = f32[32,128]{1,0:T(8,128)S(1)} collective-permute-done((f32[32,128]{1,0:T(8,128)S(1)}, f32[32,128]{1,0:T(8,128)S(1)}, u32[]{:S(2)}, u32[]{:S(2)}) %collective-permute-start.7) | collective-permute-done | bytes 16416 | tf_op jit(solution)/shard_map/ppermute | solution.py:367
  57.7 2.1 %collective-permute-start.10 = (f32[32,128]{1,0:T(8,128)S(1)}, f32[32,128]{1,0:T(8,128)S(1)}, u32[]{:S(2)}, u32[]{:S(2)}) collective-permute-start(f32[32,128]{1,0:T(8,128)S(1)} %get-tuple-element.42), channel_id=1, source_target_pairs={{0,7},{1,6},{2,5},{3,4},{4,3},{5,2},{6,1},{7,0},{8,15},{9,14},{10,... | collective-permute-start | bytes 49160 | tf_op jit(solution)/shard_map/ppermute | solution.py:367
  59.8 0.0 collective-permute-done.8.refs_1_
  59.8 0.0 collective-permute-start.11
  59.8 0.0 collective-permute-done.9.refs_2_
  59.8 1.0 %collective-permute-start.12 = (f32[32,128]{1,0:T(8,128)S(1)}, f32[32,128]{1,0:T(8,128)S(1)}, u32[]{:S(2)}, u32[]{:S(2)}) collective-permute-start(f32[32,128]{1,0:T(8,128)S(1)} %get-tuple-element.44), channel_id=1, source_target_pairs={{0,3},{1,2},{2,1},{3,0},{4,7},{5,6},{6,5},{7,4},{8,11},{9,10},{10,... | collective-permute-start | bytes 49160 | tf_op jit(solution)/shard_map/ppermute | solution.py:367
  60.8 1.3 %collective-permute-done.10.refs_3_ = f32[32,128]{1,0:T(8,128)S(1)} collective-permute-done((f32[32,128]{1,0:T(8,128)S(1)}, f32[32,128]{1,0:T(8,128)S(1)}, u32[]{:S(2)}, u32[]{:S(2)}) %collective-permute-start.10) | collective-permute-done | bytes 16416 | tf_op jit(solution)/shard_map/ppermute | solution.py:367
  62.1 0.0 collective-permute-start.13
  62.1 0.3 collective-permute-done.11.refs_4_
  62.4 1.9 %collective-permute-start.2 = (bf16[9,16,256]{2,1,0:T(8,128)(2,1)S(1)}, bf16[9,16,256]{2,1,0:T(8,128)(2,1)S(1)}, u32[]{:S(2)}, u32[]{:S(2)}) collective-permute-start(bf16[9,16,256]{2,1,0:T(8,128)(2,1)S(1)} %get-tuple-element.29), channel_id=1, source_target_pairs={{0,6},{1,7},{2,4},{3,5},{4,2},{5,3},{6,0},{7,1},{8,14},{9,15},{10,... | collective-permute-start | bytes 221192 | tf_op jit(solution)/shard_map/ppermute | solution.py:367
  64.3 0.0 collective-permute-done.12.refs_5_
  64.3 1.1 %collective-permute-start.3 = (bf16[9,16,256]{2,1,0:T(8,128)(2,1)S(1)}, bf16[9,16,256]{2,1,0:T(8,128)(2,1)S(1)}, u32[]{:S(2)}, u32[]{:S(2)}) collective-permute-start(bf16[9,16,256]{2,1,0:T(8,128)(2,1)S(1)} %get-tuple-element.30), channel_id=1, source_target_pairs={{0,7},{1,6},{2,5},{3,4},{4,3},{5,2},{6,1},{7,0},{8,15},{9,14},{10,... | collective-permute-start | bytes 221192 | tf_op jit(solution)/shard_map/ppermute | solution.py:367
  65.4 0.0 collective-permute-done.13.refs_6_
  65.4 0.0 collective-permute-start.4
  65.5 0.0 collective-permute-done.refs_0_
  65.5 1.6 %collective-permute-start.5 = (bf16[9,16,256]{2,1,0:T(8,128)(2,1)S(1)}, bf16[9,16,256]{2,1,0:T(8,128)(2,1)S(1)}, u32[]{:S(2)}, u32[]{:S(2)}) collective-permute-start(bf16[9,16,256]{2,1,0:T(8,128)(2,1)S(1)} %get-tuple-element.32), channel_id=1, source_target_pairs={{0,3},{1,2},{2,1},{3,0},{4,7},{5,6},{6,5},{7,4},{8,11},{9,10},{10,... | collective-permute-start | bytes 221192 | tf_op jit(solution)/shard_map/ppermute | solution.py:367
  67.1 0.0 collective-permute-done.1.refs_1_
  67.1 0.2 collective-permute-start.6
  67.3 0.4 station_coef.1
  67.7 0.0 collective-permute-done.2.refs_2_
  67.7 2.6 %collective-permute-done.3.refs_3_ = bf16[9,16,256]{2,1,0:T(8,128)(2,1)S(1)} collective-permute-done((bf16[9,16,256]{2,1,0:T(8,128)(2,1)S(1)}, bf16[9,16,256]{2,1,0:T(8,128)(2,1)S(1)}, u32[]{:S(2)}, u32[]{:S(2)}) %collective-permute-start.3) | collective-permute-done | bytes 73760 | tf_op jit(solution)/shard_map/ppermute | solution.py:367
  70.2 0.0 collective-permute-done.4.refs_4_
  70.2 0.8 collective-permute-done.5.refs_5_
  71.0 0.0 collective-permute-done.6.refs_6_
  71.0 1.1 %station.1.refs_12_ = bf16[16,16,128]{2,1,0:T(8,128)(2,1)} custom-call(bf16[9,16,256]{2,1,0:T(8,128)(2,1)S(1)} %collective-permute-done.refs_0_, bf16[9,16,256]{2,1,0:T(8,128)(2,1)S(1)} %collective-permute-done.1.refs_1_, bf16[9,16,256]{2,1,0:T(8,128)(2,1)S(1)} %collective-permute-done.2.refs_2_, bf16[9,16,256]{2,1,0:T(8,128)(2,1)S(1)} %collective-permute-done.3.refs_3_, ...), custom_call_target="tpu_custom_call" | custom-call | tf_op jit(solution)/shard_map/station/pallas_call | solution.py:394
  72.1 3.5 %all-to-all-start.1 = ((bf16[16,16,128]{2,1,0:T(8,128)(2,1)}), bf16[16,16,128]{2,1,0:T(8,128)(2,1)S(1)}, u32[]{:S(2)}, u32[]{:S(2)}) async-start(bf16[16,16,128]{2,1,0:T(8,128)(2,1)} %station.1.refs_12_), calls=%async_computation.1 | async-start | bytes 131072 | tf_op jit(solution)/shard_map/all_to_all | solution.py:406
  75.6 0.0 copy-done
  75.6 0.1 iota_compare_fusion
  75.7 1.3 %shard_map.86 = (f32[32,16,256]{2,1,0:T(8,128)S(1)}, f32[32,16,256]{2,1,0:T(8,128)S(1)}, f32[32,16,256]{2,1,0:T(8,128)S(1)}) custom-call(f32[32,16,256]{2,1,0:T(8,128)} %coef_ref.3), custom_call_target="tpu_custom_call" | custom-call | tf_op jit(solution)/shard_map/pallas_call | solution.py:393
  77.0 0.1 lt.20
  77.1 1.1 %solve.1 = bf16[64,16,256]{2,1,0:T(8,128)(2,1)S(1)} custom-call(bf16[9,16,256]{2,1,0:T(8,128)(2,1)S(1)} %collective-permute-done.refs_0_, bf16[9,16,256]{2,1,0:T(8,128)(2,1)S(1)} %collective-permute-done.1.refs_1_, bf16[9,16,256]{2,1,0:T(8,128)(2,1)S(1)} %collective-permute-done.2.refs_2_, bf16[9,16,256]{2,1,0:T(8,128)(2,1)S(1)} %collective-permute-done.3.refs_3_, ...), custom_call_target="tpu_custom_call" | custom-call | tf_op jit(solution)/shard_map/solve/pallas_call | solution.py:407
  78.2 0.8 copy.11
  79.0 3.0 %all-to-all-done.1 = bf16[16,16,128]{2,1,0:T(8,128)(2,1)S(1)} async-done(((bf16[16,16,128]{2,1,0:T(8,128)(2,1)}), bf16[16,16,128]{2,1,0:T(8,128)(2,1)S(1)}, u32[]{:S(2)}, u32[]{:S(2)}) %all-to-all-start.1) | async-done | bytes 65568 | tf_op jit(solution)/shard_map/all_to_all | solution.py:406
  82.0 0.1 reshape.26
  82.1 0.1 select_bitcast_fusion
  82.3 0.7 copy.10
Async XLA Ops:
  46.8 28.7 %copy-start = (s32[1,128]{1,0:T(1,128)S(1)}, s32[1,128]{1,0:T(1,128)}, u32[]{:S(2)}) copy-start(s32[1,128]{1,0:T(1,128)} %cnt_ref.1) | copy-start | bytes 1540
  46.8 18.6 %collective-permute-start = (bf16[9,16,256]{2,1,0:T(8,128)(2,1)S(1)}, bf16[9,16,256]{2,1,0:T(8,128)(2,1)S(1)}, u32[]{:S(2)}, u32[]{:S(2)}) collective-permute-start(bf16[9,16,256]{2,1,0:T(8,128)(2,1)S(1)} %get-tuple-element.27), channel_id=1, source_target_pairs={{0,4},{1,5},{2,6},{3,7},{4,0},{5,1},{6,2},{7,3},{8,12},{9,13},{10,... | collective-permute-start | bytes 221192 | tf_op jit(solution)/shard_map/ppermute | solution.py:367
  47.6 19.5 %collective-permute-start.1 = (bf16[9,16,256]{2,1,0:T(8,128)(2,1)S(1)}, bf16[9,16,256]{2,1,0:T(8,128)(2,1)S(1)}, u32[]{:S(2)}, u32[]{:S(2)}) collective-permute-start(bf16[9,16,256]{2,1,0:T(8,128)(2,1)S(1)} %get-tuple-element.28), channel_id=1, source_target_pairs={{0,5},{1,4},{2,7},{3,6},{4,1},{5,0},{6,3},{7,2},{8,13},{9,12},{10,... | collective-permute-start | bytes 221192 | tf_op jit(solution)/shard_map/ppermute | solution.py:367
  53.5 4.2 %collective-permute-start.7 = (f32[32,128]{1,0:T(8,128)S(1)}, f32[32,128]{1,0:T(8,128)S(1)}, u32[]{:S(2)}, u32[]{:S(2)}) collective-permute-start(f32[32,128]{1,0:T(8,128)S(1)} %get-tuple-element.39), channel_id=1, source_target_pairs={{0,4},{1,5},{2,6},{3,7},{4,0},{5,1},{6,2},{7,3},{8,12},{9,13},{10,... | collective-permute-start | bytes 49160 | tf_op jit(solution)/shard_map/ppermute | solution.py:367
  53.7 6.1 %collective-permute-start.8 = (f32[32,128]{1,0:T(8,128)S(1)}, f32[32,128]{1,0:T(8,128)S(1)}, u32[]{:S(2)}, u32[]{:S(2)}) collective-permute-start(f32[32,128]{1,0:T(8,128)S(1)} %get-tuple-element.40), channel_id=1, source_target_pairs={{0,5},{1,4},{2,7},{3,6},{4,1},{5,0},{6,3},{7,2},{8,13},{9,12},{10,... | collective-permute-start | bytes 49160 | tf_op jit(solution)/shard_map/ppermute | solution.py:367
  55.5 4.3 %collective-permute-start.9 = (f32[32,128]{1,0:T(8,128)S(1)}, f32[32,128]{1,0:T(8,128)S(1)}, u32[]{:S(2)}, u32[]{:S(2)}) collective-permute-start(f32[32,128]{1,0:T(8,128)S(1)} %get-tuple-element.41), channel_id=1, source_target_pairs={{0,6},{1,7},{2,4},{3,5},{4,2},{5,3},{6,0},{7,1},{8,14},{9,15},{10,... | collective-permute-start | bytes 49160 | tf_op jit(solution)/shard_map/ppermute | solution.py:367
  57.7 4.4 %collective-permute-start.10 = (f32[32,128]{1,0:T(8,128)S(1)}, f32[32,128]{1,0:T(8,128)S(1)}, u32[]{:S(2)}, u32[]{:S(2)}) collective-permute-start(f32[32,128]{1,0:T(8,128)S(1)} %get-tuple-element.42), channel_id=1, source_target_pairs={{0,7},{1,6},{2,5},{3,4},{4,3},{5,2},{6,1},{7,0},{8,15},{9,14},{10,... | collective-permute-start | bytes 49160 | tf_op jit(solution)/shard_map/ppermute | solution.py:367
  59.8 2.6 %collective-permute-start.11 = (f32[32,128]{1,0:T(8,128)S(1)}, f32[32,128]{1,0:T(8,128)S(1)}, u32[]{:S(2)}, u32[]{:S(2)}) collective-permute-start(f32[32,128]{1,0:T(8,128)S(1)} %get-tuple-element.43), channel_id=1, source_target_pairs={{0,2},{1,3},{2,0},{3,1},{4,6},{5,7},{6,4},{7,5},{8,10},{9,11},{10,... | collective-permute-start | bytes 49160 | tf_op jit(solution)/shard_map/ppermute | solution.py:367
  59.8 4.5 %collective-permute-start.12 = (f32[32,128]{1,0:T(8,128)S(1)}, f32[32,128]{1,0:T(8,128)S(1)}, u32[]{:S(2)}, u32[]{:S(2)}) collective-permute-start(f32[32,128]{1,0:T(8,128)S(1)} %get-tuple-element.44), channel_id=1, source_target_pairs={{0,3},{1,2},{2,1},{3,0},{4,7},{5,6},{6,5},{7,4},{8,11},{9,10},{10,... | collective-permute-start | bytes 49160 | tf_op jit(solution)/shard_map/ppermute | solution.py:367
  62.1 3.4 %collective-permute-start.13 = (f32[32,128]{1,0:T(8,128)S(1)}, f32[32,128]{1,0:T(8,128)S(1)}, u32[]{:S(2)}, u32[]{:S(2)}) collective-permute-start(f32[32,128]{1,0:T(8,128)S(1)} %get-tuple-element.45), channel_id=1, source_target_pairs={{0,1},{1,0},{2,3},{3,2},{4,5},{5,4},{6,7},{7,6},{8,9},{9,8},{10,11... | collective-permute-start | bytes 49160 | tf_op jit(solution)/shard_map/ppermute | solution.py:367
  62.4 5.3 %collective-permute-start.2 = (bf16[9,16,256]{2,1,0:T(8,128)(2,1)S(1)}, bf16[9,16,256]{2,1,0:T(8,128)(2,1)S(1)}, u32[]{:S(2)}, u32[]{:S(2)}) collective-permute-start(bf16[9,16,256]{2,1,0:T(8,128)(2,1)S(1)} %get-tuple-element.29), channel_id=1, source_target_pairs={{0,6},{1,7},{2,4},{3,5},{4,2},{5,3},{6,0},{7,1},{8,14},{9,15},{10,... | collective-permute-start | bytes 221192 | tf_op jit(solution)/shard_map/ppermute | solution.py:367
  64.3 5.9 %collective-permute-start.3 = (bf16[9,16,256]{2,1,0:T(8,128)(2,1)S(1)}, bf16[9,16,256]{2,1,0:T(8,128)(2,1)S(1)}, u32[]{:S(2)}, u32[]{:S(2)}) collective-permute-start(bf16[9,16,256]{2,1,0:T(8,128)(2,1)S(1)} %get-tuple-element.30), channel_id=1, source_target_pairs={{0,7},{1,6},{2,5},{3,4},{4,3},{5,2},{6,1},{7,0},{8,15},{9,14},{10,... | collective-permute-start | bytes 221192 | tf_op jit(solution)/shard_map/ppermute | solution.py:367
  65.4 4.8 %collective-permute-start.4 = (bf16[9,16,256]{2,1,0:T(8,128)(2,1)S(1)}, bf16[9,16,256]{2,1,0:T(8,128)(2,1)S(1)}, u32[]{:S(2)}, u32[]{:S(2)}) collective-permute-start(bf16[9,16,256]{2,1,0:T(8,128)(2,1)S(1)} %get-tuple-element.31), channel_id=1, source_target_pairs={{0,2},{1,3},{2,0},{3,1},{4,6},{5,7},{6,4},{7,5},{8,10},{9,11},{10,... | collective-permute-start | bytes 221192 | tf_op jit(solution)/shard_map/ppermute | solution.py:367
  65.5 5.5 %collective-permute-start.5 = (bf16[9,16,256]{2,1,0:T(8,128)(2,1)S(1)}, bf16[9,16,256]{2,1,0:T(8,128)(2,1)S(1)}, u32[]{:S(2)}, u32[]{:S(2)}) collective-permute-start(bf16[9,16,256]{2,1,0:T(8,128)(2,1)S(1)} %get-tuple-element.32), channel_id=1, source_target_pairs={{0,3},{1,2},{2,1},{3,0},{4,7},{5,6},{6,5},{7,4},{8,11},{9,10},{10,... | collective-permute-start | bytes 221192 | tf_op jit(solution)/shard_map/ppermute | solution.py:367
  67.1 3.9 %collective-permute-start.6 = (bf16[9,16,256]{2,1,0:T(8,128)(2,1)S(1)}, bf16[9,16,256]{2,1,0:T(8,128)(2,1)S(1)}, u32[]{:S(2)}, u32[]{:S(2)}) collective-permute-start(bf16[9,16,256]{2,1,0:T(8,128)(2,1)S(1)} %get-tuple-element.33), channel_id=1, source_target_pairs={{0,1},{1,0},{2,3},{3,2},{4,5},{5,4},{6,7},{7,6},{8,9},{9,8},{10,11... | collective-permute-start | bytes 221192 | tf_op jit(solution)/shard_map/ppermute | solution.py:367
  72.1 10.0 %all-to-all-start.1 = ((bf16[16,16,128]{2,1,0:T(8,128)(2,1)}), bf16[16,16,128]{2,1,0:T(8,128)(2,1)S(1)}, u32[]{:S(2)}, u32[]{:S(2)}) async-start(bf16[16,16,128]{2,1,0:T(8,128)(2,1)} %station.1.refs_12_), calls=%async_computation.1 | async-start | bytes 131072 | tf_op jit(solution)/shard_map/all_to_all | solution.py:406
